TPU v7x, 32 devices: a whole 2x2x4 slice. The times are simulated.
32 devices in a mesh: dp: 8 (over z, x), tensor: 4 (over y, core).
Axes of the slice: x: 2, y: 2, z: 4, core: 2. Of those that a mesh axis runs over, the one named last changes fastest.
Arguments:
- history: bfloat16 [9, 4096, 2048], P(None, 'dp'), may hold values from -6 to 6
- mix_weights: float32 [36, 4096], P(None, 'dp'), may hold values from -2.4 to 2.4
- segments: int32 [4096], P('dp'), may hold values from 0 to 1, as said below
- norm_gains: float32 [5, 2048], replicated, may hold values from 0.5 to 1.5
- w_query: bfloat16 [2048, 2048], P('dp', 'tensor'), may hold values from -0.125 to 0.125
- w_key: bfloat16 [2048, 2048], P('dp', 'tensor'), may hold values from -0.125 to 0.125
- w_value: bfloat16 [2048, 2048], P('dp', 'tensor'), may hold values from -0.125 to 0.125
- w_out: bfloat16 [2048, 2048], P('tensor', 'dp'), may hold values from -0.5 to 0.5
- w_up: bfloat16 [2048, 8192], P('dp', 'tensor'), may hold values from -0.125 to 0.125
- w_down: bfloat16 [8192, 2048], P('tensor', 'dp'), may hold values from -0.0625 to 0.0625
- gen_in: bfloat16 [2048, 40], replicated, may hold values from -0.125 to 0.125
- gen_out: bfloat16 [40, 40], replicated, may hold values from -1 to 1
- out_grad: bfloat16 [4096, 2048], P('dp'), may hold values from -6 to 6
- next_grad: float32 [40, 4096], P(None, 'dp'), may hold values from -6 to 6
Outputs:
- layer_out: bfloat16 [4096, 2048], P('dp')
- next_mix: float32 [40, 4096], P(None, 'dp')
- history_grad: bfloat16 [9, 4096, 2048], P(None, 'dp')
- mix_grad: float32 [36, 4096], P(None, 'dp')
- grad_gains: float32 [5, 2048], replicated
- grad_query: float32 [2048, 2048], P('dp', 'tensor')
- grad_key: float32 [2048, 2048], P('dp', 'tensor')
- grad_value: float32 [2048, 2048], P('dp', 'tensor')
- grad_out: float32 [2048, 2048], P('tensor', 'dp')
- grad_up: float32 [2048, 8192], P('dp', 'tensor')
- grad_down: float32 [8192, 2048], P('tensor', 'dp')
- grad_gen_in: float32 [2048, 40], replicated
- grad_gen_out: float32 [40, 40], replicated
Inputs may be any that keep to these rules, and one draw needn't show every extreme that they name: `segments`: each block of 512 tokens of one dp index holds either one sequence (all 0) or two of 256 tokens (0 then 1); both kinds occur in every draw.
All inputs are finite; a program needn't handle non-finite values.
Results may differ from a plain program's by a relative error of at most 0.018.
Values may be sent and summed in bfloat16 or wider, within the bound.
A program may use at most 320 MiB of HBM per device.

v0:
```python
import jax
import jax.numpy as jnp
from jax import lax
from jax.sharding import PartitionSpec as P

HEAD_DIM = 128
ROT = 32


EPSILON = 1e-05
ROPE_BASE = 10000.0


def layer_norm(values, gain_row):
    center = values - jnp.mean(values, axis=-1, keepdims=True)
    spread = jnp.mean(center * center, axis=-1, keepdims=True)
    return center * lax.rsqrt(spread + EPSILON) * gain_row


def rotary_tables(segments):
    tok_count = segments.shape[0]
    order_idx = jnp.arange(tok_count, dtype=jnp.int32)
    same_doc = segments[:, None] == segments[None, :]
    earlier = order_idx[None, :] < order_idx[:, None]
    places = jnp.sum((same_doc & earlier).astype(jnp.int32), axis=1)
    halves = jnp.arange(ROT // 2, dtype=jnp.float32)
    frequency = ROPE_BASE ** (-2.0 * halves / ROT)
    angles = places.astype(jnp.float32)[:, None] * frequency[None, :]
    allowed = same_doc & (order_idx[None, :] <= order_idx[:, None])
    return (jnp.cos(angles)[:, None, :], jnp.sin(angles)[:, None, :], allowed)


def rotate(values, cosine, sine_tab):
    first_half = values[..., : ROT // 2]
    second = values[..., ROT // 2 : ROT]
    return jnp.concatenate(
        [
            first_half * cosine - second * sine_tab,
            second * cosine + first_half * sine_tab,
            values[..., ROT:],
        ],
        axis=-1,
    )


def gelu_exact(values):
    return jax.nn.gelu(values, approximate=False)


def matmul(left_op, right_op):
    return jnp.dot(left_op, right_op, preferred_element_type=jnp.float32)


def body(
    history,
    mix_weights,
    segments,
    norm_gains,
    w_query,
    w_key,
    w_value,
    w_out,
    w_up,
    w_down,
    gen_in,
    gen_out,
    out_grad,
    next_grad,
):
    states = history.shape[0]
    tok_count = history.shape[1]
    local_cols = w_query.shape[1]
    local_heads = local_cols // HEAD_DIM
    mix_view = mix_weights.reshape(4, states, tok_count)
    streams = []
    for stream in range(4):
        running = mix_view[stream, 0][:, None] * history[0].astype(jnp.float32)
        for source in range(1, states):
            running = running + mix_view[stream, source][:, None] * history[source].astype(
                jnp.float32
            )
        streams.append(running)
    normed = [
        layer_norm(streams[stream], norm_gains[stream]).astype(jnp.bfloat16) for stream in range(4)
    ]
    cosine, sine_tab, allowed = rotary_tables(segments)
    gathered = (
        lax.all_gather(w_query, "dp", axis=0, tiled=True),
        lax.all_gather(w_key, "dp", axis=0, tiled=True),
        lax.all_gather(w_value, "dp", axis=0, tiled=True),
        lax.all_gather(w_up, "dp", axis=0, tiled=True),
        lax.all_gather(w_out, "dp", axis=1, tiled=True),
        lax.all_gather(w_down, "dp", axis=1, tiled=True),
    )
    full_query, full_key, full_value, full_up, full_out, full_down = gathered

    def split_heads(values):
        return values.reshape(tok_count, local_heads, HEAD_DIM)

    query_heads = rotate(split_heads(matmul(normed[0], full_query)), cosine, sine_tab).astype(
        jnp.bfloat16
    )
    key_heads = rotate(split_heads(matmul(normed[1], full_key)), cosine, sine_tab).astype(
        jnp.bfloat16
    )
    value_heads = split_heads(matmul(normed[2], full_value)).astype(jnp.bfloat16)
    score_scale = HEAD_DIM ** (-0.5)
    raw_scores = (
        jnp.einsum("thd,uhd->htu", query_heads, key_heads, preferred_element_type=jnp.float32)
        * score_scale
    )
    masked = jnp.where(allowed[None], raw_scores, -1e30)
    row_max = jnp.max(masked, axis=-1, keepdims=True)
    exp_scores = jnp.exp(masked - row_max)
    attn_probs = exp_scores / jnp.sum(exp_scores, axis=-1, keepdims=True)
    probs_low = attn_probs.astype(jnp.bfloat16)
    attended = (
        jnp.einsum("htu,uhd->thd", probs_low, value_heads, preferred_element_type=jnp.float32)
        .astype(jnp.bfloat16)
        .reshape(tok_count, local_cols)
    )
    hidden = matmul(normed[3], full_up)
    active = gelu_exact(hidden).astype(jnp.bfloat16)
    partial_sum = matmul(attended, full_out) + matmul(active, full_down)
    branch = lax.psum(partial_sum.astype(jnp.bfloat16), "tensor").astype(jnp.float32)
    out_full = streams[3] + branch
    gen_normed = layer_norm(out_full, norm_gains[4]).astype(jnp.bfloat16)
    gen_hidden = matmul(gen_normed, gen_in)
    gen_active = gelu_exact(gen_hidden).astype(jnp.bfloat16)
    next_mix = matmul(gen_active, gen_out)
    next_low = next_grad.T.astype(jnp.bfloat16)
    grad_gen_out = matmul(gen_active.T, next_low)
    gen_active_grad = matmul(next_low, gen_out.T)
    gelu_gen = jax.vjp(gelu_exact, gen_hidden)[1]
    gen_hidden_grad = gelu_gen(gen_active_grad)[0].astype(jnp.bfloat16)
    grad_gen_in = matmul(gen_normed.T, gen_hidden_grad)
    gen_normed_grad = matmul(gen_hidden_grad, gen_in.T)
    norm_pull = jax.vjp(layer_norm, out_full, norm_gains[4])[1]
    out_norm_grad, gain_gen_grad = norm_pull(gen_normed_grad)
    out_total = out_grad.astype(jnp.float32) + out_norm_grad
    branch_grad = out_total.astype(jnp.bfloat16)
    back_query, back_key, back_value, back_up, back_out, back_down = (
        lax.all_gather(w_query, "dp", axis=0, tiled=True),
        lax.all_gather(w_key, "dp", axis=0, tiled=True),
        lax.all_gather(w_value, "dp", axis=0, tiled=True),
        lax.all_gather(w_up, "dp", axis=0, tiled=True),
        lax.all_gather(w_out, "dp", axis=1, tiled=True),
        lax.all_gather(w_down, "dp", axis=1, tiled=True),
    )
    active_grad = matmul(branch_grad, back_down.T)
    gelu_mlp = jax.vjp(gelu_exact, hidden)[1]
    hidden_grad = gelu_mlp(active_grad)[0].astype(jnp.bfloat16)
    grad_down = matmul(active.T, branch_grad)
    grad_up = matmul(normed[3].T, hidden_grad)
    mlp_normed_grad = matmul(hidden_grad, back_up.T)
    attended_grad = (
        matmul(branch_grad, back_out.T)
        .astype(jnp.bfloat16)
        .reshape(tok_count, local_heads, HEAD_DIM)
    )
    grad_out_w = matmul(attended.T, branch_grad)
    probs_grad = jnp.einsum(
        "thd,uhd->htu", attended_grad, value_heads, preferred_element_type=jnp.float32
    )
    values_grad = jnp.einsum(
        "htu,thd->uhd", probs_low, attended_grad, preferred_element_type=jnp.float32
    ).astype(jnp.bfloat16)
    row_dot = jnp.sum(attn_probs * probs_grad, axis=-1, keepdims=True)
    scores_grad = (attn_probs * (probs_grad - row_dot)).astype(jnp.bfloat16)
    query_grad = (
        jnp.einsum("htu,uhd->thd", scores_grad, key_heads, preferred_element_type=jnp.float32)
        * score_scale
    )
    key_grad = (
        jnp.einsum("htu,thd->uhd", scores_grad, query_heads, preferred_element_type=jnp.float32)
        * score_scale
    )
    query_low = (
        rotate(query_grad, cosine, -sine_tab).reshape(tok_count, local_cols).astype(jnp.bfloat16)
    )
    key_low = (
        rotate(key_grad, cosine, -sine_tab).reshape(tok_count, local_cols).astype(jnp.bfloat16)
    )
    value_low = values_grad.reshape(tok_count, local_cols)
    grad_query = matmul(normed[0].T, query_low)
    grad_key = matmul(normed[1].T, key_low)
    grad_value = matmul(normed[2].T, value_low)
    query_normed_grad = matmul(query_low, back_query.T)
    key_normed_grad = matmul(key_low, back_key.T)
    value_normed_grad = matmul(value_low, back_value.T)
    summed_grads = (
        lax.psum(query_normed_grad.astype(jnp.bfloat16), "tensor").astype(jnp.float32),
        lax.psum(key_normed_grad.astype(jnp.bfloat16), "tensor").astype(jnp.float32),
        lax.psum(value_normed_grad.astype(jnp.bfloat16), "tensor").astype(jnp.float32),
        lax.psum(mlp_normed_grad.astype(jnp.bfloat16), "tensor").astype(jnp.float32),
    )
    stream_grads = []
    gain_grads = []
    for stream in range(4):
        stream_pull = jax.vjp(layer_norm, streams[stream], norm_gains[stream])[1]
        stream_grad, gain_grad = stream_pull(summed_grads[stream])
        stream_grads.append(stream_grad)
        gain_grads.append(gain_grad)
    stream_grads[3] = stream_grads[3] + out_total
    gain_grads.append(gain_gen_grad)
    history_rows = []
    for source in range(states):
        running = mix_view[0, source][:, None] * stream_grads[0]
        for stream in range(1, 4):
            running = running + mix_view[stream, source][:, None] * stream_grads[stream]
        history_rows.append(running.astype(jnp.bfloat16))
    history_grad = jnp.stack(history_rows)
    mix_rows = []
    for stream in range(4):
        for source in range(states):
            mix_rows.append(
                jnp.sum(history[source].astype(jnp.float32) * stream_grads[stream], axis=1)
            )
    mix_grad = jnp.stack(mix_rows)
    small_sums = (
        lax.psum(jnp.stack(gain_grads).astype(jnp.bfloat16), "dp").astype(jnp.float32),
        lax.psum(grad_gen_in.astype(jnp.bfloat16), "dp").astype(jnp.float32),
        lax.psum(grad_gen_out.astype(jnp.bfloat16), "dp").astype(jnp.float32),
    )
    grad_query_dev, grad_key_dev, grad_value_dev, grad_up_dev, grad_out_dev, grad_down_dev = (
        lax.psum_scatter(
            grad_query.astype(jnp.bfloat16), "dp", scatter_dimension=0, tiled=True
        ).astype(jnp.float32),
        lax.psum_scatter(
            grad_key.astype(jnp.bfloat16), "dp", scatter_dimension=0, tiled=True
        ).astype(jnp.float32),
        lax.psum_scatter(
            grad_value.astype(jnp.bfloat16), "dp", scatter_dimension=0, tiled=True
        ).astype(jnp.float32),
        lax.psum_scatter(
            grad_up.astype(jnp.bfloat16), "dp", scatter_dimension=0, tiled=True
        ).astype(jnp.float32),
        lax.psum_scatter(
            grad_out_w.astype(jnp.bfloat16), "dp", scatter_dimension=1, tiled=True
        ).astype(jnp.float32),
        lax.psum_scatter(
            grad_down.astype(jnp.bfloat16), "dp", scatter_dimension=1, tiled=True
        ).astype(jnp.float32),
    )
    return (
        out_full.astype(jnp.bfloat16),
        next_mix.T,
        history_grad,
        mix_grad,
        small_sums[0],
        grad_query_dev,
        grad_key_dev,
        grad_value_dev,
        grad_out_dev,
        grad_up_dev,
        grad_down_dev,
        small_sums[1],
        small_sums[2],
    )


def solution(mesh):
    in_specs = (
        P(None, "dp", None),
        P(None, "dp"),
        P("dp"),
        P(),
        P("dp", "tensor"),
        P("dp", "tensor"),
        P("dp", "tensor"),
        P("tensor", "dp"),
        P("dp", "tensor"),
        P("tensor", "dp"),
        P(),
        P(),
        P("dp", None),
        P(None, "dp"),
    )
    out_specs = (
        P("dp", None),
        P(None, "dp"),
        P(None, "dp", None),
        P(None, "dp"),
        P(),
        P("dp", "tensor"),
        P("dp", "tensor"),
        P("dp", "tensor"),
        P("tensor", "dp"),
        P("dp", "tensor"),
        P("tensor", "dp"),
        P(),
        P(),
    )
    return jax.shard_map(body, mesh=mesh, in_specs=in_specs, out_specs=out_specs, check_vma=False)
```

profile of v0, /device:TPU:0, one launch (start us, length us, event | category | flops | bytes accessed | tf_op | source)
XLA Modules:
  0.0 1367.1 jit_solution(17658311049838522774)
XLA Ops:
  16.1 8.9 fusion.271
  27.2 2.7 copy-done.2
  29.8 5.4 fusion.274
  35.8 4.6 fusion.269
  41.0 4.6 fusion.267
  47.9 5.3 fusion.137
  53.3 5.3 fusion.161
  58.7 4.5 fusion.149
  63.2 4.5 copy.38
  67.7 44.4 %all-gather.11.cloned.1.call-done = bf16[2048,512]{1,0:T(8,128)(2,1)} async-done(((bf16[256,512]{1,0:T(8,128)(2,1)}), bf16[2048,512]{1,0:T(8,128)(2,1)}) %all-gather.11.cloned.1.call-update) | async-done | bytes 2097168 | tf_op jit(solution)/shard_map/all_gather | solution.py:89
  112.1 3.9 copy.40
  116.0 46.0 %all-gather.9.cloned.1.call-done = bf16[2048,512]{1,0:T(8,128)(2,1)} async-done(((bf16[256,512]{1,0:T(8,128)(2,1)}), bf16[2048,512]{1,0:T(8,128)(2,1)}) %all-gather.9.cloned.1.call-update) | async-done | bytes 2097168 | tf_op jit(solution)/shard_map/all_gather | solution.py:88
  162.1 4.2 copy.39
  166.2 3.6 fusion.219
  173.9 3.6 fusion.279
  177.6 2.7 convolution_convert_fusion.13
  180.3 107.2 %all-gather.15.cloned.1.call-done = bf16[2048,2048]{1,0:T(8,128)(2,1)} async-done(((bf16[256,2048]{1,0:T(8,128)(2,1)}), bf16[2048,2048]{1,0:T(8,128)(2,1)}) %all-gather.15.cloned.1.call-update) | async-done | bytes 8388624 | tf_op jit(solution)/shard_map/all_gather | solution.py:91
  287.5 28.7 %multiply_convert_fusion.2 = (bf16[512,2048]{1,0:T(8,128)(2,1)}, f32[512,2048]{1,0:T(8,128)}, f32[512,2048]{1,0:T(8,128)}) fusion(bf16[2048,2048]{1,0:T(8,128)(2,1)} %all-gather.15.cloned.1.call-done, f32[512,2048]{1,0:T(8,128)} %copy-done.7, f32[2048]{0:T(1024)S(1)} %bitcast.625, f32[512]{0:T(512)S(1)} %fusion.255, f32[512]{0:T(512)S(1)} %broadcast_multiply_fusion.1), kind=kOutput, calls=%fused_computation.266 | convolution fusion | flops 4367319040 | bytes 23080960 | tf_op jit(solution)/shard_map/dot_general | solution.py:51
  316.2 96.7 %all-gather.17.cloned.1.call-done = bf16[2048,2048]{1,0:T(8,128)(2,1)} async-done(((bf16[2048,256]{1,0:T(8,128)(2,1)}), bf16[2048,2048]{1,0:T(8,128)(2,1)}) %all-gather.17.cloned.1.call-update) | async-done | bytes 8388624 | tf_op jit(solution)/shard_map/all_gather | solution.py:93
  413.0 10.5 fusion.280
  423.4 40.7 %all-gather.13.cloned.1.call-done = bf16[512,2048]{1,0:T(8,128)(2,1)} async-done(((bf16[512,256]{1,0:T(8,128)(2,1)}), bf16[512,2048]{1,0:T(8,128)(2,1)}) %all-gather.13.cloned.1.call-update) | async-done | bytes 2097168 | tf_op jit(solution)/shard_map/all_gather | solution.py:92
  464.2 5.4 add_convert_fusion.10
  469.7 49.7 %all-reduce.6.cloned.1.call-done = bf16[512,2048]{1,0:T(8,128)(2,1)} async-done(((bf16[512,2048]{1,0:T(8,128)(2,1)}), bf16[512,2048]{1,0:T(8,128)(2,1)}) %all-reduce.6.cloned.1.call-update) | async-done | bytes 2097168 | tf_op jit(solution)/shard_map/psum | solution.py:125
  519.4 3.4 fusion.266
  526.9 3.8 multiply_reduce_fusion
  530.7 2.6 fusion.264
  546.2 12.2 add_convert_fusion.9
  558.4 7.5 convolution_convert_fusion.6
  565.9 2.7 convolution_convert_fusion.7
  568.6 2.6 convolution_convert_fusion.9
  571.3 2.7 convolution_convert_fusion.8
  575.5 3.7 convolution_convert_fusion.3
  579.3 4.2 convolution_convert_fusion.2
  584.0 4.5 convolution_convert_fusion.4
  588.6 2.6 convolution_convert_fusion.5
  591.3 10.9 convolution_convert_fusion.1
  603.8 8.4 convolution_convert_fusion
  615.5 154.8 %all-reduce.10.cloned.1.call-done = (bf16[512,2048]{1,0:T(8,128)(2,1)}, bf16[512,2048]{1,0:T(8,128)(2,1)}, bf16[512,2048]{1,0:T(8,128)(2,1)}, bf16[512,2048]{1,0:T(8,128)(2,1)}) async-done(((bf16[512,2048]{1,0:T(8,128)(2,1)}, bf16[512,2048]{1,0:T(8,128)(2,1)}, bf16[512,2048]{1,0:T(8,128)(2,1)}, bf16[512,2048]{1,0:T(8,128)(2,1)}), (bf16[512,2048]{1,0:T(8,128)(2,1)}, bf16[512,2048]{1,0:T(8,128)(2,1)}, ...) | async-done | bytes 8388624 | tf_op jit(solution)/shard_map/psum | solution.py:195
  770.3 3.7 fusion.81
  775.8 2.0 fusion.87
  778.6 2.1 fusion.88
  784.5 3.8 fusion.85
  788.4 38.0 %all-reduce = (bf16[5,2048]{1,0:T(8,128)(2,1)S(1)}, bf16[40,40]{1,0:T(8,128)(2,1)S(1)}) all-reduce(bf16[5,2048]{1,0:T(8,128)(2,1)S(1)} %stack.202, bf16[40,40]{1,0:T(8,128)(2,1)S(1)} %convolution_convert_fusion.14), channel_id=1, replica_groups=mesh['dp'=8,'tensor'=4] {'dp'}, use_global_device_ids=true, to_apply=%region_70.71 | all-reduce | flops 11840 | bytes 47360 | tf_op jit(solution)/shard_map/psum | solution.py:221
  827.7 12.8 fusion.192
  840.6 12.2 fusion.190
  853.2 6.3 fusion.191
  859.5 7.9 fusion.193
  867.4 3.2 stack.201
  872.4 40.0 %reduce-scatter.13.cloned.1.call-done = bf16[512,256]{1,0:T(8,128)(2,1)} async-done(((bf16[512,2048]{1,0:T(8,128)(2,1)}), bf16[512,256]{1,0:T(8,128)(2,1)}) %reduce-scatter.13.cloned.1.call-update) | async-done | bytes 262160 | tf_op jit(solution)/shard_map/reduce_scatter | solution.py:238
  914.2 68.5 %reduce-scatter.9.cloned.1.call-done = bf16[256,512]{1,0:T(8,128)(2,1)} async-done(((bf16[2048,512]{1,0:T(8,128)(2,1)}), bf16[256,512]{1,0:T(8,128)(2,1)}) %reduce-scatter.9.cloned.1.call-update) | async-done | bytes 262160 | tf_op jit(solution)/shard_map/reduce_scatter | solution.py:229
  984.5 68.9 %reduce-scatter.7.cloned.1.call-done = bf16[256,512]{1,0:T(8,128)(2,1)} async-done(((bf16[2048,512]{1,0:T(8,128)(2,1)}), bf16[256,512]{1,0:T(8,128)(2,1)}) %reduce-scatter.7.cloned.1.call-update) | async-done | bytes 262160 | tf_op jit(solution)/shard_map/reduce_scatter | solution.py:226
  1055.3 8.0 fusion.202
  1067.2 3.3 fusion.204
  1070.5 3.3 fusion.206
  1073.8 3.3 fusion.208
  1077.2 2.5 fusion.210
  1079.7 2.5 fusion.212
  1082.3 2.8 fusion.214
  1085.1 2.5 fusion.216
  1087.6 2.5 fusion.218
  1090.1 114.9 %reduce-scatter.15.cloned.1.call-done = bf16[256,2048]{1,0:T(8,128)(2,1)} async-done(((bf16[2048,2048]{1,0:T(8,128)(2,1)}), bf16[256,2048]{1,0:T(8,128)(2,1)}) %reduce-scatter.15.cloned.1.call-update) | async-done | bytes 1048592 | tf_op jit(solution)/shard_map/reduce_scatter | solution.py:235
  1205.0 2.8 convert_element_type.498
  1207.8 149.6 %reduce-scatter.17.cloned.1.call-done = bf16[2048,256]{1,0:T(8,128)(2,1)} async-done(((bf16[2048,2048]{1,0:T(8,128)(2,1)}), bf16[2048,256]{1,0:T(8,128)(2,1)}) %reduce-scatter.17.cloned.1.call-update) | async-done | bytes 1048592 | tf_op jit(solution)/shard_map/reduce_scatter | solution.py:241
  1357.4 2.7 convert_element_type.500
  (399 shorter events, 61.2 us)
Async XLA Ops:
  7.2 517.5 %copy-start = (bf16[2048,40]{0,1:T(8,128)(2,1)S(1)}, bf16[2048,40]{0,1:T(8,128)(2,1)}, u32[]{:S(2)}) copy-start(bf16[2048,40]{0,1:T(8,128)(2,1)} %param.24) | copy-start | bytes 491524
  7.2 56.0 %all-gather.7.cloned.1.call-start = ((), (), s32[]{:S(2)}) async-start(), calls=%async_computation.6 | async-start | bytes 2359296 | tf_op jit(solution)/shard_map/all_gather | solution.py:90
  7.9 104.2 %all-gather.11.cloned.1.call-start = ((), (), s32[]{:S(2)}) async-start(), calls=%async_computation.8 | async-start | bytes 2359296 | tf_op jit(solution)/shard_map/all_gather | solution.py:89
  8.7 153.4 %all-gather.9.cloned.1.call-start = ((), (), s32[]{:S(2)}) async-start(), calls=%async_computation.7 | async-start | bytes 2359296 | tf_op jit(solution)/shard_map/all_gather | solution.py:88
  9.4 278.1 %all-gather.15.cloned.1.call-start = ((), (), s32[]{:S(2)}) async-start(), calls=%async_computation.10 | async-start | bytes 9437184 | tf_op jit(solution)/shard_map/all_gather | solution.py:91
  10.0 403.0 %all-gather.17.cloned.1.call-start = ((), (), s32[]{:S(2)}) async-start(), calls=%async_computation.11 | async-start | bytes 9437184 | tf_op jit(solution)/shard_map/all_gather | solution.py:93
  10.6 453.6 %all-gather.13.cloned.1.call-start = ((), (), s32[]{:S(2)}) async-start(), calls=%async_computation.9 | async-start | bytes 2359296 | tf_op jit(solution)/shard_map/all_gather | solution.py:92
  11.2 508.2 %all-reduce.6.cloned.1.call-start = ((), (), s32[]{:S(2)}) async-start(), calls=%async_computation.12 | async-start | bytes 4194304 | tf_op jit(solution)/shard_map/psum | solution.py:125
  12.7 14.4 %copy-start.127 = (f32[1,1,512]{2,1,0:T(1,128)}, f32[1,1,512]{2,1,0:T(1,128)S(1)}, u32[]{:S(2)}) copy-start(f32[1,1,512]{2,1,0:T(1,128)S(1)} %get-tuple-element.121) | copy-start | bytes 6148
  12.7 14.4 %copy-start.129 = (f32[1,1,512]{2,1,0:T(1,128)}, f32[1,1,512]{2,1,0:T(1,128)S(1)}, u32[]{:S(2)}) copy-start(f32[1,1,512]{2,1,0:T(1,128)S(1)} %get-tuple-element.122) | copy-start | bytes 6148
  12.8 14.4 %copy-start.131 = (f32[1,1,512]{2,1,0:T(1,128)}, f32[1,1,512]{2,1,0:T(1,128)S(1)}, u32[]{:S(2)}) copy-start(f32[1,1,512]{2,1,0:T(1,128)S(1)} %get-tuple-element.123) | copy-start | bytes 6148
  12.8 35.0 %copy-start.59 = (f32[1,1,512]{2,1,0:T(1,128)}, f32[1,1,512]{2,1,0:T(1,128)S(1)}, u32[]{:S(2)}) copy-start(f32[1,1,512]{2,1,0:T(1,128)S(1)} %get-tuple-element.114) | copy-start | bytes 6148
  12.8 35.0 %copy-start.61 = (f32[1,1,512]{2,1,0:T(1,128)}, f32[1,1,512]{2,1,0:T(1,128)S(1)}, u32[]{:S(2)}) copy-start(f32[1,1,512]{2,1,0:T(1,128)S(1)} %get-tuple-element.115) | copy-start | bytes 6148
  12.8 35.0 %copy-start.63 = (f32[1,1,512]{2,1,0:T(1,128)}, f32[1,1,512]{2,1,0:T(1,128)S(1)}, u32[]{:S(2)}) copy-start(f32[1,1,512]{2,1,0:T(1,128)S(1)} %get-tuple-element.116) | copy-start | bytes 6148
  12.8 35.0 %copy-start.65 = (f32[1,1,512]{2,1,0:T(1,128)}, f32[1,1,512]{2,1,0:T(1,128)S(1)}, u32[]{:S(2)}) copy-start(f32[1,1,512]{2,1,0:T(1,128)S(1)} %get-tuple-element.117) | copy-start | bytes 6148
  12.8 35.0 %copy-start.73 = (f32[1,1,512]{2,1,0:T(1,128)}, f32[1,1,512]{2,1,0:T(1,128)S(1)}, u32[]{:S(2)}) copy-start(f32[1,1,512]{2,1,0:T(1,128)S(1)} %get-tuple-element.118) | copy-start | bytes 6148
  12.8 35.0 %copy-start.79 = (f32[1,1,512]{2,1,0:T(1,128)}, f32[1,1,512]{2,1,0:T(1,128)S(1)}, u32[]{:S(2)}) copy-start(f32[1,1,512]{2,1,0:T(1,128)S(1)} %get-tuple-element.119) | copy-start | bytes 6148
  12.8 35.0 %copy-start.85 = (f32[1,1,512]{2,1,0:T(1,128)}, f32[1,1,512]{2,1,0:T(1,128)S(1)}, u32[]{:S(2)}) copy-start(f32[1,1,512]{2,1,0:T(1,128)S(1)} %get-tuple-element.120) | copy-start | bytes 6148
  12.8 35.0 %copy-start.91 = (f32[1,1,512]{2,1,0:T(1,128)}, f32[1,1,512]{2,1,0:T(1,128)S(1)}, u32[]{:S(2)}) copy-start(f32[1,1,512]{2,1,0:T(1,128)S(1)} %get-tuple-element.113) | copy-start | bytes 6148
  12.9 34.9 %copy-start.71 = (f32[1,1,512]{2,1,0:T(1,128)}, f32[1,1,512]{2,1,0:T(1,128)S(1)}, u32[]{:S(2)}) copy-start(f32[1,1,512]{2,1,0:T(1,128)S(1)} %get-tuple-element.112) | copy-start | bytes 6148
  12.9 40.3 %copy-start.67 = (f32[1,1,512]{2,1,0:T(1,128)}, f32[1,1,512]{2,1,0:T(1,128)S(1)}, u32[]{:S(2)}) copy-start(f32[1,1,512]{2,1,0:T(1,128)S(1)} %get-tuple-element.95) | copy-start | bytes 6148
  12.9 40.2 %copy-start.75 = (f32[1,1,512]{2,1,0:T(1,128)}, f32[1,1,512]{2,1,0:T(1,128)S(1)}, u32[]{:S(2)}) copy-start(f32[1,1,512]{2,1,0:T(1,128)S(1)} %get-tuple-element.96) | copy-start | bytes 6148
  12.9 40.2 %copy-start.81 = (f32[1,1,512]{2,1,0:T(1,128)}, f32[1,1,512]{2,1,0:T(1,128)S(1)}, u32[]{:S(2)}) copy-start(f32[1,1,512]{2,1,0:T(1,128)S(1)} %get-tuple-element.97) | copy-start | bytes 6148
  12.9 40.2 %copy-start.87 = (f32[1,1,512]{2,1,0:T(1,128)}, f32[1,1,512]{2,1,0:T(1,128)S(1)}, u32[]{:S(2)}) copy-start(f32[1,1,512]{2,1,0:T(1,128)S(1)} %get-tuple-element.98) | copy-start | bytes 6148
  12.9 40.2 %copy-start.93 = (f32[1,1,512]{2,1,0:T(1,128)}, f32[1,1,512]{2,1,0:T(1,128)S(1)}, u32[]{:S(2)}) copy-start(f32[1,1,512]{2,1,0:T(1,128)S(1)} %get-tuple-element.99) | copy-start | bytes 6148
  13.0 40.2 %copy-start.97 = (f32[1,1,512]{2,1,0:T(1,128)}, f32[1,1,512]{2,1,0:T(1,128)S(1)}, u32[]{:S(2)}) copy-start(f32[1,1,512]{2,1,0:T(1,128)S(1)} %get-tuple-element.100) | copy-start | bytes 6148
  13.0 40.2 %copy-start.101 = (f32[1,1,512]{2,1,0:T(1,128)}, f32[1,1,512]{2,1,0:T(1,128)S(1)}, u32[]{:S(2)}) copy-start(f32[1,1,512]{2,1,0:T(1,128)S(1)} %get-tuple-element.101) | copy-start | bytes 6148
  13.0 40.2 %copy-start.105 = (f32[1,1,512]{2,1,0:T(1,128)}, f32[1,1,512]{2,1,0:T(1,128)S(1)}, u32[]{:S(2)}) copy-start(f32[1,1,512]{2,1,0:T(1,128)S(1)} %get-tuple-element.102) | copy-start | bytes 6148
  13.0 40.2 %copy-start.111 = (f32[1,1,512]{2,1,0:T(1,128)}, f32[1,1,512]{2,1,0:T(1,128)S(1)}, u32[]{:S(2)}) copy-start(f32[1,1,512]{2,1,0:T(1,128)S(1)} %get-tuple-element.103) | copy-start | bytes 6148
  13.0 45.6 %copy-start.69 = (f32[1,1,512]{2,1,0:T(1,128)}, f32[1,1,512]{2,1,0:T(1,128)S(1)}, u32[]{:S(2)}) copy-start(f32[1,1,512]{2,1,0:T(1,128)S(1)} %get-tuple-element.104) | copy-start | bytes 6148
  13.0 45.6 %copy-start.77 = (f32[1,1,512]{2,1,0:T(1,128)}, f32[1,1,512]{2,1,0:T(1,128)S(1)}, u32[]{:S(2)}) copy-start(f32[1,1,512]{2,1,0:T(1,128)S(1)} %get-tuple-element.105) | copy-start | bytes 6148
  13.0 45.5 %copy-start.83 = (f32[1,1,512]{2,1,0:T(1,128)}, f32[1,1,512]{2,1,0:T(1,128)S(1)}, u32[]{:S(2)}) copy-start(f32[1,1,512]{2,1,0:T(1,128)S(1)} %get-tuple-element.106) | copy-start | bytes 6148
  13.0 45.5 %copy-start.89 = (f32[1,1,512]{2,1,0:T(1,128)}, f32[1,1,512]{2,1,0:T(1,128)S(1)}, u32[]{:S(2)}) copy-start(f32[1,1,512]{2,1,0:T(1,128)S(1)} %get-tuple-element.107) | copy-start | bytes 6148
  13.0 45.5 %copy-start.95 = (f32[1,1,512]{2,1,0:T(1,128)}, f32[1,1,512]{2,1,0:T(1,128)S(1)}, u32[]{:S(2)}) copy-start(f32[1,1,512]{2,1,0:T(1,128)S(1)} %get-tuple-element.108) | copy-start | bytes 6148
  13.0 45.5 %copy-start.99 = (f32[1,1,512]{2,1,0:T(1,128)}, f32[1,1,512]{2,1,0:T(1,128)S(1)}, u32[]{:S(2)}) copy-start(f32[1,1,512]{2,1,0:T(1,128)S(1)} %get-tuple-element.109) | copy-start | bytes 6148
  13.1 45.5 %copy-start.103 = (f32[1,1,512]{2,1,0:T(1,128)}, f32[1,1,512]{2,1,0:T(1,128)S(1)}, u32[]{:S(2)}) copy-start(f32[1,1,512]{2,1,0:T(1,128)S(1)} %get-tuple-element.110) | copy-start | bytes 6148
  13.1 45.5 %copy-start.107 = (f32[1,1,512]{2,1,0:T(1,128)}, f32[1,1,512]{2,1,0:T(1,128)S(1)}, u32[]{:S(2)}) copy-start(f32[1,1,512]{2,1,0:T(1,128)S(1)} %get-tuple-element.111) | copy-start | bytes 6148
  13.1 45.5 %copy-start.109 = (f32[1,1,512]{2,1,0:T(1,128)}, f32[1,1,512]{2,1,0:T(1,128)S(1)}, u32[]{:S(2)}) copy-start(f32[1,1,512]{2,1,0:T(1,128)S(1)} %get-tuple-element.94) | copy-start | bytes 6148
  16.1 31.8 %copy-start.46 = (f32[1,2048]{1,0:T(1,128)}, f32[1,2048]{1,0:T(1,128)S(1)}, u32[]{:S(2)}) copy-start(f32[1,2048]{1,0:T(1,128)S(1)} %get-tuple-element.135) | copy-start | bytes 24580
  16.1 37.2 %copy-start.48 = (f32[1,2048]{1,0:T(1,128)}, f32[1,2048]{1,0:T(1,128)S(1)}, u32[]{:S(2)}) copy-start(f32[1,2048]{1,0:T(1,128)S(1)} %get-tuple-element.133) | copy-start | bytes 24580
  16.1 42.5 %copy-start.50 = (f32[1,2048]{1,0:T(1,128)}, f32[1,2048]{1,0:T(1,128)S(1)}, u32[]{:S(2)}) copy-start(f32[1,2048]{1,0:T(1,128)S(1)} %get-tuple-element.134) | copy-start | bytes 24580
  25.0 22.8 %copy-start.53 = (f32[512]{0:T(512)}, f32[512]{0:T(512)S(1)}, u32[]{:S(2)}) copy-start(f32[512]{0:T(512)S(1)} %broadcast_multiply_fusion.4) | copy-start | bytes 6148
  25.6 22.3 %copy-start.113 = (f32[512]{0:T(512)}, f32[512]{0:T(512)S(1)}, u32[]{:S(2)}) copy-start(f32[512]{0:T(512)S(1)} %fusion.252) | copy-start | bytes 6148
  63.1 106.8 %copy-start.30 = (bf16[1,512,2048]{2,1,0:T(8,128)(2,1)}, bf16[1,512,2048]{2,1,0:T(8,128)(2,1)S(1)}, u32[]{:S(2)}) copy-start(bf16[1,512,2048]{2,1,0:T(8,128)(2,1)S(1)} %fusion.149) | copy-start | bytes 6291460
  469.6 144.2 %all-reduce.8.cloned.1.call-start = ((), (), s32[]{:S(2)}) async-start(), calls=%async_computation.19 | async-start | bytes 327680 | tf_op jit(solution)/shard_map/psum | solution.py:222
  544.2 226.1 %all-reduce.10.cloned.1.call-start = ((), (), s32[]{:S(2)}) async-start(), calls=%async_computation.20 | async-start | bytes 16777216 | tf_op jit(solution)/shard_map/psum | solution.py:195
  544.5 24.1 %copy-start.43 = (bf16[512,4,128]{0,2,1:T(8,128)(2,1)}, bf16[512,4,128]{0,2,1:T(8,128)(2,1)S(1)}, u32[]{:S(2)}) copy-start(bf16[512,4,128]{0,2,1:T(8,128)(2,1)S(1)} %maximum_convert_fusion) | copy-start | bytes 1572868
  544.6 26.7 %copy-start.45 = (bf16[512,4,128]{0,2,1:T(8,128)(2,1)}, bf16[512,4,128]{0,2,1:T(8,128)(2,1)S(1)}, u32[]{:S(2)}) copy-start(bf16[512,4,128]{0,2,1:T(8,128)(2,1)S(1)} %maximum_convert_fusion.1) | copy-start | bytes 1572868
  573.9 296.7 %reduce-scatter.11.cloned.1.call-start = ((), (), s32[]{:S(2)}) async-start(), calls=%async_computation.15 | async-start | bytes 2359296 | tf_op jit(solution)/shard_map/reduce_scatter | solution.py:232
  579.2 333.2 %reduce-scatter.13.cloned.1.call-start = ((), (), s32[]{:S(2)}) async-start(), calls=%async_computation.16 | async-start | bytes 2359296 | tf_op jit(solution)/shard_map/reduce_scatter | solution.py:238
  583.5 399.2 %reduce-scatter.9.cloned.1.call-start = ((), (), s32[]{:S(2)}) async-start(), calls=%async_computation.14 | async-start | bytes 2359296 | tf_op jit(solution)/shard_map/reduce_scatter | solution.py:229
  588.5 464.9 %reduce-scatter.7.cloned.1.call-start = ((), (), s32[]{:S(2)}) async-start(), calls=%async_computation.13 | async-start | bytes 2359296 | tf_op jit(solution)/shard_map/reduce_scatter | solution.py:226
  591.2 613.8 %reduce-scatter.15.cloned.1.call-start = ((), (), s32[]{:S(2)}) async-start(), calls=%async_computation.17 | async-start | bytes 9437184 | tf_op jit(solution)/shard_map/reduce_scatter | solution.py:235
  602.2 755.2 %reduce-scatter.17.cloned.1.call-start = ((), (), s32[]{:S(2)}) async-start(), calls=%async_computation.18 | async-start | bytes 9437184 | tf_op jit(solution)/shard_map/reduce_scatter | solution.py:241
  612.2 161.8 %copy-start.126 = (f32[512]{0:T(512)S(1)}, f32[512]{0:T(512)}, u32[]{:S(2)}) copy-start(f32[512]{0:T(512)} %copy-done.125) | copy-start | bytes 6148
  612.2 161.8 %copy-start.47 = (f32[1,2048]{1,0:T(1,128)S(1)}, f32[1,2048]{1,0:T(1,128)}, u32[]{:S(2)}) copy-start(f32[1,2048]{1,0:T(1,128)} %copy-done.46) | copy-start | bytes 24580
  612.2 161.8 %copy-start.54 = (f32[512]{0:T(512)S(1)}, f32[512]{0:T(512)}, u32[]{:S(2)}) copy-start(f32[512]{0:T(512)} %copy-done.53) | copy-start | bytes 6148
  827.7 25.1 %slice-start = ((s8[18874368]{0:T(1024)(128)(4,1)}), s8[4194304]{0:T(1024)(128)(4,1)S(1)}, s32[]{:S(2)}) async-start(s8[18874368]{0:T(1024)(128)(4,1)} %bitcast.596), calls=%async_computation.21 | async-start | bytes 8388608
  827.7 25.1 %slice-start.1 = ((s8[18874368]{0:T(1024)(128)(4,1)}), s8[4194304]{0:T(1024)(128)(4,1)S(1)}, s32[]{:S(2)}) async-start(s8[18874368]{0:T(1024)(128)(4,1)} %bitcast.596), calls=%async_computation.22 | async-start | bytes 8388608
  827.7 25.1 %slice-start.2 = ((s8[18874368]{0:T(1024)(128)(4,1)}), s8[4194304]{0:T(1024)(128)(4,1)S(1)}, s32[]{:S(2)}) async-start(s8[18874368]{0:T(1024)(128)(4,1)} %bitcast.596), calls=%async_computation.23 | async-start | bytes 8388608
  859.5 195.7 %copy-start.92 = (f32[1,1,512]{2,1,0:T(1,128)S(1)}, f32[1,1,512]{2,1,0:T(1,128)}, u32[]{:S(2)}) copy-start(f32[1,1,512]{2,1,0:T(1,128)} %copy-done.91) | copy-start | bytes 6148
  859.5 195.7 %copy-start.110 = (f32[1,1,512]{2,1,0:T(1,128)S(1)}, f32[1,1,512]{2,1,0:T(1,128)}, u32[]{:S(2)}) copy-start(f32[1,1,512]{2,1,0:T(1,128)} %copy-done.109) | copy-start | bytes 6148
  859.5 195.7 %copy-start.112 = (f32[1,1,512]{2,1,0:T(1,128)S(1)}, f32[1,1,512]{2,1,0:T(1,128)}, u32[]{:S(2)}) copy-start(f32[1,1,512]{2,1,0:T(1,128)} %copy-done.111) | copy-start | bytes 6148
  1087.6 272.5 %copy-start.1 = (bf16[2048,40]{0,1:T(8,128)(2,1)S(1)}, bf16[2048,40]{0,1:T(8,128)(2,1)}, u32[]{:S(2)}) copy-start(bf16[2048,40]{0,1:T(8,128)(2,1)} %param.24) | copy-start | bytes 491524
  (97 other events, 504.5 us)
Sparse Core Ops, SparseCore 0:
  10.2 51.9 all-gather.6
  64.3 47.7 all-gather.10
  114.2 47.7 all-gather.8
  164.0 123.4 all-gather.14
  289.4 123.5 all-gather.16
  414.9 49.2 all-gather.12
  469.7 49.5 all-reduce.5
  544.3 69.4 all-reduce.7
  616.5 153.6 all-reduce.9
  773.6 67.8 reduce-scatter.10
  845.1 67.2 reduce-scatter.12
  915.8 66.8 reduce-scatter.8
  986.8 66.5 reduce-scatter.6
  1056.9 148.0 reduce-scatter.14
  1208.9 148.4 reduce-scatter.16
where the time goes:
time: 1380 us; the launch traced here: 1370 us
  waiting for transfers between devices  987 us (72%)
  other arithmetic  151 us (11%)
  matrix products  131 us (9%)
  local copies, waits for them, and re-layouts  42.5 us (3%)
  blocking collectives  38 us (3%)
  between operations  16.4 us (1%)
    psum x1, waiting for transfers between devices, body(): lax.psum(mlp_normed_grad.astype(jnp.bfloat16), 'tensor').astype(jnp.float32)  155 us
    reduce_scatter x1, waiting for transfers between devices, body(): lax.psum_scatter(grad_down.astype(jnp.bfloat16), 'dp', scatter_dimension=...  150 us
    dot_general x24, matrix products, matmul(): return jnp.dot(left_op, right_op, preferred_element_type=jnp.float32)  121 us
    reduce_scatter x1, waiting for transfers between devices, body(): lax.psum_scatter(grad_up.astype(jnp.bfloat16), 'dp', scatter_dimension=0,...  115 us
    all_gather x1, waiting for transfers between devices, body(): lax.all_gather(w_up, 'dp', axis=0, tiled=True)  107 us
    all_gather x1, waiting for transfers between devices, body(): lax.all_gather(w_down, 'dp', axis=1, tiled=True)  96.7 us
    reduce_scatter x1, waiting for transfers between devices, body(): lax.psum_scatter(grad_query.astype(jnp.bfloat16), 'dp', scatter_dimension...  68.9 us
    reduce_scatter x1, waiting for transfers between devices, body(): lax.psum_scatter(grad_key.astype(jnp.bfloat16), 'dp', scatter_dimension=0...  68.5 us
  transfers between devices with their start and end apart: 15, of which 13 were waited for; matrix products, arithmetic and copies ran while one was open for 20% of the time, Pallas kernels for 0%

commit v1 on v0

v1 whole, which is shorter than its diff:
```python
import jax
import jax.numpy as jnp
from jax import lax
from jax.experimental import pallas as pl
from jax.experimental.pallas import tpu as pltpu
from jax.sharding import PartitionSpec as P

HEAD_DIM = 128
ROT = 32


EPSILON = 1e-05
ROPE_BASE = 10000.0

F32 = jnp.float32
BF16 = jnp.bfloat16


def layer_norm(values, gain_row):
    center = values - jnp.mean(values, axis=-1, keepdims=True)
    spread = jnp.mean(center * center, axis=-1, keepdims=True)
    return center * lax.rsqrt(spread + EPSILON) * gain_row


def rotary_tables(segments):
    tok_count = segments.shape[0]
    order_idx = jnp.arange(tok_count, dtype=jnp.int32)
    same_doc = segments[:, None] == segments[None, :]
    earlier = order_idx[None, :] < order_idx[:, None]
    places = jnp.sum((same_doc & earlier).astype(jnp.int32), axis=1)
    halves = jnp.arange(ROT // 2, dtype=jnp.float32)
    frequency = ROPE_BASE ** (-2.0 * halves / ROT)
    angles = places.astype(jnp.float32)[:, None] * frequency[None, :]
    allowed = same_doc & (order_idx[None, :] <= order_idx[:, None])
    return (jnp.cos(angles)[:, None, :], jnp.sin(angles)[:, None, :], allowed)


def rotate(values, cosine, sine_tab):
    first_half = values[..., : ROT // 2]
    second = values[..., ROT // 2 : ROT]
    return jnp.concatenate(
        [
            first_half * cosine - second * sine_tab,
            second * cosine + first_half * sine_tab,
            values[..., ROT:],
        ],
        axis=-1,
    )


def gelu_exact(values):
    return jax.nn.gelu(values, approximate=False)


def matmul(left_op, right_op):
    return jnp.dot(left_op, right_op, preferred_element_type=jnp.float32)


MIB = 1 << 20
GROUP = 16
CHUNK = 512


def mix_norm_kernel(history, mix, gains, streams, normed, stats):
    states, tokens, width = history.shape
    inverse = 1.0 / width

    @pl.loop(0, tokens // GROUP)
    def _(step):
        rows = pl.ds(pl.multiple_of(step * GROUP, GROUP), GROUP)
        weights = mix[rows, :]
        sums = [jnp.zeros((GROUP, 128), F32) for _ in range(4)]
        for at in range(0, width, CHUNK):
            cols = pl.ds(at, CHUNK)
            total = [None] * 4
            for source in range(states):
                state = history[source, rows, cols].astype(F32)
                for stream in range(4):
                    k = stream * states + source
                    term = weights[:, k : k + 1] * state
                    total[stream] = term if source == 0 else total[stream] + term
            for stream in range(4):
                streams[stream, rows, cols] = total[stream]
                for lane in range(0, CHUNK, 128):
                    sums[stream] = sums[stream] + total[stream][:, lane : lane + 128]
        for stream in range(4):
            mean = jnp.sum(sums[stream], axis=1, keepdims=True) * inverse
            square = jnp.zeros((GROUP, 128), F32)
            for at in range(0, width, CHUNK):
                center = streams[stream, rows, pl.ds(at, CHUNK)] - mean
                center = center * center
                for lane in range(0, CHUNK, 128):
                    square = square + center[:, lane : lane + 128]
            scale = lax.rsqrt(jnp.sum(square, axis=1, keepdims=True) * inverse + EPSILON)
            stats[rows, stream : stream + 1] = mean
            stats[rows, 4 + stream : 5 + stream] = scale
            for at in range(0, width, CHUNK):
                cols = pl.ds(at, CHUNK)
                center = streams[stream, rows, cols] - mean
                gain = gains[stream : stream + 1, cols]
                normed[stream, rows, cols] = (center * scale * gain).astype(BF16)


def mix_norm(history, mix, gains, block=64):
    states, tokens, width = history.shape
    return pl.pallas_call(
        mix_norm_kernel,
        grid=(tokens // block,),
        in_specs=[
            pl.BlockSpec((states, block, width), lambda i: (0, i, 0)),
            pl.BlockSpec((block, mix.shape[1]), lambda i: (i, 0)),
            pl.BlockSpec(gains.shape, lambda i: (0, 0)),
        ],
        out_specs=[
            pl.BlockSpec((4, block, width), lambda i: (0, i, 0)),
            pl.BlockSpec((4, block, width), lambda i: (0, i, 0)),
            pl.BlockSpec((block, 8), lambda i: (i, 0)),
        ],
        out_shape=[
            jax.ShapeDtypeStruct((4, tokens, width), F32),
            jax.ShapeDtypeStruct((4, tokens, width), BF16),
            jax.ShapeDtypeStruct((tokens, 8), F32),
        ],
        cost_estimate=pl.CostEstimate(
            flops=tokens * width * 100, bytes_accessed=tokens * width * 42, transcendentals=0
        ),
        compiler_params=pltpu.CompilerParams(vmem_limit_bytes=40 * MIB),
        name="mix_norm",
    )(history, mix, gains)


def mix_back_kernel(history, mix, gains, streams, stats, grads, out_total, history_grad, mix_grad, gain_grad, held):
    states, tokens, width = history.shape
    inverse = 1.0 / width

    @pl.when(pl.program_id(0) == 0)
    def _():
        gain_grad[...] = jnp.zeros_like(gain_grad)

    @pl.loop(0, tokens // GROUP)
    def _(step):
        rows = pl.ds(pl.multiple_of(step * GROUP, GROUP), GROUP)
        weights = mix[rows, :]
        for stream in range(4):
            mean = stats[rows, stream : stream + 1]
            scale = stats[rows, 4 + stream : 5 + stream]
            sum_e = jnp.zeros((GROUP, 128), F32)
            sum_ex = jnp.zeros((GROUP, 128), F32)
            for at in range(0, width, CHUNK):
                cols = pl.ds(at, CHUNK)
                unit = (streams[stream, rows, cols] - mean) * scale
                upstream = grads[stream, rows, cols].astype(F32)
                e = upstream * gains[stream : stream + 1, cols]
                gain = upstream * unit
                gain_grad[stream, :, cols] += gain[:8] + gain[8:]
                ex = e * unit
                for lane in range(0, CHUNK, 128):
                    sum_e = sum_e + e[:, lane : lane + 128]
                    sum_ex = sum_ex + ex[:, lane : lane + 128]
            mean_e = jnp.sum(sum_e, axis=1, keepdims=True) * inverse
            mean_ex = jnp.sum(sum_ex, axis=1, keepdims=True) * inverse
            for at in range(0, width, CHUNK):
                cols = pl.ds(at, CHUNK)
                unit = (streams[stream, rows, cols] - mean) * scale
                e = grads[stream, rows, cols].astype(F32) * gains[stream : stream + 1, cols]
                grad = scale * (e - mean_e - unit * mean_ex)
                if stream == 3:
                    grad = grad + out_total[rows, cols]
                held[stream, :, cols] = grad
        for source in range(states):
            sums = [jnp.zeros((GROUP, 128), F32) for _ in range(4)]
            for at in range(0, width, CHUNK):
                cols = pl.ds(at, CHUNK)
                state = history[source, rows, cols].astype(F32)
                total = None
                for stream in range(4):
                    k = stream * states + source
                    grad = held[stream, :, cols]
                    term = weights[:, k : k + 1] * grad
                    total = term if total is None else total + term
                    product = state * grad
                    for lane in range(0, CHUNK, 128):
                        sums[stream] = sums[stream] + product[:, lane : lane + 128]
                history_grad[source, rows, cols] = total.astype(BF16)
            for stream in range(4):
                k = stream * states + source
                mix_grad[rows, k : k + 1] = jnp.sum(sums[stream], axis=1, keepdims=True)


def mix_back(history, mix, gains, streams, stats, grads, out_total, block=64):
    states, tokens, width = history.shape
    return pl.pallas_call(
        mix_back_kernel,
        grid=(tokens // block,),
        in_specs=[
            pl.BlockSpec((states, block, width), lambda i: (0, i, 0)),
            pl.BlockSpec((block, mix.shape[1]), lambda i: (i, 0)),
            pl.BlockSpec(gains.shape, lambda i: (0, 0)),
            pl.BlockSpec((4, block, width), lambda i: (0, i, 0)),
            pl.BlockSpec((block, 8), lambda i: (i, 0)),
            pl.BlockSpec((4, block, width), lambda i: (0, i, 0)),
            pl.BlockSpec((block, width), lambda i: (i, 0)),
        ],
        out_specs=[
            pl.BlockSpec((states, block, width), lambda i: (0, i, 0)),
            pl.BlockSpec((block, mix.shape[1]), lambda i: (i, 0)),
            pl.BlockSpec((4, 8, width), lambda i: (0, 0, 0)),
        ],
        out_shape=[
            jax.ShapeDtypeStruct((states, tokens, width), BF16),
            jax.ShapeDtypeStruct((tokens, mix.shape[1]), F32),
            jax.ShapeDtypeStruct((4, 8, width), F32),
        ],
        scratch_shapes=[pltpu.VMEM((4, GROUP, width), F32)],
        cost_estimate=pl.CostEstimate(
            flops=tokens * width * 200, bytes_accessed=tokens * width * 64, transcendentals=0
        ),
        compiler_params=pltpu.CompilerParams(vmem_limit_bytes=48 * MIB),
        name="mix_back",
    )(history, mix, gains, streams, stats, grads, out_total)


def gelu(x):
    return 0.5 * x * (1.0 + lax.erf(x * (0.5**0.5)))


def gelu_slope(x):
    return 0.5 * (1.0 + lax.erf(x * (0.5**0.5))) + x * jnp.exp(-0.5 * x * x) * 0.3989422804014327


def dot(a, b, dims):
    return lax.dot_general(a, b, (dims, ((), ())), preferred_element_type=F32)


def gen_kernel(stream, branch, gain, gen_in, gen_out, out_grad, next_grad, layer_out, next_mix, out_total, branch_grad, gain_grad, in_grad, mid_grad):
    first = pl.program_id(0) == 0
    x = stream[0] + branch[...].astype(F32)
    layer_out[...] = x.astype(BF16)
    center = x - jnp.mean(x, axis=1, keepdims=True)
    scale = lax.rsqrt(jnp.mean(center * center, axis=1, keepdims=True) + EPSILON)
    unit = center * scale
    gains = gain[4:5, :]
    low = (unit * gains).astype(BF16)
    hidden = dot(low, gen_in[...], ((1,), (0,)))
    active = gelu(hidden).astype(BF16)
    next_mix[...] = dot(active, gen_out[...], ((1,), (0,)))
    upstream = next_grad[...].astype(BF16)
    active_grad = dot(upstream, gen_out[...], ((1,), (1,)))
    hidden_grad = (active_grad * gelu_slope(hidden)).astype(BF16)
    y = dot(hidden_grad, gen_in[...], ((1,), (1,)))
    e = y * gains
    grad = scale * (
        e - jnp.mean(e, axis=1, keepdims=True) - unit * jnp.mean(e * unit, axis=1, keepdims=True)
    )
    total = out_grad[...].astype(F32) + grad
    out_total[...] = total
    branch_grad[...] = total.astype(BF16)
    gain_part = jnp.sum(y * unit, axis=0, keepdims=True)
    in_part = dot(hidden_grad, low, ((0,), (0,)))
    mid_part = dot(active, upstream, ((0,), (0,)))

    @pl.when(first)
    def _():
        gain_grad[...] = gain_part
        in_grad[...] = in_part
        mid_grad[...] = mid_part

    @pl.when(jnp.logical_not(first))
    def _():
        gain_grad[...] += gain_part
        in_grad[...] += in_part
        mid_grad[...] += mid_part


def gen_stage(streams, branch, gains, gen_in, gen_out, out_grad, next_grad, block=128):
    _, tokens, width = streams.shape
    units = gen_in.shape[1]
    nxt = gen_out.shape[1]
    row = lambda i: (i, 0)
    fixed = lambda i: (0, 0)
    return pl.pallas_call(
        gen_kernel,
        grid=(tokens // block,),
        in_specs=[
            pl.BlockSpec((1, block, width), lambda i: (3, i, 0)),
            pl.BlockSpec((block, width), row),
            pl.BlockSpec(gains.shape, fixed),
            pl.BlockSpec(gen_in.shape, fixed),
            pl.BlockSpec(gen_out.shape, fixed),
            pl.BlockSpec((block, width), row),
            pl.BlockSpec((block, nxt), row),
        ],
        out_specs=[
            pl.BlockSpec((block, width), row),
            pl.BlockSpec((block, nxt), row),
            pl.BlockSpec((block, width), row),
            pl.BlockSpec((block, width), row),
            pl.BlockSpec((1, width), fixed),
            pl.BlockSpec((units, width), fixed),
            pl.BlockSpec((units, nxt), fixed),
        ],
        out_shape=[
            jax.ShapeDtypeStruct((tokens, width), BF16),
            jax.ShapeDtypeStruct((tokens, nxt), F32),
            jax.ShapeDtypeStruct((tokens, width), F32),
            jax.ShapeDtypeStruct((tokens, width), BF16),
            jax.ShapeDtypeStruct((1, width), F32),
            jax.ShapeDtypeStruct((units, width), F32),
            jax.ShapeDtypeStruct((units, nxt), F32),
        ],
        cost_estimate=pl.CostEstimate(
            flops=tokens * width * 300, bytes_accessed=tokens * width * 16, transcendentals=0
        ),
        compiler_params=pltpu.CompilerParams(vmem_limit_bytes=48 * MIB),
        name="gen_stage",
    )(streams, branch, gains, gen_in, gen_out, out_grad, next_grad)


def after(value, *others):
    return lax.optimization_barrier((value,) + others)[0]


class Ring:
    def __init__(self, size):
        self.size = size
        self.half = size // 2
        order = [2 * p if p < self.half else 2 * (size - 1 - p) + 1 for p in range(size)]
        self.right = [(order[p], order[(p + 1) % size]) for p in range(size)]
        self.left = [(b, a) for a, b in self.right]
        me = lax.axis_index("dp")
        self.place = jnp.where(lax.rem(me, 2) == 0, me // 2, size - 1 - me // 2)
        self.me = me

    def owner(self, shift):
        at = lax.rem(self.place + shift + self.size, self.size)
        return jnp.where(at < self.half, 2 * at, 2 * (self.size - 1 - at) + 1)

    def to_right(self, value):
        return lax.ppermute(value, "dp", self.right)

    def to_left(self, value):
        return lax.ppermute(value, "dp", self.left)

    def gather(self, shard):
        found = [(self.me, shard)]
        from_left, from_right = shard, shard
        for step in range(1, self.half):
            from_left, from_right = self.to_right(from_left), self.to_left(from_right)
            found.append((self.owner(-step), from_left))
            found.append((self.owner(step), from_right))
        cut = shard.shape[0] // 2
        top = self.to_right(from_left[:cut])
        low = self.to_left(from_right[cut:])
        found.append((self.owner(self.half), jnp.concatenate([top, low], axis=0)))
        return found

    def scatter(self, term, start=None):
        far = term(self.owner(self.half))
        cut = far.shape[0] // 2
        far = far.astype(BF16)
        if start is not None:
            far = after(far, start)
        top = self.to_right(far[:cut])
        low = self.to_left(far[cut:])
        near_right = term(self.owner(self.half - 1))
        near_left = term(self.owner(-(self.half - 1)))
        going_right = jnp.concatenate([near_right[:cut] + top.astype(F32), near_right[cut:]], axis=0)
        going_left = jnp.concatenate([near_left[:cut], near_left[cut:] + low.astype(F32)], axis=0)
        for distance in range(self.half - 1, 1, -1):
            got_left = self.to_right(going_right.astype(BF16))
            got_right = self.to_left(going_left.astype(BF16))
            going_right = term(self.owner(distance - 1)) + got_left.astype(F32)
            going_left = term(self.owner(1 - distance)) + got_right.astype(F32)
        got_left = self.to_right(going_right.astype(BF16))
        got_right = self.to_left(going_left.astype(BF16))
        return term(self.me) + got_left.astype(F32) + got_right.astype(F32)


def total_over(value, axis, size):
    bit = 1
    while bit < size:
        other = lax.ppermute(value, axis, [(i, i ^ bit) for i in range(size)])
        value = value + other
        bit *= 2
    return value


def tensor_sum(value, size):
    rows = value.shape[0] // 2
    core = lax.rem(lax.axis_index("tensor"), 2)
    swap = [(i, i ^ 1) for i in range(size)]
    low = value.astype(BF16)
    mine = lax.dynamic_slice_in_dim(low, core * rows, rows, 0)
    other = lax.dynamic_slice_in_dim(low, (1 - core) * rows, rows, 0)
    part = (mine.astype(F32) + lax.ppermute(other, "tensor", swap).astype(F32)).astype(BF16)
    bit = 2
    while bit < size:
        got = lax.ppermute(part, "tensor", [(i, i ^ bit) for i in range(size)])
        part = (part.astype(F32) + got.astype(F32)).astype(BF16)
        bit *= 2
    twin = lax.ppermute(part, "tensor", swap)
    first = jnp.where(core == 0, part, twin)
    second = jnp.where(core == 0, twin, part)
    return jnp.concatenate([first, second], axis=0)


def body(
    sizes,
    history,
    mix_weights,
    segments,
    norm_gains,
    w_query,
    w_key,
    w_value,
    w_out,
    w_up,
    w_down,
    gen_in,
    gen_out,
    out_grad,
    next_grad,
):
    dp_size, tensor_size = sizes
    states = history.shape[0]
    tok_count = history.shape[1]
    width = history.shape[2]
    local_cols = w_query.shape[1]
    local_hidden = w_up.shape[1]
    local_heads = local_cols // HEAD_DIM
    shard = w_query.shape[0]
    ring = Ring(dp_size)

    qkv_blocks = ring.gather(jnp.concatenate([w_query, w_key, w_value], axis=1))
    up_blocks = ring.gather(w_up)
    out_blocks = ring.gather(
        after(jnp.concatenate([w_out, w_down], axis=0), qkv_blocks[-2][1])
    )

    def by_rows(blocks):
        full = jnp.zeros((width, blocks[0][1].shape[1]), BF16)
        for owner, block in blocks:
            full = lax.dynamic_update_slice_in_dim(full, block, owner * shard, 0)
        return full

    def by_columns(blocks):
        full = jnp.zeros((blocks[0][1].shape[0], width), BF16)
        for owner, block in blocks:
            full = lax.dynamic_update_slice_in_dim(full, block, owner * shard, 1)
        return full

    mix_rows = mix_weights.T
    streams, normed, stats = mix_norm(history, mix_rows, norm_gains)
    cosine, sine_tab, allowed = rotary_tables(segments)

    full_qkv = by_rows(qkv_blocks)
    full_query = full_qkv[:, :local_cols]
    full_key = full_qkv[:, local_cols : 2 * local_cols]
    full_value = full_qkv[:, 2 * local_cols :]
    full_up = by_rows(up_blocks)

    def split_heads(values):
        return values.reshape(tok_count, local_heads, HEAD_DIM)

    query_heads = rotate(split_heads(matmul(normed[0], full_query)), cosine, sine_tab).astype(
        jnp.bfloat16
    )
    key_heads = rotate(split_heads(matmul(normed[1], full_key)), cosine, sine_tab).astype(
        jnp.bfloat16
    )
    value_heads = split_heads(matmul(normed[2], full_value)).astype(jnp.bfloat16)
    score_scale = HEAD_DIM ** (-0.5)
    raw_scores = (
        jnp.einsum("thd,uhd->htu", query_heads, key_heads, preferred_element_type=jnp.float32)
        * score_scale
    )
    masked = jnp.where(allowed[None], raw_scores, -1e30)
    row_max = jnp.max(masked, axis=-1, keepdims=True)
    exp_scores = jnp.exp(masked - row_max)
    attn_probs = exp_scores / jnp.sum(exp_scores, axis=-1, keepdims=True)
    probs_low = attn_probs.astype(jnp.bfloat16)
    attended = (
        jnp.einsum("htu,uhd->thd", probs_low, value_heads, preferred_element_type=jnp.float32)
        .astype(jnp.bfloat16)
        .reshape(tok_count, local_cols)
    )
    hidden = matmul(normed[3], full_up)
    active = gelu_exact(hidden).astype(jnp.bfloat16)
    both_low = jnp.concatenate([attended, active], axis=1)
    branch = jnp.zeros((tok_count, width), BF16)
    groups = [out_blocks[:1]] + [out_blocks[at : at + 2] for at in range(1, len(out_blocks), 2)]
    for group in groups:
        part = jnp.concatenate([matmul(both_low, block) for _, block in group], axis=1)
        summed = tensor_sum(part, tensor_size)
        for at, (owner, _) in enumerate(group):
            branch = lax.dynamic_update_slice_in_dim(
                branch, summed[:, at * shard : (at + 1) * shard], owner * shard, 1
            )
    layer_out, next_mix, out_total, branch_grad, gain_gen_grad, grad_gen_in, grad_gen_out = gen_stage(
        streams, branch, norm_gains, gen_in, gen_out, out_grad, next_grad.T
    )

    full_out_down = by_columns(out_blocks)

    def columns_of(array, owner):
        return lax.dynamic_slice_in_dim(array, owner * shard, shard, 1)

    grad_out_down = ring.scatter(lambda owner: matmul(both_low.T, columns_of(branch_grad, owner)))

    both_grad = matmul(branch_grad, full_out_down.T)
    active_grad = both_grad[:, local_cols:]
    gelu_mlp = jax.vjp(gelu_exact, hidden)[1]
    hidden_grad = gelu_mlp(active_grad)[0].astype(jnp.bfloat16)
    grad_up = ring.scatter(lambda owner: matmul(columns_of(normed[3], owner).T, hidden_grad))
    mlp_normed_grad = matmul(hidden_grad, full_up.T)
    attended_grad = (
        both_grad[:, :local_cols].astype(jnp.bfloat16).reshape(tok_count, local_heads, HEAD_DIM)
    )
    probs_grad = jnp.einsum(
        "thd,uhd->htu", attended_grad, value_heads, preferred_element_type=jnp.float32
    )
    values_grad = jnp.einsum(
        "htu,thd->uhd", probs_low, attended_grad, preferred_element_type=jnp.float32
    ).astype(jnp.bfloat16)
    row_dot = jnp.sum(attn_probs * probs_grad, axis=-1, keepdims=True)
    scores_grad = (attn_probs * (probs_grad - row_dot)).astype(jnp.bfloat16)
    query_grad = (
        jnp.einsum("htu,uhd->thd", scores_grad, key_heads, preferred_element_type=jnp.float32)
        * score_scale
    )
    key_grad = (
        jnp.einsum("htu,thd->uhd", scores_grad, query_heads, preferred_element_type=jnp.float32)
        * score_scale
    )
    query_low = (
        rotate(query_grad, cosine, -sine_tab).reshape(tok_count, local_cols).astype(jnp.bfloat16)
    )
    key_low = (
        rotate(key_grad, cosine, -sine_tab).reshape(tok_count, local_cols).astype(jnp.bfloat16)
    )
    value_low = values_grad.reshape(tok_count, local_cols)

    def qkv_term(owner):
        return jnp.concatenate(
            [
                matmul(columns_of(normed[0], owner).T, query_low),
                matmul(columns_of(normed[1], owner).T, key_low),
                matmul(columns_of(normed[2], owner).T, value_low),
            ],
            axis=1,
        )

    grad_qkv = ring.scatter(qkv_term, grad_out_down)
    summed_grads = (
        tensor_sum(matmul(query_low, full_query.T), tensor_size),
        tensor_sum(matmul(key_low, full_key.T), tensor_size),
        tensor_sum(matmul(value_low, full_value.T), tensor_size),
        tensor_sum(mlp_normed_grad, tensor_size),
    )
    history_grad, mix_grad, gain_grads = mix_back(
        history, mix_rows, norm_gains, streams, stats, jnp.stack(summed_grads), out_total
    )
    gain_rows = jnp.concatenate([jnp.sum(gain_grads, axis=1), gain_gen_grad], axis=0)
    out_rows = jnp.pad(grad_gen_out, ((0, 0), (0, width - gen_out.shape[1])))
    small = total_over(jnp.concatenate([gain_rows, grad_gen_in, out_rows], axis=0), "dp", dp_size)
    gains = gain_rows.shape[0]
    hidden_units = gen_in.shape[1]
    return (
        layer_out,
        next_mix.T,
        history_grad,
        mix_grad.T,
        small[:gains],
        grad_qkv[:, :local_cols],
        grad_qkv[:, local_cols : 2 * local_cols],
        grad_qkv[:, 2 * local_cols :],
        grad_out_down[:local_cols],
        grad_up,
        grad_out_down[local_cols:],
        small[gains : gains + hidden_units].T,
        small[gains + hidden_units :, : gen_out.shape[1]],
    )


def solution(mesh):
    sizes = (mesh.shape["dp"], mesh.shape["tensor"])
    in_specs = (
        P(None, "dp", None),
        P(None, "dp"),
        P("dp"),
        P(),
        P("dp", "tensor"),
        P("dp", "tensor"),
        P("dp", "tensor"),
        P("tensor", "dp"),
        P("dp", "tensor"),
        P("tensor", "dp"),
        P(),
        P(),
        P("dp", None),
        P(None, "dp"),
    )
    out_specs = (
        P("dp", None),
        P(None, "dp"),
        P(None, "dp", None),
        P(None, "dp"),
        P(),
        P("dp", "tensor"),
        P("dp", "tensor"),
        P("dp", "tensor"),
        P("tensor", "dp"),
        P("dp", "tensor"),
        P("tensor", "dp"),
        P(),
        P(),
    )

    def step(*arrays):
        return body(sizes, *arrays)

    return jax.shard_map(step, mesh=mesh, in_specs=in_specs, out_specs=out_specs, check_vma=False)
```

time: 1380 us -> 758 us (0.55)
  waiting for transfers between devices: 987 us -> 322 us
  other arithmetic: 151 us -> 46.9 us
  starting transfers between devices: 1.18 us -> 79.5 us
  Pallas kernels: 0 us -> 72.3 us
  local copies, waits for them, and re-layouts: 42.5 us -> 107 us
  blocking collectives: 38 us -> 0 us
    reduce_scatter x6 -> x0, waiting for transfers between devices: 442 us -> none  [the longest x1 150 us: body(): lax.psum_scatter(grad_down.astype(jnp.bfloat16), 'dp', scatter_dimension=...]
    all_gather x6 -> x0, waiting for transfers between devices: 335 us -> none  [the longest x1 107 us: body(): lax.all_gather(w_up, 'dp', axis=0, tiled=True)]
    ppermute x0 -> x78, waiting for transfers between devices: none -> 322 us  [the longest x24 187 us: to_left(): return lax.ppermute(value, 'dp', self.left)]
    psum x3 -> x0, waiting for transfers between devices: 206 us -> none  [the longest x1 155 us: body(): lax.psum(mlp_normed_grad.astype(jnp.bfloat16), 'tensor').astype(jnp.float32)]
    reduce_sum x22 -> x1, other arithmetic: 85.3 us -> 0.08 us  [body(): jnp.sum(gain_grads, axis=1)]
    ppermute x0 -> x78, starting transfers between devices: none -> 79.5 us  [the longest x24 36.7 us: to_right(): return lax.ppermute(value, 'dp', self.right)]
    pallas_call x0 -> x3, Pallas kernels: none -> 72.3 us  [the longest x1 40.7 us: mix_back(): pl.pallas_call(mix_back_kernel, grid=(tokens // block,), in_specs=[pl.Blo...]
    psum x1 -> x0, blocking collectives: 38 us -> none  [body(): lax.psum(jnp.stack(gain_grads).astype(jnp.bfloat16), 'dp')]
  transfers between devices with their start and end apart: 15 -> 78, of which waited for: 13 -> 34; matrix products, arithmetic and copies ran while one was open for 20% -> 25% of each run, Pallas kernels for 0% -> 8%
where the time goes in v1:
time: 758 us; the launch traced here: 752 us
  waiting for transfers between devices  322 us (42%)
  matrix products  121 us (16%)
  local copies, waits for them, and re-layouts  107 us (14%)
  starting transfers between devices  79.5 us (10%)
  Pallas kernels  72.3 us (10%)
  other arithmetic  46.9 us (6%)
    ppermute x24, waiting for transfers between devices, to_left(): return lax.ppermute(value, 'dp', self.left)  187 us
    dot_general x57, matrix products, matmul(): return jnp.dot(left_op, right_op, preferred_element_type=jnp.float32)  108 us
    ppermute x9, waiting for transfers between devices, tensor_sum(): got = lax.ppermute(part, 'tensor', [(i, i ^ bit) for i in range(size)])  59.7 us
    ppermute x24, waiting for transfers between devices, to_right(): return lax.ppermute(value, 'dp', self.right)  49.2 us
    pallas_call x1, Pallas kernels, mix_back(): pl.pallas_call(mix_back_kernel, grid=(tokens // block,), in_specs=[pl.Blo...  40.7 us
    ppermute x24, starting transfers between devices, to_right(): return lax.ppermute(value, 'dp', self.right)  36.7 us
    ppermute x24, starting transfers between devices, to_left(): return lax.ppermute(value, 'dp', self.left)  25.5 us
    dynamic_update_slice x15, local copies, waits for them, and re-layouts, by_rows(): full = lax.dynamic_update_slice_in_dim(full, block, owner * shard, 0)  23.1 us
  transfers between devices with their start and end apart: 78, of which 34 were waited for; matrix products, arithmetic and copies ran while one was open for 25% of the time, Pallas kernels for 8%

profile of v1, /device:TPU:0, one launch (start us, length us, event | category | flops | bytes accessed | tf_op | source)
XLA Modules:
  0.0 752.0 jit_solution(5792051210853484040)
XLA Ops:
  5.7 2.9 collective-permute-start.1
  17.5 3.3 copy-done.8
  20.8 3.4 broadcast_in_dim.17
  26.7 23.1 %mix_norm.1 = (f32[4,512,2048]{2,1,0:T(8,128)}, bf16[4,512,2048]{2,1,0:T(8,128)(2,1)S(1)}, f32[512,8]{1,0:T(8,128)S(1)}) custom-call(bf16[9,512,2048]{2,1,0:T(8,128)(2,1)} %history.3, f32[512,36]{1,0:T(8,128)S(1)} %bitcast.208, f32[5,2048]{1,0:T(8,128)S(1)} %copy-done.2), custom_call_target="tpu_custom_call" | custom-call | flops 104857600 | bytes 44040192 | tf_op jit(solution)/shard_map/mix_norm/pallas_call | solution.py:106
  49.7 3.7 fusion.221
  64.6 2.4 constant_dynamic-update-slice_fusion.13
  67.0 2.3 constant_dynamic-update-slice_fusion.12
  69.3 8.5 %collective-permute-done.2 = bf16[256,1536]{1,0:T(8,128)(2,1)} collective-permute-done((bf16[256,1536]{1,0:T(8,128)(2,1)}, bf16[256,1536]{1,0:T(8,128)(2,1)}, u32[]{:S(2)}, u32[]{:S(2)}) %collective-permute-start.2) | collective-permute-done | bytes 786464 | tf_op jit(solution)/shard_map/ppermute | solution.py:339
  84.6 17.7 %collective-permute-done.11 = bf16[256,2048]{1,0:T(8,128)(2,1)} collective-permute-done((bf16[256,2048]{1,0:T(8,128)(2,1)}, bf16[256,2048]{1,0:T(8,128)(2,1)}, u32[]{:S(2)}, u32[]{:S(2)}) %collective-permute-start.11) | collective-permute-done | bytes 1048608 | tf_op jit(solution)/shard_map/ppermute | solution.py:342
  104.3 2.4 constant_dynamic-update-slice_fusion.11
  106.7 2.3 constant_dynamic-update-slice_fusion.10
  109.0 10.1 %collective-permute-done.5 = bf16[256,1536]{1,0:T(8,128)(2,1)} collective-permute-done((bf16[256,1536]{1,0:T(8,128)(2,1)}, bf16[256,1536]{1,0:T(8,128)(2,1)}, u32[]{:S(2)}, u32[]{:S(2)}) %collective-permute-start.5) | collective-permute-done | bytes 786464 | tf_op jit(solution)/shard_map/ppermute | solution.py:342
  129.6 5.4 broadcast_in_dim.25
  136.1 13.9 %collective-permute-done.7 = bf16[128,1536]{1,0:T(8,128)(2,1)} collective-permute-done((bf16[128,1536]{1,0:T(8,128)(2,1)}, bf16[128,1536]{1,0:T(8,128)(2,1)}, u32[]{:S(2)}, u32[]{:S(2)}) %collective-permute-start.7) | collective-permute-done | bytes 393248 | tf_op jit(solution)/shard_map/ppermute | solution.py:342
  156.2 5.3 fusion.222
  161.5 2.9 fusion.12
  164.4 2.9 fusion.10
  168.3 4.8 fusion.227
  173.0 3.7 fusion.28
  186.4 2.3 constant_dynamic-update-slice_fusion.9
  188.7 2.3 constant_dynamic-update-slice_fusion.8
  193.2 18.0 %multiply_convert_fusion.1 = (bf16[512,2048]{1,0:T(8,128)(2,1)S(1)}, f32[512,2048]{1,0:T(8,128)}, f32[512,2048]{1,0:T(8,128)}) fusion(bf16[2048,2048]{1,0:T(8,128)(2,1)} %maximum_dynamic-update-slice_fusion, bf16[4,512,2048]{2,1,0:T(8,128)(2,1)} %copy-done), kind=kOutput, calls=%fused_computation.7 | convolution fusion | flops 4363124736 | bytes 20971520 | tf_op jit(solution)/shard_map/dot_general | solution.py:56
  212.1 2.2 convolution_convert_fusion.14
  219.1 2.5 constant_dynamic-update-slice_fusion.6
  223.2 2.5 constant_dynamic-update-slice_fusion.5
  228.8 6.9 collective-permute-done.22
  235.8 12.5 %collective-permute-done.24 = bf16[2560,256]{1,0:T(8,128)(2,1)S(1)} collective-permute-done((bf16[2560,256]{1,0:T(8,128)(2,1)}, bf16[2560,256]{1,0:T(8,128)(2,1)S(1)}, u32[]{:S(2)}, u32[]{:S(2)}) %collective-permute-start.24) | collective-permute-done | bytes 1310752 | tf_op jit(solution)/shard_map/ppermute | solution.py:339
  251.6 11.5 %collective-permute-start.29 = (bf16[2560,256]{1,0:T(8,128)(2,1)S(1)}, bf16[2560,256]{1,0:T(8,128)(2,1)S(1)}, u32[]{:S(2)}, u32[]{:S(2)}) collective-permute-start(bf16[2560,256]{1,0:T(8,128)(2,1)S(1)} %collective-permute-done.24), channel_id=1, source_target_pairs={{0,8},{8,16},{16,24},{24,28},{28,20},{20,12},{12,4},{4,0},{1,9},{9... | collective-permute-start | bytes 3932168 | tf_op jit(solution)/shard_map/ppermute | solution.py:339
  265.9 5.6 collective-permute-done.27
  273.3 8.1 %collective-permute-done.30 = bf16[2560,256]{1,0:T(8,128)(2,1)S(1)} collective-permute-done((bf16[2560,256]{1,0:T(8,128)(2,1)S(1)}, bf16[2560,256]{1,0:T(8,128)(2,1)S(1)}, u32[]{:S(2)}, u32[]{:S(2)}) %collective-permute-start.30) | collective-permute-done | bytes 1310752 | tf_op jit(solution)/shard_map/ppermute | solution.py:342
  282.8 10.5 %collective-permute-done.29 = bf16[2560,256]{1,0:T(8,128)(2,1)S(1)} collective-permute-done((bf16[2560,256]{1,0:T(8,128)(2,1)S(1)}, bf16[2560,256]{1,0:T(8,128)(2,1)S(1)}, u32[]{:S(2)}, u32[]{:S(2)}) %collective-permute-start.29) | collective-permute-done | bytes 1310752 | tf_op jit(solution)/shard_map/ppermute | solution.py:339
  300.4 5.7 collective-permute-done.32
  306.2 3.2 collective-permute-done.34
  313.5 4.1 collective-permute-done.37
  319.2 8.5 %gen_stage.1 = (bf16[512,2048]{1,0:T(8,128)(2,1)}, f32[512,40]{1,0:T(8,128)S(1)}, f32[512,2048]{1,0:T(8,128)}, bf16[512,2048]{1,0:T(8,128)(2,1)S(1)}, f32[1,2048...) custom-call(f32[4,512,2048]{2,1,0:T(8,128)} %get-tuple-element.28.stream.streams, ...), custom_call_target="tpu_custom_call" | custom-call | flops 314572800 | bytes 16777216 | tf_op jit(solution)/shard_map/gen_stage/pallas_call | solution.py:281
  327.7 9.1 %fusion.228 = f32[512,2560]{1,0:T(8,128)S(1)} fusion(bf16[512,2048]{1,0:T(8,128)(2,1)S(1)} %get-tuple-element.34, bf16[2560,2048]{1,0:T(8,128)(2,1)} %constant_dynamic-update-slice_fusion), kind=kOutput, calls=%fused_computation.417 | convolution fusion | flops 5368709120 | bytes 17825792 | tf_op jit(solution)/shard_map/dot_general | solution.py:56
  336.9 2.3 copy-done.17
  339.5 3.2 convolution_convert_fusion.6
  353.3 5.0 convolution_convert_fusion.2
  360.6 6.1 convolution_convert_fusion.1
  373.3 2.4 fusion.131
  395.2 3.1 convolution_convert_fusion.4
  398.3 3.0 convolution_convert_fusion.3
  410.8 3.1 fusion.142
  416.3 2.5 fusion.152
  424.0 7.2 collective-permute-done.58
  441.6 15.8 %collective-permute-done.75 = bf16[256,2048]{1,0:T(8,128)(2,1)S(1)} collective-permute-done((bf16[256,2048]{1,0:T(8,128)(2,1)S(1)}, bf16[256,2048]{1,0:T(8,128)(2,1)S(1)}, u32[]{:S(2)}, u32[]{:S(2)}) %collective-permute-start.75) | collective-permute-done | bytes 1048608 | tf_op jit(solution)/shard_map/ppermute | solution.py:342
  462.8 22.3 %collective-permute-done.59 = bf16[2560,256]{1,0:T(8,128)(2,1)S(1)} collective-permute-done((bf16[2560,256]{1,0:T(8,128)(2,1)S(1)}, bf16[2560,256]{1,0:T(8,128)(2,1)S(1)}, u32[]{:S(2)}, u32[]{:S(2)}) %collective-permute-start.59) | collective-permute-done | bytes 1310752 | tf_op jit(solution)/shard_map/ppermute | solution.py:342
  493.0 17.7 %collective-permute-done.40 = bf16[256,2048]{1,0:T(8,128)(2,1)S(1)} collective-permute-done((bf16[256,2048]{1,0:T(8,128)(2,1)S(1)}, bf16[256,2048]{1,0:T(8,128)(2,1)S(1)}, u32[]{:S(2)}, u32[]{:S(2)}) %collective-permute-start.40) | collective-permute-done | bytes 1048608 | tf_op jit(solution)/shard_map/ppermute | solution.py:398
  512.8 18.7 %collective-permute-done.43 = bf16[256,2048]{1,0:T(8,128)(2,1)S(1)} collective-permute-done((bf16[256,2048]{1,0:T(8,128)(2,1)S(1)}, bf16[256,2048]{1,0:T(8,128)(2,1)S(1)}, u32[]{:S(2)}, u32[]{:S(2)}) %collective-permute-start.43) | collective-permute-done | bytes 1048608 | tf_op jit(solution)/shard_map/ppermute | solution.py:398
  536.4 3.8 collective-permute-done.60
  546.4 45.7 %collective-permute-done.61 = bf16[2560,256]{1,0:T(8,128)(2,1)S(1)} collective-permute-done((bf16[2560,256]{1,0:T(8,128)(2,1)S(1)}, bf16[2560,256]{1,0:T(8,128)(2,1)S(1)}, u32[]{:S(2)}, u32[]{:S(2)}) %collective-permute-start.61) | collective-permute-done | bytes 1310752 | tf_op jit(solution)/shard_map/ppermute | solution.py:342
  596.8 4.1 pad_maximum_fusion.grads
  601.3 40.7 %mix_back.1 = (bf16[9,512,2048]{2,1,0:T(8,128)(2,1)}, f32[512,36]{1,0:T(8,128)S(1)}, f32[4,8,2048]{2,1,0:T(8,128)S(1)}) custom-call(bf16[9,512,2048]{2,1,0:T(8,128)(2,1)} %history.3, f32[512,36]{1,0:T(8,128)S(1)} %bitcast.209, f32[5,2048]{1,0:T(8,128)S(1)} %copy-done.2, f32[4,512,2048]{2,1,0:T(8,128)} %get-tuple-element.28.stream.streams, ...), custom_call_target="tpu_custom_call" | custom-call | flops 209715200 | bytes 67108864 | tf_op jit(solution)/shard_map/mix_back/pallas_call | solution.py:192
  646.0 18.6 %collective-permute-done.66 = bf16[128,1536]{1,0:T(8,128)(2,1)S(1)} collective-permute-done((bf16[128,1536]{1,0:T(8,128)(2,1)}, bf16[128,1536]{1,0:T(8,128)(2,1)S(1)}, u32[]{:S(2)}, u32[]{:S(2)}) %collective-permute-start.66) | collective-permute-done | bytes 393248 | tf_op jit(solution)/shard_map/ppermute | solution.py:342
  664.8 2.4 collective-permute-start.67
  667.4 7.0 collective-permute-done.63
  675.6 9.8 %collective-permute-done.67 = bf16[256,1536]{1,0:T(8,128)(2,1)S(1)} collective-permute-done((bf16[256,1536]{1,0:T(8,128)(2,1)S(1)}, bf16[256,1536]{1,0:T(8,128)(2,1)S(1)}, u32[]{:S(2)}, u32[]{:S(2)}) %collective-permute-start.67) | collective-permute-done | bytes 786464 | tf_op jit(solution)/shard_map/ppermute | solution.py:342
  686.4 2.5 add_convert_fusion.7
  694.6 14.0 %collective-permute-done.52 = f32[85,2048]{1,0:T(8,128)} collective-permute-done((f32[85,2048]{1,0:T(8,128)S(1)}, f32[85,2048]{1,0:T(8,128)}, u32[]{:S(2)}, u32[]{:S(2)}) %collective-permute-start.52) | collective-permute-done | bytes 696352 | tf_op jit(solution)/shard_map/ppermute | solution.py:382
  711.8 13.7 %collective-permute-done.68 = bf16[256,1536]{1,0:T(8,128)(2,1)} collective-permute-done((bf16[256,1536]{1,0:T(8,128)(2,1)}, bf16[256,1536]{1,0:T(8,128)(2,1)}, u32[]{:S(2)}, u32[]{:S(2)}) %collective-permute-start.68) | collective-permute-done | bytes 786464 | tf_op jit(solution)/shard_map/ppermute | solution.py:342
  726.9 3.5 convert_add_fusion.1
  732.7 8.8 %collective-permute-done.53 = f32[85,2048]{1,0:T(8,128)S(1)} collective-permute-done((f32[85,2048]{1,0:T(8,128)S(1)}, f32[85,2048]{1,0:T(8,128)S(1)}, u32[]{:S(2)}, u32[]{:S(2)}) %collective-permute-start.53) | collective-permute-done | bytes 696352 | tf_op jit(solution)/shard_map/ppermute | solution.py:382
  743.6 6.7 collective-permute-done.65
  (477 shorter events, 219.0 us)
Async XLA Ops:
  5.7 53.3 %collective-permute-start.1 = (bf16[256,1536]{1,0:T(8,128)(2,1)}, bf16[256,1536]{1,0:T(8,128)(2,1)}, u32[]{:S(2)}, u32[]{:S(2)}) collective-permute-start(bf16[256,1536]{1,0:T(8,128)(2,1)} %constant_dynamic-update-slice_fusion.23), channel_id=1, source_target_pairs={{8,0},{16,8},{24,16},{28,24},{20,28},{12,20},{4,12},{0,4},{9,1},{1... | collective-permute-start | bytes 2359304 | tf_op jit(solution)/shard_map/ppermute | solution.py:342
  8.6 46.9 %collective-permute-start = (bf16[256,1536]{1,0:T(8,128)(2,1)}, bf16[256,1536]{1,0:T(8,128)(2,1)}, u32[]{:S(2)}, u32[]{:S(2)}) collective-permute-start(bf16[256,1536]{1,0:T(8,128)(2,1)} %constant_dynamic-update-slice_fusion.23), channel_id=1, source_target_pairs={{0,8},{8,16},{16,24},{24,28},{28,20},{20,12},{12,4},{4,0},{1,9},{9... | collective-permute-start | bytes 2359304 | tf_op jit(solution)/shard_map/ppermute | solution.py:339
  8.7 52.7 %collective-permute-start.9 = (bf16[256,2048]{1,0:T(8,128)(2,1)}, bf16[256,2048]{1,0:T(8,128)(2,1)}, u32[]{:S(2)}, u32[]{:S(2)}) collective-permute-start(bf16[256,2048]{1,0:T(8,128)(2,1)} %param.22), channel_id=1, source_target_pairs={{8,0},{16,8},{24,16},{28,24},{20,28},{12,20},{4,12},{0,4},{9,1},{1... | collective-permute-start | bytes 3145736 | tf_op jit(solution)/shard_map/ppermute | solution.py:342
  10.7 52.7 %collective-permute-start.8 = (bf16[256,2048]{1,0:T(8,128)(2,1)}, bf16[256,2048]{1,0:T(8,128)(2,1)}, u32[]{:S(2)}, u32[]{:S(2)}) collective-permute-start(bf16[256,2048]{1,0:T(8,128)(2,1)} %param.22), channel_id=1, source_target_pairs={{0,8},{8,16},{16,24},{24,28},{28,20},{20,12},{12,4},{4,0},{1,9},{9... | collective-permute-start | bytes 3145736 | tf_op jit(solution)/shard_map/ppermute | solution.py:339
  57.0 20.9 %collective-permute-start.2 = (bf16[256,1536]{1,0:T(8,128)(2,1)}, bf16[256,1536]{1,0:T(8,128)(2,1)}, u32[]{:S(2)}, u32[]{:S(2)}) collective-permute-start(bf16[256,1536]{1,0:T(8,128)(2,1)} %collective-permute-done), channel_id=1, source_target_pairs={{0,8},{8,16},{16,24},{24,28},{28,20},{20,12},{12,4},{4,0},{1,9},{9... | collective-permute-start | bytes 2359304 | tf_op jit(solution)/shard_map/ppermute | solution.py:339
  59.0 22.3 %collective-permute-start.3 = (bf16[256,1536]{1,0:T(8,128)(2,1)}, bf16[256,1536]{1,0:T(8,128)(2,1)}, u32[]{:S(2)}, u32[]{:S(2)}) collective-permute-start(bf16[256,1536]{1,0:T(8,128)(2,1)} %collective-permute-done.1), channel_id=1, source_target_pairs={{8,0},{16,8},{24,16},{28,24},{20,28},{12,20},{4,12},{0,4},{9,1},{1... | collective-permute-start | bytes 2359304 | tf_op jit(solution)/shard_map/ppermute | solution.py:342
  61.4 40.9 %collective-permute-start.11 = (bf16[256,2048]{1,0:T(8,128)(2,1)}, bf16[256,2048]{1,0:T(8,128)(2,1)}, u32[]{:S(2)}, u32[]{:S(2)}) collective-permute-start(bf16[256,2048]{1,0:T(8,128)(2,1)} %collective-permute-done.9), channel_id=1, source_target_pairs={{8,0},{16,8},{24,16},{28,24},{20,28},{12,20},{4,12},{0,4},{9,1},{1... | collective-permute-start | bytes 3145736 | tf_op jit(solution)/shard_map/ppermute | solution.py:342
  63.4 39.0 %collective-permute-start.10 = (bf16[256,2048]{1,0:T(8,128)(2,1)}, bf16[256,2048]{1,0:T(8,128)(2,1)}, u32[]{:S(2)}, u32[]{:S(2)}) collective-permute-start(bf16[256,2048]{1,0:T(8,128)(2,1)} %collective-permute-done.8), channel_id=1, source_target_pairs={{0,8},{8,16},{16,24},{24,28},{28,20},{20,12},{12,4},{4,0},{1,9},{9... | collective-permute-start | bytes 3145736 | tf_op jit(solution)/shard_map/ppermute | solution.py:339
  79.2 41.7 %collective-permute-start.4 = (bf16[256,1536]{1,0:T(8,128)(2,1)}, bf16[256,1536]{1,0:T(8,128)(2,1)}, u32[]{:S(2)}, u32[]{:S(2)}) collective-permute-start(bf16[256,1536]{1,0:T(8,128)(2,1)} %collective-permute-done.2), channel_id=1, source_target_pairs={{0,8},{8,16},{16,24},{24,28},{28,20},{20,12},{12,4},{4,0},{1,9},{9... | collective-permute-start | bytes 2359304 | tf_op jit(solution)/shard_map/ppermute | solution.py:339
  81.3 37.9 %collective-permute-start.5 = (bf16[256,1536]{1,0:T(8,128)(2,1)}, bf16[256,1536]{1,0:T(8,128)(2,1)}, u32[]{:S(2)}, u32[]{:S(2)}) collective-permute-start(bf16[256,1536]{1,0:T(8,128)(2,1)} %collective-permute-done.3), channel_id=1, source_target_pairs={{8,0},{16,8},{24,16},{28,24},{20,28},{12,20},{4,12},{0,4},{9,1},{1... | collective-permute-start | bytes 2359304 | tf_op jit(solution)/shard_map/ppermute | solution.py:342
  102.3 74.4 %collective-permute-start.13 = (bf16[256,2048]{1,0:T(8,128)(2,1)}, bf16[256,2048]{1,0:T(8,128)(2,1)}, u32[]{:S(2)}, u32[]{:S(2)}) collective-permute-start(bf16[256,2048]{1,0:T(8,128)(2,1)} %collective-permute-done.11), channel_id=1, source_target_pairs={{8,0},{16,8},{24,16},{28,24},{20,28},{12,20},{4,12},{0,4},{9,1},{1... | collective-permute-start | bytes 3145736 | tf_op jit(solution)/shard_map/ppermute | solution.py:342
  102.3 77.0 %collective-permute-start.12 = (bf16[256,2048]{1,0:T(8,128)(2,1)}, bf16[256,2048]{1,0:T(8,128)(2,1)}, u32[]{:S(2)}, u32[]{:S(2)}) collective-permute-start(bf16[256,2048]{1,0:T(8,128)(2,1)} %collective-permute-done.10), channel_id=1, source_target_pairs={{0,8},{8,16},{16,24},{24,28},{28,20},{20,12},{12,4},{4,0},{1,9},{9... | collective-permute-start | bytes 3145736 | tf_op jit(solution)/shard_map/ppermute | solution.py:339
  120.9 29.1 %collective-permute-start.7 = (bf16[128,1536]{1,0:T(8,128)(2,1)}, bf16[128,1536]{1,0:T(8,128)(2,1)}, u32[]{:S(2)}, u32[]{:S(2)}) collective-permute-start(bf16[128,1536]{1,0:T(8,128)(2,1)} %slice.278), channel_id=1, source_target_pairs={{8,0},{16,8},{24,16},{28,24},{20,28},{12,20},{4,12},{0,4},{9,1},{1... | collective-permute-start | bytes 1179656 | tf_op jit(solution)/shard_map/ppermute | solution.py:342
  122.7 29.1 %collective-permute-start.6 = (bf16[128,1536]{1,0:T(8,128)(2,1)}, bf16[128,1536]{1,0:T(8,128)(2,1)}, u32[]{:S(2)}, u32[]{:S(2)}) collective-permute-start(bf16[128,1536]{1,0:T(8,128)(2,1)} %slice.277), channel_id=1, source_target_pairs={{0,8},{8,16},{16,24},{24,28},{28,20},{20,12},{12,4},{4,0},{1,9},{9... | collective-permute-start | bytes 1179656 | tf_op jit(solution)/shard_map/ppermute | solution.py:339
  124.7 89.6 %collective-permute-start.20 = (bf16[2560,256]{1,0:T(8,128)(2,1)S(1)}, bf16[2560,256]{1,0:T(8,128)(2,1)}, u32[]{:S(2)}, u32[]{:S(2)}) collective-permute-start(bf16[2560,256]{1,0:T(8,128)(2,1)S(1)} %pad_maximum_fusion.4), channel_id=1, source_target_pairs={{8,0},{16,8},{24,16},{28,24},{20,28},{12,20},{4,12},{0,4},{9,1},{1... | collective-permute-start | bytes 3932168 | tf_op jit(solution)/shard_map/ppermute | solution.py:342
  150.0 62.1 %collective-permute-start.19 = (bf16[2560,256]{1,0:T(8,128)(2,1)S(1)}, bf16[2560,256]{1,0:T(8,128)(2,1)}, u32[]{:S(2)}, u32[]{:S(2)}) collective-permute-start(bf16[2560,256]{1,0:T(8,128)(2,1)S(1)} %pad_maximum_fusion.4), channel_id=1, source_target_pairs={{0,8},{8,16},{16,24},{24,28},{28,20},{20,12},{12,4},{4,0},{1,9},{9... | collective-permute-start | bytes 3932168 | tf_op jit(solution)/shard_map/ppermute | solution.py:339
  178.8 12.3 %collective-permute-start.15 = (bf16[128,2048]{1,0:T(8,128)(2,1)}, bf16[128,2048]{1,0:T(8,128)(2,1)S(1)}, u32[]{:S(2)}, u32[]{:S(2)}) collective-permute-start(bf16[128,2048]{1,0:T(8,128)(2,1)} %slice.289), channel_id=1, source_target_pairs={{8,0},{16,8},{24,16},{28,24},{20,28},{12,20},{4,12},{0,4},{9,1},{1... | collective-permute-start | bytes 1572872 | tf_op jit(solution)/shard_map/ppermute | solution.py:342
  181.2 9.9 %collective-permute-start.14 = (bf16[128,2048]{1,0:T(8,128)(2,1)}, bf16[128,2048]{1,0:T(8,128)(2,1)}, u32[]{:S(2)}, u32[]{:S(2)}) collective-permute-start(bf16[128,2048]{1,0:T(8,128)(2,1)} %slice.288), channel_id=1, source_target_pairs={{0,8},{8,16},{16,24},{24,28},{28,20},{20,12},{12,4},{4,0},{1,9},{9... | collective-permute-start | bytes 1572872 | tf_op jit(solution)/shard_map/ppermute | solution.py:339
  212.0 9.5 %collective-permute-start.16 = (bf16[256,256]{1,0:T(8,128)(2,1)S(1)}, bf16[256,256]{1,0:T(8,128)(2,1)S(1)}, u32[]{:S(2)}, u32[]{:S(2)}) collective-permute-start(bf16[256,256]{1,0:T(8,128)(2,1)S(1)} %constant_dynamic-slice_fusion.5), channel_id=1, source_target_pairs={{0,1},{1,0},{2,3},{3,2},{4,5},{5,4},{6,7},{7,6},{8,9},{9,8},{10,11... | collective-permute-start | bytes 393224 | tf_op jit(solution)/shard_map/ppermute | solution.py:395
  216.5 10.3 %collective-permute-start.21 = (bf16[256,512]{1,0:T(8,128)(2,1)S(1)}, bf16[256,512]{1,0:T(8,128)(2,1)S(1)}, u32[]{:S(2)}, u32[]{:S(2)}) collective-permute-start(bf16[256,512]{1,0:T(8,128)(2,1)S(1)} %fusion.49), channel_id=1, source_target_pairs={{0,1},{1,0},{2,3},{3,2},{4,5},{5,4},{6,7},{7,6},{8,9},{9,8},{10,11... | collective-permute-start | bytes 786440 | tf_op jit(solution)/shard_map/ppermute | solution.py:395
  217.1 32.0 %collective-permute-start.25 = (bf16[2560,256]{1,0:T(8,128)(2,1)}, bf16[2560,256]{1,0:T(8,128)(2,1)S(1)}, u32[]{:S(2)}, u32[]{:S(2)}) collective-permute-start(bf16[2560,256]{1,0:T(8,128)(2,1)} %collective-permute-done.20), channel_id=1, source_target_pairs={{8,0},{16,8},{24,16},{28,24},{20,28},{12,20},{4,12},{0,4},{9,1},{1... | collective-permute-start | bytes 3932168 | tf_op jit(solution)/shard_map/ppermute | solution.py:342
  217.5 30.7 %collective-permute-start.24 = (bf16[2560,256]{1,0:T(8,128)(2,1)}, bf16[2560,256]{1,0:T(8,128)(2,1)S(1)}, u32[]{:S(2)}, u32[]{:S(2)}) collective-permute-start(bf16[2560,256]{1,0:T(8,128)(2,1)} %collective-permute-done.19), channel_id=1, source_target_pairs={{0,8},{8,16},{16,24},{24,28},{28,20},{20,12},{12,4},{4,0},{1,9},{9... | collective-permute-start | bytes 3932168 | tf_op jit(solution)/shard_map/ppermute | solution.py:339
  235.7 14.4 %collective-permute-start.23 = (bf16[256,512]{1,0:T(8,128)(2,1)S(1)}, bf16[256,512]{1,0:T(8,128)(2,1)S(1)}, u32[]{:S(2)}, u32[]{:S(2)}) collective-permute-start(bf16[256,512]{1,0:T(8,128)(2,1)S(1)} %add_convert_fusion.21), channel_id=1, source_target_pairs={{0,1},{1,0},{2,3},{3,2},{4,5},{5,4},{6,7},{7,6},{8,9},{9,8},{10,11... | collective-permute-start | bytes 786440 | tf_op jit(solution)/shard_map/ppermute | solution.py:401
  250.0 13.1 %collective-permute-start.26 = (bf16[256,512]{1,0:T(8,128)(2,1)S(1)}, bf16[256,512]{1,0:T(8,128)(2,1)S(1)}, u32[]{:S(2)}, u32[]{:S(2)}) collective-permute-start(bf16[256,512]{1,0:T(8,128)(2,1)S(1)} %fusion.47), channel_id=1, source_target_pairs={{0,1},{1,0},{2,3},{3,2},{4,5},{5,4},{6,7},{7,6},{8,9},{9,8},{10,11... | collective-permute-start | bytes 786440 | tf_op jit(solution)/shard_map/ppermute | solution.py:395
  250.2 31.2 %collective-permute-start.30 = (bf16[2560,256]{1,0:T(8,128)(2,1)S(1)}, bf16[2560,256]{1,0:T(8,128)(2,1)S(1)}, u32[]{:S(2)}, u32[]{:S(2)}) collective-permute-start(bf16[2560,256]{1,0:T(8,128)(2,1)S(1)} %collective-permute-done.25), channel_id=1, source_target_pairs={{8,0},{16,8},{24,16},{28,24},{20,28},{12,20},{4,12},{0,4},{9,1},{1... | collective-permute-start | bytes 3932168 | tf_op jit(solution)/shard_map/ppermute | solution.py:342
  251.6 41.7 %collective-permute-start.29 = (bf16[2560,256]{1,0:T(8,128)(2,1)S(1)}, bf16[2560,256]{1,0:T(8,128)(2,1)S(1)}, u32[]{:S(2)}, u32[]{:S(2)}) collective-permute-start(bf16[2560,256]{1,0:T(8,128)(2,1)S(1)} %collective-permute-done.24), channel_id=1, source_target_pairs={{0,8},{8,16},{16,24},{24,28},{28,20},{20,12},{12,4},{4,0},{1,9},{9... | collective-permute-start | bytes 3932168 | tf_op jit(solution)/shard_map/ppermute | solution.py:339
  281.4 28.0 %collective-permute-start.35 = (bf16[1280,256]{1,0:T(8,128)(2,1)S(1)}, bf16[1280,256]{1,0:T(8,128)(2,1)S(1)}, u32[]{:S(2)}, u32[]{:S(2)}) collective-permute-start(bf16[1280,256]{1,0:T(8,128)(2,1)S(1)} %slice.297), channel_id=1, source_target_pairs={{8,0},{16,8},{24,16},{28,24},{20,28},{12,20},{4,12},{0,4},{9,1},{1... | collective-permute-start | bytes 1966088 | tf_op jit(solution)/shard_map/ppermute | solution.py:342
  293.3 16.1 %collective-permute-start.34 = (bf16[1280,256]{1,0:T(8,128)(2,1)S(1)}, bf16[1280,256]{1,0:T(8,128)(2,1)S(1)}, u32[]{:S(2)}, u32[]{:S(2)}) collective-permute-start(bf16[1280,256]{1,0:T(8,128)(2,1)S(1)} %slice.296), channel_id=1, source_target_pairs={{0,8},{8,16},{16,24},{24,28},{28,20},{20,12},{12,4},{4,0},{1,9},{9... | collective-permute-start | bytes 1966088 | tf_op jit(solution)/shard_map/ppermute | solution.py:339
  402.4 19.7 %collective-permute-start.70 = (bf16[128,2048]{1,0:T(8,128)(2,1)}, bf16[128,2048]{1,0:T(8,128)(2,1)}, u32[]{:S(2)}, u32[]{:S(2)}) collective-permute-start(bf16[128,2048]{1,0:T(8,128)(2,1)} %get-tuple-element.86), channel_id=1, source_target_pairs={{0,8},{8,16},{16,24},{24,28},{28,20},{20,12},{12,4},{4,0},{1,9},{9... | collective-permute-start | bytes 1572872 | tf_op jit(solution)/shard_map/ppermute | solution.py:339
  403.4 17.4 %collective-permute-start.74 = (bf16[128,2048]{1,0:T(8,128)(2,1)S(1)}, bf16[128,2048]{1,0:T(8,128)(2,1)}, u32[]{:S(2)}, u32[]{:S(2)}) collective-permute-start(bf16[128,2048]{1,0:T(8,128)(2,1)S(1)} %get-tuple-element.87), channel_id=1, source_target_pairs={{8,0},{16,8},{24,16},{28,24},{20,28},{12,20},{4,12},{0,4},{9,1},{1... | collective-permute-start | bytes 1572872 | tf_op jit(solution)/shard_map/ppermute | solution.py:342
  404.4 29.5 %collective-permute-start.48 = (bf16[256,2048]{1,0:T(8,128)(2,1)S(1)}, bf16[256,2048]{1,0:T(8,128)(2,1)}, u32[]{:S(2)}, u32[]{:S(2)}) collective-permute-start(bf16[256,2048]{1,0:T(8,128)(2,1)S(1)} %constant_dynamic-slice_fusion), channel_id=1, source_target_pairs={{0,1},{1,0},{2,3},{3,2},{4,5},{5,4},{6,7},{7,6},{8,9},{9,8},{10,11... | collective-permute-start | bytes 3145736 | tf_op jit(solution)/shard_map/ppermute | solution.py:395
  405.6 25.6 %collective-permute-start.58 = (bf16[1280,256]{1,0:T(8,128)(2,1)}, bf16[1280,256]{1,0:T(8,128)(2,1)S(1)}, u32[]{:S(2)}, u32[]{:S(2)}) collective-permute-start(bf16[1280,256]{1,0:T(8,128)(2,1)} %get-tuple-element.77), channel_id=1, source_target_pairs={{8,0},{16,8},{24,16},{28,24},{20,28},{12,20},{4,12},{0,4},{9,1},{1... | collective-permute-start | bytes 1966088 | tf_op jit(solution)/shard_map/ppermute | solution.py:342
  413.9 17.5 %collective-permute-start.54 = (bf16[1280,256]{1,0:T(8,128)(2,1)S(1)}, bf16[1280,256]{1,0:T(8,128)(2,1)}, u32[]{:S(2)}, u32[]{:S(2)}) collective-permute-start(bf16[1280,256]{1,0:T(8,128)(2,1)S(1)} %copy-done.47), channel_id=1, source_target_pairs={{0,8},{8,16},{16,24},{24,28},{28,20},{20,12},{12,4},{4,0},{1,9},{9... | collective-permute-start | bytes 1966088 | tf_op jit(solution)/shard_map/ppermute | solution.py:339
  420.8 15.8 %collective-permute-start.45 = (bf16[256,2048]{1,0:T(8,128)(2,1)S(1)}, bf16[256,2048]{1,0:T(8,128)(2,1)S(1)}, u32[]{:S(2)}, u32[]{:S(2)}) collective-permute-start(bf16[256,2048]{1,0:T(8,128)(2,1)S(1)} %constant_dynamic-slice_fusion.1), channel_id=1, source_target_pairs={{0,1},{1,0},{2,3},{3,2},{4,5},{5,4},{6,7},{7,6},{8,9},{9,8},{10,11... | collective-permute-start | bytes 3145736 | tf_op jit(solution)/shard_map/ppermute | solution.py:395
  422.1 16.0 %collective-permute-start.39 = (bf16[256,2048]{1,0:T(8,128)(2,1)S(1)}, bf16[256,2048]{1,0:T(8,128)(2,1)S(1)}, u32[]{:S(2)}, u32[]{:S(2)}) collective-permute-start(bf16[256,2048]{1,0:T(8,128)(2,1)S(1)} %constant_dynamic-slice_fusion.3), channel_id=1, source_target_pairs={{0,1},{1,0},{2,3},{3,2},{4,5},{5,4},{6,7},{7,6},{8,9},{9,8},{10,11... | collective-permute-start | bytes 3145736 | tf_op jit(solution)/shard_map/ppermute | solution.py:395
  431.4 26.0 %collective-permute-start.75 = (bf16[256,2048]{1,0:T(8,128)(2,1)S(1)}, bf16[256,2048]{1,0:T(8,128)(2,1)S(1)}, u32[]{:S(2)}, u32[]{:S(2)}) collective-permute-start(bf16[256,2048]{1,0:T(8,128)(2,1)S(1)} %pad_maximum_fusion.8), channel_id=1, source_target_pairs={{8,0},{16,8},{24,16},{28,24},{20,28},{12,20},{4,12},{0,4},{9,1},{1... | collective-permute-start | bytes 3145736 | tf_op jit(solution)/shard_map/ppermute | solution.py:342
  434.0 26.1 %collective-permute-start.71 = (bf16[256,2048]{1,0:T(8,128)(2,1)S(1)}, bf16[256,2048]{1,0:T(8,128)(2,1)S(1)}, u32[]{:S(2)}, u32[]{:S(2)}) collective-permute-start(bf16[256,2048]{1,0:T(8,128)(2,1)S(1)} %pad_maximum_fusion.7), channel_id=1, source_target_pairs={{0,8},{8,16},{16,24},{24,28},{28,20},{20,12},{12,4},{4,0},{1,9},{9... | collective-permute-start | bytes 3145736 | tf_op jit(solution)/shard_map/ppermute | solution.py:339
  436.6 48.5 %collective-permute-start.59 = (bf16[2560,256]{1,0:T(8,128)(2,1)S(1)}, bf16[2560,256]{1,0:T(8,128)(2,1)S(1)}, u32[]{:S(2)}, u32[]{:S(2)}) collective-permute-start(bf16[2560,256]{1,0:T(8,128)(2,1)S(1)} %pad_maximum_fusion.6), channel_id=1, source_target_pairs={{8,0},{16,8},{24,16},{28,24},{20,28},{12,20},{4,12},{0,4},{9,1},{1... | collective-permute-start | bytes 3932168 | tf_op jit(solution)/shard_map/ppermute | solution.py:342
  438.1 49.4 %collective-permute-start.55 = (bf16[2560,256]{1,0:T(8,128)(2,1)S(1)}, bf16[2560,256]{1,0:T(8,128)(2,1)S(1)}, u32[]{:S(2)}, u32[]{:S(2)}) collective-permute-start(bf16[2560,256]{1,0:T(8,128)(2,1)S(1)} %pad_maximum_fusion.5), channel_id=1, source_target_pairs={{0,8},{8,16},{16,24},{24,28},{28,20},{20,12},{12,4},{4,0},{1,9},{9... | collective-permute-start | bytes 3932168 | tf_op jit(solution)/shard_map/ppermute | solution.py:339
  439.6 50.2 %collective-permute-start.49 = (bf16[256,2048]{1,0:T(8,128)(2,1)S(1)}, bf16[256,2048]{1,0:T(8,128)(2,1)S(1)}, u32[]{:S(2)}, u32[]{:S(2)}) collective-permute-start(bf16[256,2048]{1,0:T(8,128)(2,1)S(1)} %add_convert_fusion.10), channel_id=1, source_target_pairs={{0,2},{1,3},{2,0},{3,1},{4,6},{5,7},{6,4},{7,5},{8,10},{9,11},{10,... | collective-permute-start | bytes 3145736 | tf_op jit(solution)/shard_map/ppermute | solution.py:398
  457.4 33.6 %collective-permute-start.46 = (bf16[256,2048]{1,0:T(8,128)(2,1)S(1)}, bf16[256,2048]{1,0:T(8,128)(2,1)S(1)}, u32[]{:S(2)}, u32[]{:S(2)}) collective-permute-start(bf16[256,2048]{1,0:T(8,128)(2,1)S(1)} %add_convert_fusion.12), channel_id=1, source_target_pairs={{0,2},{1,3},{2,0},{3,1},{4,6},{5,7},{6,4},{7,5},{8,10},{9,11},{10,... | collective-permute-start | bytes 3145736 | tf_op jit(solution)/shard_map/ppermute | solution.py:398
  460.0 50.7 %collective-permute-start.40 = (bf16[256,2048]{1,0:T(8,128)(2,1)S(1)}, bf16[256,2048]{1,0:T(8,128)(2,1)S(1)}, u32[]{:S(2)}, u32[]{:S(2)}) collective-permute-start(bf16[256,2048]{1,0:T(8,128)(2,1)S(1)} %add_convert_fusion.16), channel_id=1, source_target_pairs={{0,2},{1,3},{2,0},{3,1},{4,6},{5,7},{6,4},{7,5},{8,10},{9,11},{10,... | collective-permute-start | bytes 3145736 | tf_op jit(solution)/shard_map/ppermute | solution.py:398
  485.1 46.4 %collective-permute-start.43 = (bf16[256,2048]{1,0:T(8,128)(2,1)S(1)}, bf16[256,2048]{1,0:T(8,128)(2,1)S(1)}, u32[]{:S(2)}, u32[]{:S(2)}) collective-permute-start(bf16[256,2048]{1,0:T(8,128)(2,1)S(1)} %add_convert_fusion.14), channel_id=1, source_target_pairs={{0,2},{1,3},{2,0},{3,1},{4,6},{5,7},{6,4},{7,5},{8,10},{9,11},{10,... | collective-permute-start | bytes 3145736 | tf_op jit(solution)/shard_map/ppermute | solution.py:398
  487.6 44.4 %collective-permute-start.76 = (bf16[256,2048]{1,0:T(8,128)(2,1)S(1)}, bf16[256,2048]{1,0:T(8,128)(2,1)S(1)}, u32[]{:S(2)}, u32[]{:S(2)}) collective-permute-start(bf16[256,2048]{1,0:T(8,128)(2,1)S(1)} %add_convert_fusion.6), channel_id=1, source_target_pairs={{8,0},{16,8},{24,16},{28,24},{20,28},{12,20},{4,12},{0,4},{9,1},{1... | collective-permute-start | bytes 3145736 | tf_op jit(solution)/shard_map/ppermute | solution.py:342
  489.9 196.6 %collective-permute-start.72 = (bf16[256,2048]{1,0:T(8,128)(2,1)}, bf16[256,2048]{1,0:T(8,128)(2,1)}, u32[]{:S(2)}, u32[]{:S(2)}) collective-permute-start(bf16[256,2048]{1,0:T(8,128)(2,1)} %add_convert_fusion.8), channel_id=1, source_target_pairs={{0,8},{8,16},{16,24},{24,28},{28,20},{20,12},{12,4},{4,0},{1,9},{9... | collective-permute-start | bytes 3145736 | tf_op jit(solution)/shard_map/ppermute | solution.py:339
  491.0 49.2 %collective-permute-start.60 = (bf16[2560,256]{1,0:T(8,128)(2,1)S(1)}, bf16[2560,256]{1,0:T(8,128)(2,1)S(1)}, u32[]{:S(2)}, u32[]{:S(2)}) collective-permute-start(bf16[2560,256]{1,0:T(8,128)(2,1)S(1)} %add_convert_fusion.2), channel_id=1, source_target_pairs={{8,0},{16,8},{24,16},{28,24},{20,28},{12,20},{4,12},{0,4},{9,1},{1... | collective-permute-start | bytes 3932168 | tf_op jit(solution)/shard_map/ppermute | solution.py:342
  510.7 31.7 %collective-permute-start.56 = (bf16[2560,256]{1,0:T(8,128)(2,1)S(1)}, bf16[2560,256]{1,0:T(8,128)(2,1)S(1)}, u32[]{:S(2)}, u32[]{:S(2)}) collective-permute-start(bf16[2560,256]{1,0:T(8,128)(2,1)S(1)} %add_convert_fusion.4), channel_id=1, source_target_pairs={{0,8},{8,16},{16,24},{24,28},{28,20},{20,12},{12,4},{4,0},{1,9},{9... | collective-permute-start | bytes 3932168 | tf_op jit(solution)/shard_map/ppermute | solution.py:339
  534.2 10.8 %collective-permute-start.50 = (bf16[256,2048]{1,0:T(8,128)(2,1)S(1)}, bf16[256,2048]{1,0:T(8,128)(2,1)S(1)}, u32[]{:S(2)}, u32[]{:S(2)}) collective-permute-start(bf16[256,2048]{1,0:T(8,128)(2,1)S(1)} %add_convert_fusion.9), channel_id=1, source_target_pairs={{0,1},{1,0},{2,3},{3,2},{4,5},{5,4},{6,7},{7,6},{8,9},{9,8},{10,11... | collective-permute-start | bytes 3145736 | tf_op jit(solution)/shard_map/ppermute | solution.py:401
  535.7 10.0 %collective-permute-start.47 = (bf16[256,2048]{1,0:T(8,128)(2,1)S(1)}, bf16[256,2048]{1,0:T(8,128)(2,1)S(1)}, u32[]{:S(2)}, u32[]{:S(2)}) collective-permute-start(bf16[256,2048]{1,0:T(8,128)(2,1)S(1)} %add_convert_fusion.11), channel_id=1, source_target_pairs={{0,1},{1,0},{2,3},{3,2},{4,5},{5,4},{6,7},{7,6},{8,9},{9,8},{10,11... | collective-permute-start | bytes 3145736 | tf_op jit(solution)/shard_map/ppermute | solution.py:401
  540.2 186.6 %collective-permute-start.77 = (bf16[256,2048]{1,0:T(8,128)(2,1)}, bf16[256,2048]{1,0:T(8,128)(2,1)}, u32[]{:S(2)}, u32[]{:S(2)}) collective-permute-start(bf16[256,2048]{1,0:T(8,128)(2,1)} %add_convert_fusion.5), channel_id=1, source_target_pairs={{8,0},{16,8},{24,16},{28,24},{20,28},{12,20},{4,12},{0,4},{9,1},{1... | collective-permute-start | bytes 3145736 | tf_op jit(solution)/shard_map/ppermute | solution.py:342
  542.4 49.8 %collective-permute-start.61 = (bf16[2560,256]{1,0:T(8,128)(2,1)S(1)}, bf16[2560,256]{1,0:T(8,128)(2,1)S(1)}, u32[]{:S(2)}, u32[]{:S(2)}) collective-permute-start(bf16[2560,256]{1,0:T(8,128)(2,1)S(1)} %add_convert_fusion.1), channel_id=1, source_target_pairs={{8,0},{16,8},{24,16},{28,24},{20,28},{12,20},{4,12},{0,4},{9,1},{1... | collective-permute-start | bytes 3932168 | tf_op jit(solution)/shard_map/ppermute | solution.py:342
  545.0 47.1 %collective-permute-start.57 = (bf16[2560,256]{1,0:T(8,128)(2,1)S(1)}, bf16[2560,256]{1,0:T(8,128)(2,1)S(1)}, u32[]{:S(2)}, u32[]{:S(2)}) collective-permute-start(bf16[2560,256]{1,0:T(8,128)(2,1)S(1)} %add_convert_fusion.3), channel_id=1, source_target_pairs={{0,8},{8,16},{16,24},{24,28},{28,20},{20,12},{12,4},{4,0},{1,9},{9... | collective-permute-start | bytes 3932168 | tf_op jit(solution)/shard_map/ppermute | solution.py:339
  595.0 49.2 %collective-permute-start.62 = (bf16[128,1536]{1,0:T(8,128)(2,1)}, bf16[128,1536]{1,0:T(8,128)(2,1)}, u32[]{:S(2)}, u32[]{:S(2)}) collective-permute-start(bf16[128,1536]{1,0:T(8,128)(2,1)} %get-tuple-element.88), channel_id=1, source_target_pairs={{0,8},{8,16},{16,24},{24,28},{28,20},{20,12},{12,4},{4,0},{1,9},{9... | collective-permute-start | bytes 1179656 | tf_op jit(solution)/shard_map/ppermute | solution.py:339
  642.1 25.1 %collective-permute-start.51 = (f32[85,2048]{1,0:T(8,128)S(1)}, f32[85,2048]{1,0:T(8,128)S(1)}, u32[]{:S(2)}, u32[]{:S(2)}) collective-permute-start(f32[85,2048]{1,0:T(8,128)S(1)} %select_maximum_fusion), channel_id=1, source_target_pairs={{0,4},{4,0},{8,12},{12,8},{16,20},{20,16},{24,28},{28,24},{1,5},{5... | collective-permute-start | bytes 2088968 | tf_op jit(solution)/shard_map/ppermute | solution.py:382
  642.5 22.1 %collective-permute-start.66 = (bf16[128,1536]{1,0:T(8,128)(2,1)}, bf16[128,1536]{1,0:T(8,128)(2,1)S(1)}, u32[]{:S(2)}, u32[]{:S(2)}) collective-permute-start(bf16[128,1536]{1,0:T(8,128)(2,1)} %get-tuple-element.89), channel_id=1, source_target_pairs={{8,0},{16,8},{24,16},{28,24},{20,28},{12,20},{4,12},{0,4},{9,1},{1... | collective-permute-start | bytes 1179656 | tf_op jit(solution)/shard_map/ppermute | solution.py:342
  645.6 28.8 %collective-permute-start.63 = (bf16[256,1536]{1,0:T(8,128)(2,1)S(1)}, bf16[256,1536]{1,0:T(8,128)(2,1)S(1)}, u32[]{:S(2)}, u32[]{:S(2)}) collective-permute-start(bf16[256,1536]{1,0:T(8,128)(2,1)S(1)} %pad_maximum_fusion.11), channel_id=1, source_target_pairs={{0,8},{8,16},{16,24},{24,28},{28,20},{20,12},{12,4},{4,0},{1,9},{9... | collective-permute-start | bytes 2359304 | tf_op jit(solution)/shard_map/ppermute | solution.py:339
  664.8 20.5 %collective-permute-start.67 = (bf16[256,1536]{1,0:T(8,128)(2,1)S(1)}, bf16[256,1536]{1,0:T(8,128)(2,1)S(1)}, u32[]{:S(2)}, u32[]{:S(2)}) collective-permute-start(bf16[256,1536]{1,0:T(8,128)(2,1)S(1)} %pad_maximum_fusion.12), channel_id=1, source_target_pairs={{8,0},{16,8},{24,16},{28,24},{20,28},{12,20},{4,12},{0,4},{9,1},{1... | collective-permute-start | bytes 2359304 | tf_op jit(solution)/shard_map/ppermute | solution.py:342
  667.3 41.3 %collective-permute-start.52 = (f32[85,2048]{1,0:T(8,128)S(1)}, f32[85,2048]{1,0:T(8,128)}, u32[]{:S(2)}, u32[]{:S(2)}) collective-permute-start(f32[85,2048]{1,0:T(8,128)S(1)} %fusion.212), channel_id=1, source_target_pairs={{0,8},{4,12},{8,0},{12,4},{16,24},{20,28},{24,16},{28,20},{1,9},{5... | collective-permute-start | bytes 2088968 | tf_op jit(solution)/shard_map/ppermute | solution.py:382
  675.6 34.4 %collective-permute-start.64 = (bf16[256,1536]{1,0:T(8,128)(2,1)}, bf16[256,1536]{1,0:T(8,128)(2,1)}, u32[]{:S(2)}, u32[]{:S(2)}) collective-permute-start(bf16[256,1536]{1,0:T(8,128)(2,1)} %fusion.21), channel_id=1, source_target_pairs={{0,8},{8,16},{16,24},{24,28},{28,20},{20,12},{12,4},{4,0},{1,9},{9... | collective-permute-start | bytes 2359304 | tf_op jit(solution)/shard_map/ppermute | solution.py:339
  686.4 39.0 %collective-permute-start.68 = (bf16[256,1536]{1,0:T(8,128)(2,1)}, bf16[256,1536]{1,0:T(8,128)(2,1)}, u32[]{:S(2)}, u32[]{:S(2)}) collective-permute-start(bf16[256,1536]{1,0:T(8,128)(2,1)} %fusion.23), channel_id=1, source_target_pairs={{8,0},{16,8},{24,16},{28,24},{20,28},{12,20},{4,12},{0,4},{9,1},{1... | collective-permute-start | bytes 2359304 | tf_op jit(solution)/shard_map/ppermute | solution.py:342
  688.9 37.9 %collective-permute-start.73 = (bf16[256,2048]{1,0:T(8,128)(2,1)}, bf16[256,2048]{1,0:T(8,128)(2,1)}, u32[]{:S(2)}, u32[]{:S(2)}) collective-permute-start(bf16[256,2048]{1,0:T(8,128)(2,1)} %add_convert_fusion.7), channel_id=1, source_target_pairs={{0,8},{8,16},{16,24},{24,28},{28,20},{20,12},{12,4},{4,0},{1,9},{9... | collective-permute-start | bytes 3145736 | tf_op jit(solution)/shard_map/ppermute | solution.py:339
  709.9 31.7 %collective-permute-start.53 = (f32[85,2048]{1,0:T(8,128)S(1)}, f32[85,2048]{1,0:T(8,128)S(1)}, u32[]{:S(2)}, u32[]{:S(2)}) collective-permute-start(f32[85,2048]{1,0:T(8,128)S(1)} %add.210), channel_id=1, source_target_pairs={{0,16},{4,20},{8,24},{12,28},{16,0},{20,4},{24,8},{28,12},{1,17},{... | collective-permute-start | bytes 2088968 | tf_op jit(solution)/shard_map/ppermute | solution.py:382
  711.7 38.6 %collective-permute-start.65 = (bf16[256,1536]{1,0:T(8,128)(2,1)S(1)}, bf16[256,1536]{1,0:T(8,128)(2,1)S(1)}, u32[]{:S(2)}, u32[]{:S(2)}) collective-permute-start(bf16[256,1536]{1,0:T(8,128)(2,1)S(1)} %fusion.20), channel_id=1, source_target_pairs={{0,8},{8,16},{16,24},{24,28},{28,20},{20,12},{12,4},{4,0},{1,9},{9... | collective-permute-start | bytes 2359304 | tf_op jit(solution)/shard_map/ppermute | solution.py:339
  726.8 23.5 %collective-permute-start.69 = (bf16[256,1536]{1,0:T(8,128)(2,1)S(1)}, bf16[256,1536]{1,0:T(8,128)(2,1)S(1)}, u32[]{:S(2)}, u32[]{:S(2)}) collective-permute-start(bf16[256,1536]{1,0:T(8,128)(2,1)S(1)} %fusion.22), channel_id=1, source_target_pairs={{8,0},{16,8},{24,16},{28,24},{20,28},{12,20},{4,12},{0,4},{9,1},{1... | collective-permute-start | bytes 2359304 | tf_op jit(solution)/shard_map/ppermute | solution.py:342
  (89 other events, 886.0 us)

commit v2 on v0

v2 whole, which is shorter than its diff:
```python
import jax
import jax.numpy as jnp
from jax import lax
from jax.experimental import pallas as pl
from jax.experimental.pallas import tpu as pltpu
from jax.sharding import PartitionSpec as P

HEAD_DIM = 128
ROT = 32


EPSILON = 1e-05
ROPE_BASE = 10000.0

F32 = jnp.float32
BF16 = jnp.bfloat16


def rotary_tables(segments):
    tok_count = segments.shape[0]
    order_idx = jnp.arange(tok_count, dtype=jnp.int32)
    same_doc = segments[:, None] == segments[None, :]
    earlier = order_idx[None, :] < order_idx[:, None]
    places = jnp.sum((same_doc & earlier).astype(jnp.int32), axis=1)
    halves = jnp.arange(ROT // 2, dtype=jnp.float32)
    frequency = ROPE_BASE ** (-2.0 * halves / ROT)
    angles = places.astype(jnp.float32)[:, None] * frequency[None, :]
    return jnp.cos(angles), jnp.sin(angles)


MIB = 1 << 20
GROUP = 16
CHUNK = 512


def gelu(x):
    return 0.5 * x * (1.0 + lax.erf(x * (0.5**0.5)))


def gelu_slope(x):
    return 0.5 * (1.0 + lax.erf(x * (0.5**0.5))) + x * jnp.exp(-0.5 * x * x) * 0.3989422804014327


def dot(a, b, dims):
    return lax.dot_general(a, b, (dims, ((), ())), preferred_element_type=F32)


def gen_kernel(stream, branch, gain, gen_in, gen_out, out_grad, next_grad, layer_out, next_mix, out_total, branch_grad, gain_grad, in_grad, mid_grad):
    first = pl.program_id(0) == 0
    x = stream[0] + jnp.concatenate([branch[owner] for owner in range(branch.shape[0])], axis=1).astype(F32)
    layer_out[...] = x.astype(BF16)
    center = x - jnp.mean(x, axis=1, keepdims=True)
    scale = lax.rsqrt(jnp.mean(center * center, axis=1, keepdims=True) + EPSILON)
    unit = center * scale
    gains = gain[4:5, :]
    low = (unit * gains).astype(BF16)
    hidden = dot(low, gen_in[...], ((1,), (0,)))
    active = gelu(hidden).astype(BF16)
    next_mix[...] = dot(active, gen_out[...], ((1,), (0,)))
    upstream = next_grad[...].astype(BF16)
    active_grad = dot(upstream, gen_out[...], ((1,), (1,)))
    hidden_grad = (active_grad * gelu_slope(hidden)).astype(BF16)
    y = dot(hidden_grad, gen_in[...], ((1,), (1,)))
    e = y * gains
    grad = scale * (
        e - jnp.mean(e, axis=1, keepdims=True) - unit * jnp.mean(e * unit, axis=1, keepdims=True)
    )
    total = out_grad[...].astype(F32) + grad
    out_total[...] = total
    low_total = total.astype(BF16)
    shard = branch_grad.shape[2]
    for owner in range(branch_grad.shape[0]):
        branch_grad[owner] = low_total[:, owner * shard : (owner + 1) * shard]
    gain_part = jnp.sum(y * unit, axis=0, keepdims=True)
    in_part = dot(hidden_grad, low, ((0,), (0,)))
    mid_part = dot(active, upstream, ((0,), (0,)))

    @pl.when(first)
    def _():
        gain_grad[...] = gain_part
        in_grad[...] = in_part
        mid_grad[...] = mid_part

    @pl.when(jnp.logical_not(first))
    def _():
        gain_grad[...] += gain_part
        in_grad[...] += in_part
        mid_grad[...] += mid_part


def gen_stage(size, streams, branch, gains, gen_in, gen_out, out_grad, next_grad, block=128):
    _, tokens, width = streams.shape
    units = gen_in.shape[1]
    nxt = gen_out.shape[1]
    row = lambda i: (i, 0)
    fixed = lambda i: (0, 0)
    return pl.pallas_call(
        gen_kernel,
        grid=(tokens // block,),
        in_specs=[
            pl.BlockSpec((1, block, width), lambda i: (3, i, 0)),
            pl.BlockSpec((size, block, width // size), lambda i: (0, i, 0)),
            pl.BlockSpec(gains.shape, fixed),
            pl.BlockSpec(gen_in.shape, fixed),
            pl.BlockSpec(gen_out.shape, fixed),
            pl.BlockSpec((block, width), row),
            pl.BlockSpec((block, nxt), row),
        ],
        out_specs=[
            pl.BlockSpec((block, width), row),
            pl.BlockSpec((block, nxt), row),
            pl.BlockSpec((block, width), row),
            pl.BlockSpec((size, block, width // size), lambda i: (0, i, 0)),
            pl.BlockSpec((1, width), fixed),
            pl.BlockSpec((units, width), fixed),
            pl.BlockSpec((units, nxt), fixed),
        ],
        out_shape=[
            jax.ShapeDtypeStruct((tokens, width), BF16),
            jax.ShapeDtypeStruct((tokens, nxt), F32),
            jax.ShapeDtypeStruct((tokens, width), F32),
            jax.ShapeDtypeStruct((size, tokens, width // size), BF16),
            jax.ShapeDtypeStruct((1, width), F32),
            jax.ShapeDtypeStruct((units, width), F32),
            jax.ShapeDtypeStruct((units, nxt), F32),
        ],
        cost_estimate=pl.CostEstimate(
            flops=tokens * width * 300, bytes_accessed=tokens * width * 16, transcendentals=0
        ),
        compiler_params=pltpu.CompilerParams(vmem_limit_bytes=48 * MIB),
        name="gen_stage",
    )(streams, branch, gains, gen_in, gen_out, out_grad, next_grad)


MESH = pl.DeviceIdType.MESH


def place_of(me, size):
    odd = lax.rem(me, 2)
    at = lax.div(me, 2)
    return (1 - odd) * at + odd * (size - 1 - at)


def index_at(place, size):
    at = lax.rem(place + 2 * size, size)
    back = lax.div(at, size // 2)
    return (1 - back) * 2 * at + back * (2 * (size - 1 - at) + 1)


UNIT = 32


def back_kernel(
    size,
    normed,
    hidden_grad,
    qkv_low,
    stats,
    mix,
    gains,
    parts_in,
    history,
    streams,
    out_total,
    grad_up,
    grad_query,
    grad_key,
    grad_value,
    history_grad,
    mix_grad,
    gain_sum,
    gain_grad,
    gain_sent,
    gain_got,
    parts,
    from_core,
    from_link,
    far,
    ring,
    state_in,
    stream_in,
    total_in,
    state_out,
    held,
    ring_send,
    ring_recv,
    core_send,
    core_recv,
    link_send,
    link_recv,
    twin_send,
    twin_recv,
    load_sem,
    unit_sem,
    store_sem,
    gain_send,
    gain_recv,
    freed,
):
    half = size // 2
    shard = normed.shape[3]
    cut = shard // 2
    tokens, hidden_cols = hidden_grad.shape
    width = history.shape[2]
    inverse = 1.0 / width
    states = history.shape[0]
    me = lax.axis_index("dp")
    lane = lax.axis_index("tensor")
    place = place_of(me, size)
    right = index_at(place + 1, size)
    left = index_at(place - 1, size)
    core = lax.rem(lane, 2)
    chip = lax.div(lane, 2)
    twin = chip * 2 + 1 - core
    across = (1 - chip) * 2 + core

    barrier = pltpu.get_barrier_semaphore()
    steps = size.bit_length() - 1
    partners = [me + (1 << step) * (1 - 2 * lax.rem(lax.div(me, 1 << step), 2)) for step in range(steps)]
    for there in [(right, lane), (left, lane), (me, twin), (me, across)] + [(it, lane) for it in partners]:
        pl.semaphore_signal(barrier, inc=1, device_id=there, device_id_type=MESH)
    pl.semaphore_wait(barrier, 4 + steps)

    block = 64
    rows_half = tokens // 2
    blocks = rows_half // block
    load = pltpu.make_async_copy(parts_in, parts, load_sem)
    load.start()

    wide = 512 if half <= 4 else hidden_cols
    pieces = [(0, at, wide) for at in range(0, hidden_cols, wide)]
    local = qkv_low.shape[1] // 3
    pieces += [(1 + which, which * local, local) for which in range(3)]
    starts = []
    offset = 0
    for _, _, cols in pieces:
        starts.append(offset)
        offset += cols

    def term(distance, piece):
        owner = index_at(place + distance, size)
        which, at, cols = pieces[piece]
        if which == 0:
            return dot(normed[3, owner], hidden_grad[:, at : at + cols], ((0,), (0,)))
        return dot(normed[which - 1, owner], qkv_low[:, at : at + cols], ((0,), (0,)))

    def send(hop, way, piece):
        cols = pl.ds(starts[piece], pieces[piece][2])
        if hop == 0:
            rows = pl.ds(way * cut, cut)
            source = far.at[rows, cols]
            target = ring.at[0, way, rows, cols]
        else:
            source = ring.at[hop - 1, way, :, cols]
            target = ring.at[hop, way, :, cols]
        return pltpu.make_async_remote_copy(
            src_ref=source,
            dst_ref=target,
            send_sem=ring_send.at[hop, way, piece],
            recv_sem=ring_recv.at[hop, way, piece],
            device_id=((right, left)[way], lane),
            device_id_type=MESH,
        )

    for piece in range(len(pieces)):
        cols = pl.ds(starts[piece], pieces[piece][2])
        far[:, cols] = term(half, piece).astype(BF16)
        for way in range(2):
            send(0, way, piece).start()
        if piece == 0:
            load.wait()
            for at in range(blocks):
                rows = pl.ds(pl.multiple_of((1 - core) * rows_half + at * block, block), block)
                pltpu.make_async_remote_copy(
                    src_ref=parts.at[:, rows, :],
                    dst_ref=from_core.at[at],
                    send_sem=core_send.at[at],
                    recv_sem=core_recv.at[at],
                    device_id=(me, twin),
                    device_id_type=MESH,
                ).start()

    def mine(at):
        return pl.ds(pl.multiple_of(core * rows_half + at * block, block), block)

    def core_copy(at):
        rows = pl.ds(pl.multiple_of((1 - core) * rows_half + at * block, block), block)
        return pltpu.make_async_remote_copy(
            src_ref=parts.at[:, rows, :],
            dst_ref=from_core.at[at],
            send_sem=core_send.at[at],
            recv_sem=core_recv.at[at],
            device_id=(me, twin),
            device_id_type=MESH,
        )

    def link_copy(at):
        return pltpu.make_async_remote_copy(
            src_ref=parts.at[:, mine(at), :],
            dst_ref=from_link.at[at],
            send_sem=link_send.at[at],
            recv_sem=link_recv.at[at],
            device_id=(me, across),
            device_id_type=MESH,
        )

    def twin_copy(at):
        return pltpu.make_async_remote_copy(
            src_ref=parts.at[:, mine(at), :],
            dst_ref=parts.at[:, mine(at), :],
            send_sem=twin_send.at[at],
            recv_sem=twin_recv.at[at],
            device_id=(me, twin),
            device_id_type=MESH,
        )

    def add_into(at, other):
        base = core * rows_half + at * block

        @pl.loop(0, block // 16)
        def _(step):
            rows = pl.ds(pl.multiple_of(base + step * 16, 16), 16)
            theirs = pl.ds(pl.multiple_of(step * 16, 16), 16)
            for stream in range(4):
                total = parts[stream, rows, :].astype(F32) + other[at, stream, theirs, :].astype(F32)
                parts[stream, rows, :] = total.astype(BF16)

    def to_link(at):
        copy = core_copy(at)
        copy.wait_send()
        pl.semaphore_signal(freed.at[at], inc=1, device_id=(me, twin), device_id_type=MESH)
        copy.wait_recv()
        add_into(at, from_core)
        link_copy(at).start()

    def to_twin(at):
        copy = link_copy(at)
        copy.wait_send()
        copy.wait_recv()
        add_into(at, from_link)
        pl.semaphore_wait(freed.at[at], 1)
        twin_copy(at).start()

    def ready(at):
        copy = twin_copy(at)
        copy.wait_send()
        copy.wait_recv()

    per_block = 2 * block // UNIT
    units = tokens // UNIT

    def unit_base(unit):
        at, inner = divmod(unit, per_block)
        side, part = divmod(inner, per_block // 2)
        return side * rows_half + at * block + part * UNIT

    def unit_loads(unit):
        rows = pl.ds(unit_base(unit), UNIT)
        slot = unit % 2
        return (
            pltpu.make_async_copy(history.at[:, rows, :], state_in.at[slot], unit_sem.at[slot, 0]),
            pltpu.make_async_copy(streams.at[:, rows, :], stream_in.at[slot], unit_sem.at[slot, 1]),
            pltpu.make_async_copy(out_total.at[rows, :], total_in.at[slot], unit_sem.at[slot, 2]),
        )

    def unit_store(unit):
        rows = pl.ds(unit_base(unit), UNIT)
        slot = unit % 2
        return pltpu.make_async_copy(state_out.at[slot], history_grad.at[:, rows, :], store_sem.at[slot])

    gain_grad[...] = jnp.zeros_like(gain_grad)
    for copy in unit_loads(0):
        copy.start()

    def run_unit(unit):
        slot = unit % 2
        base = unit_base(unit)
        if unit + 1 < units:
            for copy in unit_loads(unit + 1):
                copy.start()
        for copy in unit_loads(unit):
            copy.wait()
        if unit >= 2:
            unit_store(unit - 2).wait()

        @pl.loop(0, UNIT // GROUP)
        def _(step):
            rows = pl.ds(pl.multiple_of(base + step * GROUP, GROUP), GROUP)
            inner = pl.ds(pl.multiple_of(step * GROUP, GROUP), GROUP)
            weights = mix[rows, :]
            for stream in range(4):
                mean = stats[rows, stream : stream + 1]
                scale = stats[rows, 4 + stream : 5 + stream]
                sum_e = jnp.zeros((GROUP, 128), F32)
                sum_ex = jnp.zeros((GROUP, 128), F32)
                for at in range(0, width, CHUNK):
                    cols = pl.ds(at, CHUNK)
                    unit_x = (stream_in[slot, stream, inner, cols] - mean) * scale
                    upstream = parts[stream, rows, cols].astype(F32)
                    e = upstream * gains[stream : stream + 1, cols]
                    gain = upstream * unit_x
                    gain_grad[stream, :, cols] += gain[:8] + gain[8:]
                    ex = e * unit_x
                    for lane_at in range(0, CHUNK, 128):
                        sum_e = sum_e + e[:, lane_at : lane_at + 128]
                        sum_ex = sum_ex + ex[:, lane_at : lane_at + 128]
                mean_e = jnp.sum(sum_e, axis=1, keepdims=True) * inverse
                mean_ex = jnp.sum(sum_ex, axis=1, keepdims=True) * inverse
                for at in range(0, width, CHUNK):
                    cols = pl.ds(at, CHUNK)
                    unit_x = (stream_in[slot, stream, inner, cols] - mean) * scale
                    e = parts[stream, rows, cols].astype(F32) * gains[stream : stream + 1, cols]
                    grad = scale * (e - mean_e - unit_x * mean_ex)
                    if stream == 3:
                        grad = grad + total_in[slot, inner, cols]
                    held[stream, :, cols] = grad
            for source in range(states):
                sums = [jnp.zeros((GROUP, 128), F32) for _ in range(4)]
                for at in range(0, width, CHUNK):
                    cols = pl.ds(at, CHUNK)
                    state = state_in[slot, source, inner, cols].astype(F32)
                    total = None
                    for stream in range(4):
                        k = stream * states + source
                        grad = held[stream, :, cols]
                        piece = weights[:, k : k + 1] * grad
                        total = piece if total is None else total + piece
                        product = state * grad
                        for lane_at in range(0, CHUNK, 128):
                            sums[stream] = sums[stream] + product[:, lane_at : lane_at + 128]
                    state_out[slot, source, inner, cols] = total.astype(BF16)
                for stream in range(4):
                    k = stream * states + source
                    mix_grad[rows, k : k + 1] = jnp.sum(sums[stream], axis=1, keepdims=True)

        unit_store(unit).start()

    def gain_copy(step):
        return pltpu.make_async_remote_copy(
            src_ref=gain_sent.at[step],
            dst_ref=gain_got.at[step],
            send_sem=gain_send.at[step],
            recv_sem=gain_recv.at[step],
            device_id=(partners[step], lane),
            device_id_type=MESH,
        )

    def gain_step(step):
        if step == 0:
            for stream in range(4):
                gain_sent[0, stream : stream + 1, :] = jnp.sum(
                    gain_grad[stream], axis=0, keepdims=True
                )
        else:
            gain_copy(step - 1).wait_recv()
            total = gain_sent[step - 1] + gain_got[step - 1]
            if step == steps:
                gain_sum[...] = total
            else:
                gain_sent[step] = total
        if step < steps:
            gain_copy(step).start()

    tasks = []
    for at in range(blocks):
        tasks.append((0.02 + 0.03 * at, to_link, at))
        tasks.append((0.19 + 0.16 * at, to_twin, at))
        tasks.append((0.23 + 0.16 * at, ready, at))
        for inner in range(per_block):
            tasks.append((0.24 + 0.16 * at + 0.035 * inner, run_unit, at * per_block + inner))
    for step in range(steps + 1):
        tasks.append((0.87 + 0.12 * step / steps, gain_step, step))
    tasks.sort(key=lambda item: item[0])
    first_part = 0.5 / (half - 0.5)
    for hop in range(1, half + 1):
        for piece in range(len(pieces)):
            passed = ((hop - 1.5 if hop > 1 else 0.0) + (piece + 1) / len(pieces) * (1 if hop > 1 else 0.5)) / (half - 0.5)
            cols = pl.ds(starts[piece], pieces[piece][2])
            for way in range(2):
                send(hop - 1, way, piece).wait_recv()
                if hop == half:
                    continue
                distance = (half - hop) * (1 - 2 * way)
                if hop == 1:
                    with_rows = pl.ds(way * cut, cut)
                    only_rows = pl.ds((1 - way) * cut, cut)
                    full = term(distance, piece)
                    got = ring[0, way, with_rows, cols].astype(F32)
                    ring[0, way, with_rows, cols] = (full[way * cut : way * cut + cut] + got).astype(BF16)
                    ring[0, way, only_rows, cols] = full[
                        (1 - way) * cut : (1 - way) * cut + cut
                    ].astype(BF16)
                else:
                    got = ring[hop - 1, way, :, cols].astype(F32)
                    ring[hop - 1, way, :, cols] = (term(distance, piece) + got).astype(BF16)
                send(hop, way, piece).start()
            if hop == half:
                total = (
                    term(0, piece)
                    + ring[hop - 1, 0, :, cols].astype(F32)
                    + ring[hop - 1, 1, :, cols].astype(F32)
                )
                which, at, count = pieces[piece]
                if which == 0:
                    grad_up[:, at : at + count] = total
                else:
                    (grad_query, grad_key, grad_value)[which - 1][...] = total
            while tasks and tasks[0][0] <= passed:
                _, run, value = tasks.pop(0)
                run(value)
    for _, run, value in tasks:
        run(value)
    for unit in range(max(units - 2, 0), units):
        unit_store(unit).wait()
    for step in range(steps):
        gain_copy(step).wait_send()
    for hop in range(half):
        for piece in range(len(pieces)):
            for way in range(2):
                send(hop, way, piece).wait_send()


def back_stage(size, normed, hidden_grad, qkv_low, stats, mix, gains, parts, history, streams, out_total):
    half = size // 2
    tokens, hidden = hidden_grad.shape
    states, _, width = history.shape
    shard = normed.shape[3]
    local = qkv_low.shape[1] // 3
    cols = hidden + 3 * local
    count = (hidden // 512 if half <= 4 else 1) + 3
    blocks = tokens // 128
    steps = size.bit_length() - 1
    vmem = pl.BlockSpec(memory_space=pltpu.VMEM)
    hbm = pl.BlockSpec(memory_space=pl.ANY)
    dma = pltpu.SemaphoreType.DMA
    small = jax.ShapeDtypeStruct((shard, local), F32)
    return pl.pallas_call(
        lambda *refs: back_kernel(size, *refs),
        in_specs=[vmem] * 6 + [hbm] * 4,
        out_specs=[vmem] * 4 + [hbm, vmem, vmem],
        out_shape=[
            jax.ShapeDtypeStruct((shard, hidden), F32),
            small,
            small,
            small,
            jax.ShapeDtypeStruct((states, tokens, width), BF16),
            jax.ShapeDtypeStruct((tokens, mix.shape[1]), F32),
            jax.ShapeDtypeStruct((4, width), F32),
        ],
        scratch_shapes=[
            pltpu.VMEM((4, 8, width), F32),
            pltpu.VMEM((steps, 4, width), F32),
            pltpu.VMEM((steps, 4, width), F32),
            pltpu.VMEM((4, tokens, width), BF16),
            pltpu.VMEM((blocks, 4, 64, width), BF16),
            pltpu.VMEM((blocks, 4, 64, width), BF16),
            pltpu.VMEM((shard, cols), BF16),
            pltpu.VMEM((half, 2, shard, cols), BF16),
            pltpu.VMEM((2, states, UNIT, width), BF16),
            pltpu.VMEM((2, 4, UNIT, width), F32),
            pltpu.VMEM((2, UNIT, width), F32),
            pltpu.VMEM((2, states, UNIT, width), BF16),
            pltpu.VMEM((4, GROUP, width), F32),
            dma((half, 2, count)),
            dma((half, 2, count)),
            dma((blocks,)),
            dma((blocks,)),
            dma((blocks,)),
            dma((blocks,)),
            dma((blocks,)),
            dma((blocks,)),
            dma(()),
            dma((2, 3)),
            dma((2,)),
            dma((steps,)),
            dma((steps,)),
            pltpu.SemaphoreType.REGULAR((blocks,)),
        ],
        cost_estimate=pl.CostEstimate(
            flops=tokens * width * 2000, bytes_accessed=tokens * width * 64, transcendentals=0
        ),
        compiler_params=pltpu.CompilerParams(
            collective_id=1, has_side_effects=True, vmem_limit_bytes=62 * MIB
        ),
        name="back_stage",
    )(normed, hidden_grad, qkv_low, stats, mix, gains, parts, history, streams, out_total)


TILE = 512


def unrotate(values, turn):
    return (
        values * turn[0]
        + pltpu.roll(values, HEAD_DIM - ROT // 2, 1) * turn[1]
        + pltpu.roll(values, ROT // 2, 1) * turn[2]
    )


def attention_probs(query, key, seg_col, seg_row):
    tokens = query.shape[0]
    scores = dot(query, key, ((1,), (1,))) * (HEAD_DIM ** (-0.5))
    later = lax.broadcasted_iota(jnp.int32, (tokens, tokens), 1) > lax.broadcasted_iota(
        jnp.int32, (tokens, tokens), 0
    )
    scores = jnp.where(jnp.logical_or(seg_col != seg_row, later), -1e30, scores)
    weights = jnp.exp(scores - jnp.max(scores, axis=1, keepdims=True))
    return weights / jnp.sum(weights, axis=1, keepdims=True)


def mid_kernel(
    size,
    low_t,
    grad_blocks,
    hidden,
    heads,
    turn,
    seg_col,
    seg_row,
    gen_grad,
    gen_gain,
    gen_mid,
    low_all,
    up_full,
    qkv_full,
    grad_out,
    grad_down,
    hidden_grad,
    qkv_low,
    parts,
    gen_sum,
    mid_sum,
    attended_grad,
    far,
    ring,
    low_tile,
    up_tile,
    qkv_tile,
    stage,
    gen_sent,
    gen_got,
    mid_sent,
    mid_got,
    ring_send,
    ring_recv,
    tile_sem,
    stage_sem,
    gen_send,
    gen_recv,
):
    half = size // 2
    rows_all, tokens = low_t.shape
    shard = grad_blocks.shape[2]
    local = heads.shape[1] // 3
    me = lax.axis_index("dp")
    lane = lax.axis_index("tensor")
    place = place_of(me, size)
    right = index_at(place + 1, size)
    left = index_at(place - 1, size)
    steps = size.bit_length() - 1
    partners = [me + (1 << step) * (1 - 2 * lax.rem(lax.div(me, 1 << step), 2)) for step in range(steps)]
    barrier = pltpu.get_barrier_semaphore()
    for there in [right, left] + partners:
        pl.semaphore_signal(barrier, inc=1, device_id=(there, lane), device_id_type=MESH)
    pl.semaphore_wait(barrier, 2 + steps)

    low_tiles = rows_all // TILE
    width_tiles = up_full.shape[0] // TILE
    order = (
        [("low", at) for at in range(low_tiles)]
        + [("up", at) for at in range(width_tiles)]
        + [("qkv", at) for at in range(width_tiles)]
    )

    def load(index):
        kind, at = order[index]
        slot = at % 2
        rows = pl.ds(at * TILE, TILE)
        if kind == "low":
            return pltpu.make_async_copy(low_all.at[:, rows, :], low_tile.at[slot], tile_sem.at[0, slot])
        if kind == "up":
            return pltpu.make_async_copy(up_full.at[rows, :], up_tile.at[slot], tile_sem.at[1, slot])
        return pltpu.make_async_copy(qkv_full.at[rows, :], qkv_tile.at[slot], tile_sem.at[2, slot])

    load(0).start()

    pieces = rows_all // TILE
    cut = TILE // 2

    def term(distance, piece):
        owner = index_at(place + distance, size)
        return jnp.dot(
            low_t[pl.ds(piece * TILE, TILE), :], grad_blocks[owner], preferred_element_type=F32
        )

    def send(hop, way, piece):
        if hop == 0:
            rows = pl.ds(piece * TILE + way * cut, cut)
            source = far.at[rows, :]
        else:
            rows = pl.ds(piece * TILE, TILE)
            source = ring.at[hop - 1, way, rows, :]
        return pltpu.make_async_remote_copy(
            src_ref=source,
            dst_ref=ring.at[hop, way, rows, :],
            send_sem=ring_send.at[hop, way, piece],
            recv_sem=ring_recv.at[hop, way, piece],
            device_id=((right, left)[way], lane),
            device_id_type=MESH,
        )

    for piece in range(pieces):
        far[pl.ds(piece * TILE, TILE), :] = term(half, piece).astype(BF16)
        for way in range(2):
            send(0, way, piece).start()

    def low_grad(at):
        index = at
        load(index + 1).start()
        load(index).wait()
        total = None
        for owner in range(size):
            part = dot(grad_blocks[owner], low_tile[at % 2, owner], ((1,), (1,)))
            total = part if total is None else total + part
        base = at * TILE
        if base < local:
            attended_grad[:, base : base + TILE] = total.astype(BF16)
        else:
            cols = slice(base - local, base - local + TILE)
            hidden_grad[:, cols] = (total * gelu_slope(hidden[:, cols])).astype(BF16)

    def head_grad(head):
        cols = slice(head * HEAD_DIM, (head + 1) * HEAD_DIM)
        key_cols = slice(local + head * HEAD_DIM, local + (head + 1) * HEAD_DIM)
        value_cols = slice(2 * local + head * HEAD_DIM, 2 * local + (head + 1) * HEAD_DIM)
        query, key, value = heads[:, cols], heads[:, key_cols], heads[:, value_cols]
        upstream = attended_grad[:, cols]
        probs = attention_probs(query, key, seg_col[...], seg_row[...])
        probs_grad = dot(upstream, value, ((1,), (1,)))
        qkv_low[:, value_cols] = dot(probs.astype(BF16), upstream, ((0,), (0,))).astype(BF16)
        row = jnp.sum(probs * probs_grad, axis=1, keepdims=True)
        scores_grad = (probs * (probs_grad - row)).astype(BF16)
        scale = HEAD_DIM ** (-0.5)
        turns = [turn[which] for which in range(3)]
        query_grad = dot(scores_grad, key, ((1,), (0,))) * scale
        qkv_low[:, cols] = unrotate(query_grad, turns).astype(BF16)
        key_grad = dot(scores_grad, query, ((0,), (0,))) * scale
        qkv_low[:, key_cols] = unrotate(key_grad, turns).astype(BF16)

    def part_store(stream, at):
        return pltpu.make_async_copy(
            stage.at[stream], parts.at[stream, :, pl.ds(at * TILE, TILE)], stage_sem.at[stream]
        )

    def up_part(at):
        index = low_tiles + at
        load(index + 1).start()
        load(index).wait()
        if at:
            part_store(3, at - 1).wait()
        stage[3] = dot(hidden_grad[...], up_tile[at % 2], ((1,), (1,))).astype(BF16)
        part_store(3, at).start()

    def qkv_part(at):
        index = low_tiles + width_tiles + at
        if index + 1 < len(order):
            load(index + 1).start()
        load(index).wait()
        for stream in range(3):
            if at:
                part_store(stream, at - 1).wait()
            cols = slice(stream * local, (stream + 1) * local)
            stage[stream] = dot(qkv_low[:, cols], qkv_tile[at % 2, :, cols], ((1,), (1,))).astype(BF16)
            part_store(stream, at).start()

    def gen_copies(step):
        return [
            pltpu.make_async_remote_copy(
                src_ref=sent.at[step],
                dst_ref=got.at[step],
                send_sem=gen_send.at[step, which],
                recv_sem=gen_recv.at[step, which],
                device_id=(partners[step], lane),
                device_id_type=MESH,
            )
            for which, (sent, got) in enumerate(((gen_sent, gen_got), (mid_sent, mid_got)))
        ]

    def gen_step(step):
        if step == 0:
            units = gen_grad.shape[0]
            gen_sent[0, :units, :] = gen_grad[...].astype(BF16)
            gen_sent[0, units:, :] = jnp.broadcast_to(
                gen_gain[...].astype(BF16), (gen_sent.shape[1] - units, gen_sent.shape[2])
            )
            mid_sent[0] = gen_mid[...]
        else:
            for copy in gen_copies(step - 1):
                copy.wait_recv()
            total = gen_sent[step - 1].astype(F32) + gen_got[step - 1].astype(F32)
            mid_total = mid_sent[step - 1] + mid_got[step - 1]
            if step == steps:
                gen_sum[...] = total
                mid_sum[...] = mid_total
            else:
                gen_sent[step] = total.astype(BF16)
                mid_sent[step] = mid_total
        if step < steps:
            for copy in gen_copies(step):
                copy.start()

    tasks = [(low_grad, at) for at in range(low_tiles)]
    tasks += [(head_grad, head) for head in range(local // HEAD_DIM)]
    tasks += [(up_part, at) for at in range(width_tiles)]
    tasks += [(qkv_part, at) for at in range(width_tiles)]
    for step in range(steps + 1):
        tasks.insert(2 + 5 * step if steps < 4 else 2 + 3 * step, (gen_step, step))
    count = len(tasks)
    slots = half * pieces
    slot = 0
    for hop in range(1, half + 1):
        for piece in range(pieces):
            rows = pl.ds(piece * TILE, TILE)
            for way in range(2):
                send(hop - 1, way, piece).wait_recv()
                if hop == half:
                    continue
                full = term((half - hop) * (1 - 2 * way), piece)
                if hop == 1:
                    with_rows = pl.ds(piece * TILE + way * cut, cut)
                    only_rows = pl.ds(piece * TILE + (1 - way) * cut, cut)
                    got = ring[0, way, with_rows, :].astype(F32)
                    ring[0, way, with_rows, :] = (full[way * cut : way * cut + cut] + got).astype(BF16)
                    ring[0, way, only_rows, :] = full[(1 - way) * cut : (1 - way) * cut + cut].astype(BF16)
                else:
                    got = ring[hop - 1, way, rows, :].astype(F32)
                    ring[hop - 1, way, rows, :] = (full + got).astype(BF16)
                send(hop, way, piece).start()
            if hop == half:
                total = (
                    term(0, piece)
                    + ring[hop - 1, 0, rows, :].astype(F32)
                    + ring[hop - 1, 1, rows, :].astype(F32)
                )
                base = piece * TILE
                if base < local:
                    grad_out[base : base + TILE, :] = total
                else:
                    grad_down[base - local : base - local + TILE, :] = total
            slot += 1
            while tasks and (slot == slots or len(tasks) * (slots - 2) > count * max(slots - 2 - slot, 0)):
                run, value = tasks.pop(0)
                run(value)
    for stream in range(4):
        part_store(stream, width_tiles - 1).wait()
    for step in range(steps):
        for copy in gen_copies(step):
            copy.wait_send()
    for hop in range(half):
        for piece in range(pieces):
            for way in range(2):
                send(hop, way, piece).wait_send()


def mid_stage(
    size,
    low_t,
    grad_blocks,
    hidden,
    heads,
    turn,
    seg_col,
    seg_row,
    gen_grad,
    gen_gain,
    gen_mid,
    low_all,
    up_full,
    qkv_full,
):
    half = size // 2
    rows_all, tokens = low_t.shape
    shard = grad_blocks.shape[2]
    hidden_cols = hidden.shape[1]
    local = heads.shape[1] // 3
    width = up_full.shape[0]
    pieces = rows_all // TILE
    steps = size.bit_length() - 1
    units = gen_grad.shape[0]
    vmem = pl.BlockSpec(memory_space=pltpu.VMEM)
    hbm = pl.BlockSpec(memory_space=pl.ANY)
    dma = pltpu.SemaphoreType.DMA
    return pl.pallas_call(
        lambda *refs: mid_kernel(size, *refs),
        in_specs=[vmem] * 10 + [hbm] * 3,
        out_specs=[vmem] * 4 + [hbm, vmem, vmem],
        out_shape=[
            jax.ShapeDtypeStruct((local, shard), F32),
            jax.ShapeDtypeStruct((hidden_cols, shard), F32),
            jax.ShapeDtypeStruct((tokens, hidden_cols), BF16),
            jax.ShapeDtypeStruct((tokens, 3 * local), BF16),
            jax.ShapeDtypeStruct((4, tokens, width), BF16),
            jax.ShapeDtypeStruct((units + 8, width), F32),
            jax.ShapeDtypeStruct(gen_mid.shape, F32),
        ],
        scratch_shapes=[
            pltpu.VMEM((tokens, local), BF16),
            pltpu.VMEM((rows_all, shard), BF16),
            pltpu.VMEM((half, 2, rows_all, shard), BF16),
            pltpu.VMEM((2, size, TILE, shard), BF16),
            pltpu.VMEM((2, TILE, hidden_cols), BF16),
            pltpu.VMEM((2, TILE, 3 * local), BF16),
            pltpu.VMEM((4, tokens, TILE), BF16),
            pltpu.VMEM((steps, units + 8, width), BF16),
            pltpu.VMEM((steps, units + 8, width), BF16),
            pltpu.VMEM((steps,) + gen_mid.shape, F32),
            pltpu.VMEM((steps,) + gen_mid.shape, F32),
            dma((half, 2, pieces)),
            dma((half, 2, pieces)),
            dma((3, 2)),
            dma((4,)),
            dma((steps, 2)),
            dma((steps, 2)),
        ],
        cost_estimate=pl.CostEstimate(
            flops=tokens * width * 4000, bytes_accessed=tokens * width * 40, transcendentals=0
        ),
        compiler_params=pltpu.CompilerParams(
            collective_id=2, has_side_effects=True, vmem_limit_bytes=62 * MIB
        ),
        name="mid_stage",
    )(
        low_t,
        grad_blocks,
        hidden,
        heads,
        turn,
        seg_col,
        seg_row,
        gen_grad,
        gen_gain,
        gen_mid,
        low_all,
        up_full,
        qkv_full,
    )


def front_kernel(
    size,
    mix,
    gains,
    turn,
    seg_col,
    seg_row,
    history,
    w_query,
    w_key,
    w_value,
    w_up,
    w_out,
    w_down,
    stats,
    heads,
    hidden,
    low_t,
    branch,
    normed_out,
    streams,
    qkv_all,
    up_all,
    low_all,
    normed,
    low,
    weight_tile,
    low_tile,
    state_in,
    stream_out,
    from_core,
    from_link,
    qkv_send,
    qkv_recv,
    up_send,
    up_recv,
    low_send,
    low_recv,
    own_sem,
    state_sem,
    stream_sem,
    normed_sem,
    weight_sem,
    tile_sem,
    core_send,
    core_recv,
    link_send,
    link_recv,
    twin_send,
    twin_recv,
    freed,
):
    half = size // 2
    states, tokens, width = history.shape
    shard = width // size
    local = w_query.shape[1]
    hidden_cols = w_up.shape[1]
    inverse = 1.0 / width
    me = lax.axis_index("dp")
    lane = lax.axis_index("tensor")
    place = place_of(me, size)
    right = index_at(place + 1, size)
    left = index_at(place - 1, size)
    core = lax.rem(lane, 2)
    chip = lax.div(lane, 2)
    twin = chip * 2 + 1 - core
    across = (1 - chip) * 2 + core
    rows_half = tokens // 2

    barrier = pltpu.get_barrier_semaphore()
    for there in ((right, lane), (left, lane), (me, twin), (me, across)):
        pl.semaphore_signal(barrier, inc=1, device_id=there, device_id_type=MESH)
    pl.semaphore_wait(barrier, 4)

    wide = TILE
    groups = [
        [(w_query, 0, 0), (w_key, 0, local), (w_value, 0, 2 * local)],
        [(w_up, at, at) for at in range(0, hidden_cols, wide)],
        [(w_out, at, at) for at in range(0, local, wide)]
        + [(w_down, at, local + at) for at in range(0, hidden_cols, wide)],
    ]
    sems = [(qkv_send, qkv_recv), (up_send, up_recv), (low_send, low_recv)]
    cut = (shard // 2, shard // 2, wide // 2)

    def own(group, piece, lo, count):
        source, at, _ = groups[group][piece]
        if group == 2:
            return source.at[pl.ds(at + lo, count), :]
        cols = local if group == 0 else wide
        return source.at[pl.ds(lo, count), pl.ds(at, cols)]

    def held(group, piece, owner, lo, count):
        _, _, at = groups[group][piece]
        if group == 2:
            return low_all.at[owner, pl.ds(at + lo, count), :]
        rows = pl.ds(pl.multiple_of(owner * shard + lo, cut[0]), count)
        if group == 0:
            return qkv_all.at[rows, pl.ds(at, local)]
        return up_all.at[rows, pl.ds(at, wide)]

    def send(group, hop, way, piece):
        owner = index_at(place + (hop - 1) * (2 * way - 1), size)
        whole = shard if group < 2 else wide
        lo, count = (0, whole) if hop < half else (way * cut[group], cut[group])
        target = held(group, piece, owner, lo, count)
        source = own(group, piece, lo, count) if hop == 1 else target
        send_sem, recv_sem = sems[group]
        return pltpu.make_async_remote_copy(
            src_ref=source,
            dst_ref=target,
            send_sem=send_sem.at[hop - 1, way, piece],
            recv_sem=recv_sem.at[hop - 1, way, piece],
            device_id=((right, left)[way], lane),
            device_id_type=MESH,
        )

    def own_copies(group):
        whole = shard if group < 2 else wide
        return [
            pltpu.make_async_copy(
                own(group, piece, 0, whole), held(group, piece, me, 0, whole), own_sem.at[group, piece]
            )
            for piece in range(len(groups[group]))
        ]

    units = tokens // UNIT

    def state_load(unit):
        return pltpu.make_async_copy(
            history.at[:, pl.ds(unit * UNIT, UNIT), :], state_in.at[unit % 2], state_sem.at[unit % 2]
        )

    def stream_store(unit):
        return pltpu.make_async_copy(
            stream_out.at[unit % 2], streams.at[:, pl.ds(unit * UNIT, UNIT), :], stream_sem.at[unit % 2]
        )

    def mix_unit(unit):
        slot = unit % 2
        if unit + 1 < units:
            state_load(unit + 1).start()
        state_load(unit).wait()
        if unit >= 2:
            stream_store(unit - 2).wait()

        @pl.loop(0, UNIT // GROUP)
        def _(step):
            rows = pl.ds(pl.multiple_of(unit * UNIT + step * GROUP, GROUP), GROUP)
            inner = pl.ds(pl.multiple_of(step * GROUP, GROUP), GROUP)
            weights = mix[rows, :]
            sums = [jnp.zeros((GROUP, 128), F32) for _ in range(4)]
            for at in range(0, width, CHUNK):
                cols = pl.ds(at, CHUNK)
                total = [None] * 4
                for source in range(states):
                    state = state_in[slot, source, inner, cols].astype(F32)
                    for stream in range(4):
                        k = stream * states + source
                        term = weights[:, k : k + 1] * state
                        total[stream] = term if source == 0 else total[stream] + term
                for stream in range(4):
                    stream_out[slot, stream, inner, cols] = total[stream]
                    for at_lane in range(0, CHUNK, 128):
                        sums[stream] = sums[stream] + total[stream][:, at_lane : at_lane + 128]
            for stream in range(4):
                mean = jnp.sum(sums[stream], axis=1, keepdims=True) * inverse
                square = jnp.zeros((GROUP, 128), F32)
                for at in range(0, width, CHUNK):
                    center = stream_out[slot, stream, inner, pl.ds(at, CHUNK)] - mean
                    center = center * center
                    for at_lane in range(0, CHUNK, 128):
                        square = square + center[:, at_lane : at_lane + 128]
                scale = lax.rsqrt(jnp.sum(square, axis=1, keepdims=True) * inverse + EPSILON)
                stats[rows, stream : stream + 1] = mean
                stats[rows, 4 + stream : 5 + stream] = scale
                for at in range(0, width, CHUNK):
                    cols = pl.ds(at, CHUNK)
                    center = stream_out[slot, stream, inner, cols] - mean
                    value = (center * scale * gains[stream : stream + 1, cols]).astype(BF16)
                    for owner in range(at // shard, (at + CHUNK) // shard):
                        base = owner * shard - at
                        normed[stream, owner, rows, :] = value[:, base : base + shard]

        stream_store(unit).start()
        if unit == units - 1:
            normed_store().start()

    def normed_store():
        return pltpu.make_async_copy(normed, normed_out, normed_sem)

    tiles = 3 + hidden_cols // wide

    def weight_load(tile):
        if tile < 3:
            source = qkv_all.at[:, pl.ds(tile * local, local)]
        else:
            source = up_all.at[:, pl.ds((tile - 3) * wide, wide)]
        return pltpu.make_async_copy(source, weight_tile.at[tile % 2], weight_sem.at[tile % 2])

    def arrived(group):
        for copy in own_copies(group):
            copy.wait()
        for piece in range(len(groups[group])):
            for way in range(2):
                send(group, half, way, piece).wait_recv()

    def tile_product(tile, stream):
        weight_load(tile).wait()
        total = None
        for owner in range(size):
            part = jnp.dot(
                normed[stream, owner],
                weight_tile[tile % 2, owner * shard : (owner + 1) * shard, :],
                preferred_element_type=F32,
            )
            total = part if total is None else total + part
        return total

    def qkv_task(which):
        if which == 0:
            arrived(0)
            weight_load(0).start()
        if which < 2:
            weight_load(which + 1).start()
        product = tile_product(which, which)
        for head in range(local // HEAD_DIM):
            at = head * HEAD_DIM
            part = product[:, at : at + HEAD_DIM]
            if which < 2:
                part = (
                    part * turn[0]
                    - pltpu.roll(part, HEAD_DIM - ROT // 2, 1) * turn[1]
                    - pltpu.roll(part, ROT // 2, 1) * turn[2]
                )
            heads[:, which * local + at : which * local + at + HEAD_DIM] = part.astype(BF16)

    def head_task(head):
        at = head * HEAD_DIM
        query = heads[:, at : at + HEAD_DIM]
        key = heads[:, local + at : local + at + HEAD_DIM]
        value = heads[:, 2 * local + at : 2 * local + at + HEAD_DIM]
        probs = attention_probs(query, key, seg_col[...], seg_row[...]).astype(BF16)
        attended = jnp.dot(probs, value, preferred_element_type=F32)
        low[:, at : at + HEAD_DIM] = attended.astype(BF16)
        low_t[at : at + HEAD_DIM, :] = attended.T.astype(BF16)

    def up_task(at):
        if at == 0:
            arrived(1)
            weight_load(3).start()
        if at + 1 < tiles - 3:
            weight_load(4 + at).start()
        product = tile_product(3 + at, 3)
        cols = slice(at * wide, (at + 1) * wide)
        hidden[:, cols] = product
        active = gelu(product)
        low[:, local + at * wide : local + (at + 1) * wide] = active.astype(BF16)
        low_t[local + at * wide : local + (at + 1) * wide, :] = active.T.astype(BF16)

    distances = [0]
    for hop in range(1, half):
        distances += [-hop, hop]
    distances += [half]

    def tile_load(index):
        owner = index_at(place + distances[index], size)
        return pltpu.make_async_copy(low_all.at[owner], low_tile.at[index % 2], tile_sem.at[index % 2])

    def mine(index):
        return pl.ds(pl.multiple_of(core * rows_half, rows_half), rows_half)

    def core_copy(index):
        owner = index_at(place + distances[index], size)
        rows = pl.ds(pl.multiple_of((1 - core) * rows_half, rows_half), rows_half)
        return pltpu.make_async_remote_copy(
            src_ref=branch.at[owner, rows, :],
            dst_ref=from_core.at[index],
            send_sem=core_send.at[index],
            recv_sem=core_recv.at[index],
            device_id=(me, twin),
            device_id_type=MESH,
        )

    def link_copy(index):
        owner = index_at(place + distances[index], size)
        return pltpu.make_async_remote_copy(
            src_ref=branch.at[owner, mine(index), :],
            dst_ref=from_link.at[index],
            send_sem=link_send.at[index],
            recv_sem=link_recv.at[index],
            device_id=(me, across),
            device_id_type=MESH,
        )

    def twin_copy(index):
        owner = index_at(place + distances[index], size)
        return pltpu.make_async_remote_copy(
            src_ref=branch.at[owner, mine(index), :],
            dst_ref=branch.at[owner, mine(index), :],
            send_sem=twin_send.at[index],
            recv_sem=twin_recv.at[index],
            device_id=(me, twin),
            device_id_type=MESH,
        )

    def low_task(index):
        if index == 0:
            for copy in own_copies(2):
                copy.wait()
        owner = index_at(place + distances[index], size)
        load = tile_load(index)
        load.start()
        load.wait()
        branch[owner] = jnp.dot(low[...], low_tile[index % 2], preferred_element_type=F32).astype(BF16)
        core_copy(index).start()

    def add_into(index, other):
        owner = index_at(place + distances[index], size)
        rows = mine(index)
        branch[owner, rows, :] = (
            branch[owner, rows, :].astype(F32) + other[index].astype(F32)
        ).astype(BF16)

    def link_task(index):
        copy = core_copy(index)
        copy.wait_send()
        pl.semaphore_signal(freed.at[index], inc=1, device_id=(me, twin), device_id_type=MESH)
        copy.wait_recv()
        add_into(index, from_core)
        link_copy(index).start()

    def twin_task(index):
        copy = link_copy(index)
        copy.wait_send()
        copy.wait_recv()
        add_into(index, from_link)
        pl.semaphore_wait(freed.at[index], 1)
        twin_copy(index).start()

    state_load(0).start()
    slots = [(group, hop) for group in range(3) for hop in range(1, half + 1)]
    counts = [len(pieces) for pieces in groups]
    first = [0, counts[0] * half, (counts[0] + counts[1]) * half]
    total_slots = sum(counts) * half
    tasks = []
    span = max(first[1] - 2, 1)
    for unit in range(units):
        tasks.append((counts[0] - 1 + unit * (first[1] - counts[0]) / units, mix_unit, unit))
    early = first[1] + counts[1]
    for which in range(3):
        tasks.append((early + which, qkv_task, which))
    for head in range(local // HEAD_DIM):
        tasks.append((early + 3 + head, head_task, head))
    middle = first[2] + counts[2]
    for at in range(tiles - 3):
        tasks.append((middle + at, up_task, at))
    for index in range(len(distances) - 1):
        due = max(first[2] + counts[2] * (abs(distances[index]) + 1) - 1, middle + tiles - 3) + 0.5 * (index % 2)
        tasks.append((due, low_task, index))
        tasks.append((due + 1, link_task, index))
        tasks.append((due + 3, twin_task, index))
    tasks.sort(key=lambda item: item[0])

    at_slot = 0
    for group, hop in slots:
        if hop == 1:
            for copy in own_copies(group):
                copy.start()
        for piece in range(counts[group]):
            for way in range(2):
                if hop > 1:
                    send(group, hop - 1, way, piece).wait_recv()
                if hop < half or True:
                    send(group, hop, way, piece).start()
            while tasks and tasks[0][0] <= at_slot and at_slot < total_slots - 1:
                _, run, value = tasks.pop(0)
                run(value)
            at_slot += 1
    for _, run, value in tasks:
        run(value)
    for piece in range(counts[2]):
        for way in range(2):
            send(2, half, way, piece).wait_recv()
    last = len(distances) - 1
    low_task(last)
    link_task(last)
    twin_task(last)
    for index in range(len(distances)):
        copy = twin_copy(index)
        copy.wait_send()
        copy.wait_recv()
    for unit in range(units - 2, units):
        stream_store(unit).wait()
    normed_store().wait()
    for group, hop in slots:
        for piece in range(counts[group]):
            for way in range(2):
                send(group, hop, way, piece).wait_send()


def front_stage(size, mix, gains, turn, seg_col, seg_row, history, w_query, w_key, w_value, w_up, w_out, w_down):
    half = size // 2
    states, tokens, width = history.shape
    shard = width // size
    local = w_query.shape[1]
    hidden_cols = w_up.shape[1]
    rows_all = local + hidden_cols
    vmem = pl.BlockSpec(memory_space=pltpu.VMEM)
    hbm = pl.BlockSpec(memory_space=pl.ANY)
    dma = pltpu.SemaphoreType.DMA
    up_pieces = hidden_cols // TILE
    low_pieces = rows_all // TILE
    return pl.pallas_call(
        lambda *refs: front_kernel(size, *refs),
        in_specs=[vmem] * 5 + [hbm] * 7,
        out_specs=[vmem] * 5 + [hbm] * 5,
        out_shape=[
            jax.ShapeDtypeStruct((tokens, 8), F32),
            jax.ShapeDtypeStruct((tokens, 3 * local), BF16),
            jax.ShapeDtypeStruct((tokens, hidden_cols), F32),
            jax.ShapeDtypeStruct((rows_all, tokens), BF16),
            jax.ShapeDtypeStruct((size, tokens, shard), BF16),
            jax.ShapeDtypeStruct((4, size, tokens, shard), BF16),
            jax.ShapeDtypeStruct((4, tokens, width), F32),
            jax.ShapeDtypeStruct((width, 3 * local), BF16),
            jax.ShapeDtypeStruct((width, hidden_cols), BF16),
            jax.ShapeDtypeStruct((size, rows_all, shard), BF16),
        ],
        scratch_shapes=[
            pltpu.VMEM((4, size, tokens, shard), BF16),
            pltpu.VMEM((tokens, rows_all), BF16),
            pltpu.VMEM((2, width, TILE), BF16),
            pltpu.VMEM((2, rows_all, shard), BF16),
            pltpu.VMEM((2, states, UNIT, width), BF16),
            pltpu.VMEM((2, 4, UNIT, width), F32),
            pltpu.VMEM((size, tokens // 2, shard), BF16),
            pltpu.VMEM((size, tokens // 2, shard), BF16),
            dma((half, 2, 3)),
            dma((half, 2, 3)),
            dma((half, 2, up_pieces)),
            dma((half, 2, up_pieces)),
            dma((half, 2, low_pieces)),
            dma((half, 2, low_pieces)),
            dma((3, low_pieces)),
            dma((2,)),
            dma((2,)),
            dma(()),
            dma((2,)),
            dma((2,)),
            dma((size,)),
            dma((size,)),
            dma((size,)),
            dma((size,)),
            dma((size,)),
            dma((size,)),
            pltpu.SemaphoreType.REGULAR((size,)),
        ],
        cost_estimate=pl.CostEstimate(
            flops=tokens * width * 8000, bytes_accessed=tokens * width * 80, transcendentals=0
        ),
        compiler_params=pltpu.CompilerParams(
            collective_id=3, has_side_effects=True, vmem_limit_bytes=62 * MIB
        ),
        name="front_stage",
    )(mix, gains, turn, seg_col, seg_row, history, w_query, w_key, w_value, w_up, w_out, w_down)


def body(
    sizes,
    history,
    mix_weights,
    segments,
    norm_gains,
    w_query,
    w_key,
    w_value,
    w_out,
    w_up,
    w_down,
    gen_in,
    gen_out,
    out_grad,
    next_grad,
):
    dp_size, tensor_size = sizes
    width = history.shape[2]
    tok_count = history.shape[1]
    mix_rows = mix_weights.T
    cos_row, sin_row = rotary_tables(segments)
    blank = jnp.zeros((tok_count, HEAD_DIM - ROT // 2), F32)
    turn = jnp.stack(
        [
            jnp.concatenate([cos_row, cos_row, blank[:, ROT // 2 :] + 1.0], axis=1),
            jnp.concatenate([sin_row, blank], axis=1),
            jnp.concatenate([blank[:, : ROT // 2], -sin_row, blank[:, ROT // 2 :]], axis=1),
        ]
    )
    seg_col, seg_row = segments[:, None], segments[None, :]
    stats, heads, hidden, low_t, branch, normed, streams, full_qkv, full_up, low_all = front_stage(
        dp_size,
        mix_rows,
        norm_gains,
        turn,
        seg_col,
        seg_row,
        history,
        w_query,
        w_key,
        w_value,
        w_up,
        w_out,
        w_down,
    )
    layer_out, next_mix, out_total, branch_grad, gain_gen_grad, grad_gen_in, grad_gen_out = gen_stage(
        dp_size, streams, branch, norm_gains, gen_in, gen_out, out_grad, next_grad.T
    )

    gen_units, gen_next = gen_out.shape
    gen_mid = jnp.pad(grad_gen_out, ((0, 0), (0, 128 - gen_next)))
    grad_out, grad_down, hidden_grad, qkv_low, parts, gen_sum, mid_sum = mid_stage(
        dp_size,
        low_t,
        branch_grad,
        hidden,
        heads,
        turn,
        seg_col,
        seg_row,
        grad_gen_in,
        gain_gen_grad,
        gen_mid,
        low_all,
        full_up,
        full_qkv,
    )
    grad_up, grad_query, grad_key, grad_value, history_grad, mix_grad, gain_sums = back_stage(
        dp_size,
        normed,
        hidden_grad,
        qkv_low,
        stats,
        mix_rows,
        norm_gains,
        parts,
        history,
        streams,
        out_total,
    )
    return (
        layer_out,
        next_mix.T,
        history_grad,
        mix_grad.T,
        jnp.concatenate([gain_sums, gen_sum[gen_units : gen_units + 1]], axis=0),
        grad_query,
        grad_key,
        grad_value,
        grad_out,
        grad_up,
        grad_down,
        gen_sum[:gen_units].T,
        mid_sum[:, :gen_next],
    )


def solution(mesh):
    sizes = (mesh.shape["dp"], mesh.shape["tensor"])
    in_specs = (
        P(None, "dp", None),
        P(None, "dp"),
        P("dp"),
        P(),
        P("dp", "tensor"),
        P("dp", "tensor"),
        P("dp", "tensor"),
        P("tensor", "dp"),
        P("dp", "tensor"),
        P("tensor", "dp"),
        P(),
        P(),
        P("dp", None),
        P(None, "dp"),
    )
    out_specs = (
        P("dp", None),
        P(None, "dp"),
        P(None, "dp", None),
        P(None, "dp"),
        P(),
        P("dp", "tensor"),
        P("dp", "tensor"),
        P("dp", "tensor"),
        P("tensor", "dp"),
        P("dp", "tensor"),
        P("tensor", "dp"),
        P(),
        P(),
    )

    def step(*arrays):
        return body(sizes, *arrays)

    return jax.shard_map(step, mesh=mesh, in_specs=in_specs, out_specs=out_specs, check_vma=False)
```

time: 1380 us -> 598 us (0.43)
  waiting for transfers between devices: 987 us -> 0 us
  Pallas kernels: 0 us -> 546 us
  other arithmetic: 151 us -> 4.56 us
  matrix products: 131 us -> 0 us
  blocking collectives: 38 us -> 0 us
  between operations: 16.4 us -> 1.22 us
    pallas_call x0 -> x4, Pallas kernels: none -> 546 us  [the longest x1 260 us: front_stage(): pl.pallas_call(lambda *refs: front_kernel(size, *refs), in_specs=[vmem] *...]
    reduce_scatter x6 -> x0, waiting for transfers between devices: 442 us -> none  [the longest x1 150 us: body(): lax.psum_scatter(grad_down.astype(jnp.bfloat16), 'dp', scatter_dimension=...]
    all_gather x6 -> x0, waiting for transfers between devices: 335 us -> none  [the longest x1 107 us: body(): lax.all_gather(w_up, 'dp', axis=0, tiled=True)]
    psum x3 -> x0, waiting for transfers between devices: 206 us -> none  [the longest x1 155 us: body(): lax.psum(mlp_normed_grad.astype(jnp.bfloat16), 'tensor').astype(jnp.float32)]
    dot_general x29 -> x0, matrix products: 127 us -> none  [the longest x24 121 us: matmul(): return jnp.dot(left_op, right_op, preferred_element_type=jnp.float32)]
    reduce_sum x22 -> x0, other arithmetic: 85.3 us -> none  [the longest x4 39.3 us: body(): jnp.sum(history[source].astype(jnp.float32) * stream_grads[stream], axis=1)]
    psum x1 -> x0, blocking collectives: 38 us -> none  [body(): lax.psum(jnp.stack(gain_grads).astype(jnp.bfloat16), 'dp')]
    convert_element_type x17 -> x0, other arithmetic: 33.1 us -> none  [the longest x3 15 us: body(): layer_norm(streams[stream], norm_gains[stream]).astype(jnp.bfloat16)]
  transfers between devices with their start and end apart: 15 -> 0, of which waited for: 13 -> 0; matrix products, arithmetic and copies ran while one was open for 20% -> 0% of each run, Pallas kernels for 0% -> 0%
where the time goes in v2:
time: 598 us; the launch traced here: 588 us
  Pallas kernels  546 us (91%)
  local copies, waits for them, and re-layouts  37.2 us (6%)
    pallas_call x1, Pallas kernels, front_stage(): pl.pallas_call(lambda *refs: front_kernel(size, *refs), in_specs=[vmem] *...  260 us
    pallas_call x1, Pallas kernels, back_stage(): pl.pallas_call(lambda *refs: back_kernel(size, *refs), in_specs=[vmem] *...  156 us
    pallas_call x1, Pallas kernels, mid_stage(): pl.pallas_call(lambda *refs: mid_kernel(size, *refs), in_specs=[vmem] * 1...  121 us
    unnamed x41, local copies, waits for them, and re-layouts  34.1 us

profile of v2, /device:TPU:0, one launch (start us, length us, event | category | flops | bytes accessed | tf_op | source)
XLA Modules:
  0.0 588.4 jit_solution(3643885114263237618)
XLA Ops:
  0.7 0.1 pad.16.clone
  0.7 0.1 pad.13.clone
  0.8 1.0 convert_reduce_fusion
  1.8 1.5 copy.48.refs_3_.refs_5_
  3.4 1.7 copy.46
  5.1 1.0 copy.49
  6.1 1.2 copy.50.gen_in
  7.3 1.0 multiply_cosine_fusion
  8.3 0.2 maximum_bitcast_fusion
  8.6 0.9 pad_maximum_fusion.refs_2_.refs_4_
  9.5 0.0 copy-start.3
  9.5 0.0 copy-start.4
  9.5 259.6 %front_stage.1 = (f32[512,8]{1,0:T(8,128)}, bf16[512,1536]{1,0:T(8,128)(2,1)}, f32[512,2048]{1,0:T(8,128)}, bf16[2560,512]{1,0:T(8,128)(2,1)}, bf16[8,512,256]{2...) custom-call(f32[512,36]{1,0:T(8,128)} %bitcast.17, ...), custom_call_target="tpu_custom_call" | custom-call | flops 8388608000 | bytes 83886080 | tf_op jit(solution)/shard_map/front_stage/pallas_call | solution.py:1361
  269.1 0.0 copy-done.3
  269.1 0.0 copy-done.4
  269.2 0.0 copy-start.1
  269.2 1.6 copy-done.1
  270.7 8.7 %gen_stage.1 = (bf16[512,2048]{1,0:T(8,128)(2,1)}, f32[512,40]{1,0:T(8,128)S(1)}, f32[512,2048]{1,0:T(8,128)}, bf16[8,512,256]{2,1,0:T(8,128)(2,1)S(1)}, f32[1,2...) custom-call(f32[4,512,2048]{2,1,0:T(8,128)} %get-tuple-element.44.stream.refs_8_, ...), custom_call_target="tpu_custom_call" | custom-call | flops 314572800 | bytes 16777216 | tf_op jit(solution)/shard_map/gen_stage/pallas_call | solution.py:97
  279.4 0.0 copy-start
  279.4 1.3 copy-done
  280.7 0.0 copy-start.2
  280.7 0.7 copy-done.2
  281.5 0.0 copy-start.5
  281.5 0.6 copy-done.5
  282.1 0.7 copy.52
  282.8 0.6 pad.5.refs_9_
  283.4 121.1 %mid_stage.1 = (f32[512,256]{1,0:T(8,128)}, f32[2048,256]{1,0:T(8,128)}, bf16[512,2048]{1,0:T(8,128)(2,1)}, bf16[512,1536]{1,0:T(8,128)(2,1)}, bf16[4,512,2048]{...) custom-call(bf16[2560,512]{1,0:T(8,128)(2,1)} %get-tuple-element.49.refs_0_, bf16[8,512,256]{2,1,0:T(8,128)(2,1)} %copy-done, ...), custom_call_target="tpu_custom_call" | custom-call | flops 4194304000 | bytes 41943040 | tf_op jit(solution)/shard_map/mid_stage/pallas_call | solution.py:893
  404.5 0.0 copy-start.12
  404.5 156.2 %back_stage.1 = (f32[256,2048]{1,0:T(8,128)}, f32[256,512]{1,0:T(8,128)}, f32[256,512]{1,0:T(8,128)}, f32[256,512]{1,0:T(8,128)}, bf16[9,512,2048]{2,1,0:T(8,128...) custom-call(bf16[4,8,512,256]{3,2,1,0:T(8,128)(2,1)} %get-tuple-element.48.refs_0_, ...), custom_call_target="tpu_custom_call" | custom-call | flops 2097152000 | bytes 67108864 | tf_op jit(solution)/shard_map/back_stage/pallas_call | solution.py:537
  560.7 1.7 copy.53
  562.4 0.0 copy-done.12
  562.4 0.7 slice_bitcast_fusion
  563.1 1.4 pad_maximum_fusion.1
  564.5 0.0 copy-start.11
  564.5 0.0 copy-start.10
  564.5 0.0 copy-start.9
  564.5 17.0 %copy.62 = bf16[9,512,2048]{2,1,0:T(8,128)(2,1)} copy(bf16[9,512,2048]{2,1,0:T(8,128)(2,1)} %get-tuple-element.147) | data formatting | bytes 37748736
  581.5 0.0 copy-done.11
  581.5 0.0 copy-start.8
  581.5 0.0 copy-start.7
  581.6 0.8 copy.63
  582.4 0.0 copy-done.10
  582.4 0.8 copy.64
  583.1 0.0 copy-done.9
  583.1 0.8 copy.65
  583.9 0.0 copy-done.8
  583.9 0.0 copy-start.6
  583.9 0.8 copy.66
  584.7 0.0 copy-done.7
  584.7 1.3 copy.67
  586.1 0.0 copy-done.6
  586.1 0.0 copy-start.13
  586.1 1.3 copy.68
  587.4 0.0 copy-done.13
  587.4 0.6 copy.69
  (8 shorter events, 0.1 us)
Async XLA Ops:
  9.5 259.6 %copy-start.3 = (f32[5,2048]{1,0:T(8,128)S(1)}, f32[5,2048]{1,0:T(8,128)}, u32[]{:S(2)}) copy-start(f32[5,2048]{1,0:T(8,128)} %refs_5_.3) | copy-start | bytes 122884
  9.5 259.7 %copy-start.4 = (bf16[40,40]{1,0:T(8,128)(2,1)S(1)}, bf16[40,40]{1,0:T(8,128)(2,1)}, u32[]{:S(2)}) copy-start(bf16[40,40]{1,0:T(8,128)(2,1)} %gen_out.1) | copy-start | bytes 9604
  269.2 1.6 copy-start.1
  279.4 1.3 copy-start
  280.7 0.7 copy-start.2
  281.5 0.6 copy-start.5
  404.5 157.9 %copy-start.12 = (f32[48,2048]{1,0:T(8,128)S(1)}, f32[48,2048]{1,0:T(8,128)}, u32[]{:S(2)}) copy-start(f32[48,2048]{1,0:T(8,128)} %get-tuple-element.67) | copy-start | bytes 1179652
  564.5 17.0 %copy-start.11 = (f32[256,512]{1,0:T(8,128)S(1)}, f32[256,512]{1,0:T(8,128)}, u32[]{:S(2)}) copy-start(f32[256,512]{1,0:T(8,128)} %get-tuple-element.150) | copy-start | bytes 1572868
  564.5 17.8 %copy-start.10 = (f32[256,512]{1,0:T(8,128)S(1)}, f32[256,512]{1,0:T(8,128)}, u32[]{:S(2)}) copy-start(f32[256,512]{1,0:T(8,128)} %get-tuple-element.151) | copy-start | bytes 1572868
  564.5 18.6 %copy-start.9 = (f32[256,512]{1,0:T(8,128)S(1)}, f32[256,512]{1,0:T(8,128)}, u32[]{:S(2)}) copy-start(f32[256,512]{1,0:T(8,128)} %get-tuple-element.152) | copy-start | bytes 1572868
  581.5 2.4 copy-start.8
  581.5 3.2 copy-start.7
  583.9 2.1 copy-start.6
  586.1 1.3 copy-start.13

commit v3 on v2

--- a/solution.py
+++ b/solution.py
@@ -1,5 +1,6 @@
 import jax
 import jax.numpy as jnp
+import numpy as np
 from jax import lax
 from jax.experimental import pallas as pl
 from jax.experimental.pallas import tpu as pltpu
@@ -14,18 +15,6 @@
 
 F32 = jnp.float32
 BF16 = jnp.bfloat16
-
-
-def rotary_tables(segments):
-    tok_count = segments.shape[0]
-    order_idx = jnp.arange(tok_count, dtype=jnp.int32)
-    same_doc = segments[:, None] == segments[None, :]
-    earlier = order_idx[None, :] < order_idx[:, None]
-    places = jnp.sum((same_doc & earlier).astype(jnp.int32), axis=1)
-    halves = jnp.arange(ROT // 2, dtype=jnp.float32)
-    frequency = ROPE_BASE ** (-2.0 * halves / ROT)
-    angles = places.astype(jnp.float32)[:, None] * frequency[None, :]
-    return jnp.cos(angles), jnp.sin(angles)
 
 
 MIB = 1 << 20
@@ -54,13 +43,13 @@
     unit = center * scale
     gains = gain[4:5, :]
     low = (unit * gains).astype(BF16)
-    hidden = dot(low, gen_in[...], ((1,), (0,)))
+    hidden = dot(low, gen_in[...], ((1,), (1,)))
     active = gelu(hidden).astype(BF16)
-    next_mix[...] = dot(active, gen_out[...], ((1,), (0,)))
-    upstream = next_grad[...].astype(BF16)
+    next_mix[...] = dot(active, gen_out[...], ((1,), (0,))).T
+    upstream = next_grad[...].T.astype(BF16)
     active_grad = dot(upstream, gen_out[...], ((1,), (1,)))
     hidden_grad = (active_grad * gelu_slope(hidden)).astype(BF16)
-    y = dot(hidden_grad, gen_in[...], ((1,), (1,)))
+    y = dot(hidden_grad, gen_in[...], ((1,), (0,)))
     e = y * gains
     grad = scale * (
         e - jnp.mean(e, axis=1, keepdims=True) - unit * jnp.mean(e * unit, axis=1, keepdims=True)
@@ -79,18 +68,19 @@
     def _():
         gain_grad[...] = gain_part
         in_grad[...] = in_part
-        mid_grad[...] = mid_part
+        mid_grad[...] = jnp.zeros_like(mid_grad)
+        mid_grad[:, : mid_part.shape[1]] = mid_part
 
     @pl.when(jnp.logical_not(first))
     def _():
         gain_grad[...] += gain_part
         in_grad[...] += in_part
-        mid_grad[...] += mid_part
+        mid_grad[:, : mid_part.shape[1]] += mid_part
 
 
 def gen_stage(size, streams, branch, gains, gen_in, gen_out, out_grad, next_grad, block=128):
     _, tokens, width = streams.shape
-    units = gen_in.shape[1]
+    units = gen_in.shape[0]
     nxt = gen_out.shape[1]
     row = lambda i: (i, 0)
     fixed = lambda i: (0, 0)
@@ -104,30 +94,30 @@
             pl.BlockSpec(gen_in.shape, fixed),
             pl.BlockSpec(gen_out.shape, fixed),
             pl.BlockSpec((block, width), row),
-            pl.BlockSpec((block, nxt), row),
+            pl.BlockSpec((nxt, block), lambda i: (0, i)),
         ],
         out_specs=[
             pl.BlockSpec((block, width), row),
-            pl.BlockSpec((block, nxt), row),
+            pl.BlockSpec((nxt, block), lambda i: (0, i)),
             pl.BlockSpec((block, width), row),
             pl.BlockSpec((size, block, width // size), lambda i: (0, i, 0)),
             pl.BlockSpec((1, width), fixed),
             pl.BlockSpec((units, width), fixed),
-            pl.BlockSpec((units, nxt), fixed),
+            pl.BlockSpec((units, 128), fixed),
         ],
         out_shape=[
             jax.ShapeDtypeStruct((tokens, width), BF16),
-            jax.ShapeDtypeStruct((tokens, nxt), F32),
+            jax.ShapeDtypeStruct((nxt, tokens), F32),
             jax.ShapeDtypeStruct((tokens, width), F32),
             jax.ShapeDtypeStruct((size, tokens, width // size), BF16),
             jax.ShapeDtypeStruct((1, width), F32),
             jax.ShapeDtypeStruct((units, width), F32),
-            jax.ShapeDtypeStruct((units, nxt), F32),
+            jax.ShapeDtypeStruct((units, 128), F32),
         ],
         cost_estimate=pl.CostEstimate(
             flops=tokens * width * 300, bytes_accessed=tokens * width * 16, transcendentals=0
         ),
-        compiler_params=pltpu.CompilerParams(vmem_limit_bytes=48 * MIB),
+        compiler_params=pltpu.CompilerParams(vmem_limit_bytes=62 * MIB),
         name="gen_stage",
     )(streams, branch, gains, gen_in, gen_out, out_grad, next_grad)
 
@@ -152,23 +142,28 @@
 
 def back_kernel(
     size,
-    normed,
-    hidden_grad,
-    qkv_low,
     stats,
     mix,
     gains,
+    normed_in,
+    hidden_grad_in,
+    qkv_low_in,
     parts_in,
     history,
     streams,
     out_total,
-    grad_up,
-    grad_query,
-    grad_key,
-    grad_value,
-    history_grad,
     mix_grad,
     gain_sum,
+    grad_up_out,
+    grad_query_out,
+    grad_key_out,
+    grad_value_out,
+    stream_grad,
+    normed,
+    hidden_grad,
+    qkv_low,
+    grad_up,
+    grad_qkv,
     gain_grad,
     gain_sent,
     gain_got,
@@ -180,8 +175,11 @@
     state_in,
     stream_in,
     total_in,
-    state_out,
+    grad_out,
     held,
+    flipped,
+    in_sem,
+    out_sem,
     ring_send,
     ring_recv,
     core_send,
@@ -214,6 +212,17 @@
     twin = chip * 2 + 1 - core
     across = (1 - chip) * 2 + core
 
+    loads = [
+        pltpu.make_async_copy(hidden_grad_in, hidden_grad, in_sem.at[4]),
+        pltpu.make_async_copy(normed_in.at[3], normed.at[3], in_sem.at[3]),
+        pltpu.make_async_copy(qkv_low_in, qkv_low, in_sem.at[5]),
+    ] + [
+        pltpu.make_async_copy(normed_in.at[stream], normed.at[stream], in_sem.at[stream])
+        for stream in range(3)
+    ]
+    for copy in loads:
+        copy.start()
+
     barrier = pltpu.get_barrier_semaphore()
     steps = size.bit_length() - 1
     partners = [me + (1 << step) * (1 - 2 * lax.rem(lax.div(me, 1 << step), 2)) for step in range(steps)]
@@ -237,12 +246,18 @@
         starts.append(offset)
         offset += cols
 
-    def term(distance, piece):
+    def flip(way, distance, some=(0, 1, 2, 3)):
         owner = index_at(place + distance, size)
+        for stream in some:
+            flipped[way, stream] = normed[stream, owner].T
+
+    def term(way, piece, rows):
         which, at, cols = pieces[piece]
-        if which == 0:
-            return dot(normed[3, owner], hidden_grad[:, at : at + cols], ((0,), (0,)))
-        return dot(normed[which - 1, owner], qkv_low[:, at : at + cols], ((0,), (0,)))
+        stream = 3 if which == 0 else which - 1
+        other = hidden_grad if which == 0 else qkv_low
+        return jnp.dot(
+            flipped[way, stream, rows, :], other[:, at : at + cols], preferred_element_type=F32
+        )
 
     def send(hop, way, piece):
         cols = pl.ds(starts[piece], pieces[piece][2])
@@ -262,9 +277,20 @@
             device_id_type=MESH,
         )
 
+    for copy in loads[:2]:
+        copy.wait()
+    flip(0, half, (3,))
     for piece in range(len(pieces)):
+        if pieces[piece][0] == 1:
+            for copy in loads[2:]:
+                copy.wait()
+            flip(0, half, (0, 1, 2))
         cols = pl.ds(starts[piece], pieces[piece][2])
-        far[:, cols] = term(half, piece).astype(BF16)
+
+        def far_rows(rows):
+            far[rows, cols] = term(0, piece, rows).astype(BF16)
+
+        row_loop(0, shard, far_rows)
         for way in range(2):
             send(0, way, piece).start()
         if piece == 0:
@@ -346,94 +372,115 @@
         copy.wait_send()
         copy.wait_recv()
 
-    per_block = 2 * block // UNIT
-    units = tokens // UNIT
-
-    def unit_base(unit):
-        at, inner = divmod(unit, per_block)
-        side, part = divmod(inner, per_block // 2)
-        return side * rows_half + at * block + part * UNIT
-
-    def unit_loads(unit):
-        rows = pl.ds(unit_base(unit), UNIT)
-        slot = unit % 2
+    def grad_copy(piece):
+        which, at, count = pieces[piece]
+        if which == 0:
+            source = grad_up.at[:, pl.ds(at, count)]
+            target = grad_up_out.at[:, pl.ds(at, count)]
+        else:
+            source = grad_qkv.at[which - 1]
+            target = (grad_query_out, grad_key_out, grad_value_out)[which - 1]
+        return pltpu.make_async_copy(source, target, out_sem.at[piece])
+
+    def unit_loads(base, slot):
+        rows = pl.ds(pl.multiple_of(base, UNIT), UNIT)
         return (
             pltpu.make_async_copy(history.at[:, rows, :], state_in.at[slot], unit_sem.at[slot, 0]),
             pltpu.make_async_copy(streams.at[:, rows, :], stream_in.at[slot], unit_sem.at[slot, 1]),
             pltpu.make_async_copy(out_total.at[rows, :], total_in.at[slot], unit_sem.at[slot, 2]),
         )
 
-    def unit_store(unit):
-        rows = pl.ds(unit_base(unit), UNIT)
-        slot = unit % 2
-        return pltpu.make_async_copy(state_out.at[slot], history_grad.at[:, rows, :], store_sem.at[slot])
+    def unit_store(base, slot):
+        rows = pl.ds(pl.multiple_of(base, UNIT), UNIT)
+        return pltpu.make_async_copy(grad_out.at[slot], stream_grad.at[:, rows, :], store_sem.at[slot])
+
+    mixes = 2 * blocks
+
+    def task_base(task):
+        at, side = divmod(task, 2)
+        return side * rows_half + at * block
 
     gain_grad[...] = jnp.zeros_like(gain_grad)
-    for copy in unit_loads(0):
+    mix_grad[...] = jnp.zeros_like(mix_grad)
+    for copy in unit_loads(0, 0):
         copy.start()
 
-    def run_unit(unit):
-        slot = unit % 2
-        base = unit_base(unit)
-        if unit + 1 < units:
-            for copy in unit_loads(unit + 1):
-                copy.start()
-        for copy in unit_loads(unit):
-            copy.wait()
-        if unit >= 2:
-            unit_store(unit - 2).wait()
-
-        @pl.loop(0, UNIT // GROUP)
-        def _(step):
-            rows = pl.ds(pl.multiple_of(base + step * GROUP, GROUP), GROUP)
-            inner = pl.ds(pl.multiple_of(step * GROUP, GROUP), GROUP)
-            weights = mix[rows, :]
+    def mix_task(task):
+        first = task_base(task)
+
+        @pl.loop(0, 2)
+        def _(slot):
+            @pl.when(slot == 0)
+            def _():
+                for copy in unit_loads(first + UNIT, 1):
+                    copy.start()
+
+            if task + 1 < mixes:
+
+                @pl.when(slot == 1)
+                def _():
+                    for copy in unit_loads(task_base(task + 1), 0):
+                        copy.start()
+
+            for copy in unit_loads(first + slot * UNIT, slot):
+                copy.wait()
+            if task > 0:
+                unit_store(task_base(task - 1) + slot * UNIT, slot).wait()
+
+            @pl.loop(0, UNIT // GROUP)
+            def _(step):
+                mix_group(first + slot * UNIT + step * GROUP, slot, step * GROUP)
+
+            unit_store(first + slot * UNIT, slot).start()
+
+    def mix_group(base, slot, inner_base):
+        rows = pl.ds(pl.multiple_of(base, GROUP), GROUP)
+        inner = pl.ds(pl.multiple_of(inner_base, GROUP), GROUP)
+        zero = jnp.zeros((GROUP, 128), F32)
+        chunks = width // CHUNK
+
+        def window(at):
+            return pl.ds(at * CHUNK, CHUNK)
+
+        def lanes(total, value):
+            for at_lane in range(0, CHUNK, 128):
+                total = total + value[:, at_lane : at_lane + 128]
+            return total
+
+        for stream in range(4):
+            mean = stats[rows, stream : stream + 1]
+            scale = stats[rows, 4 + stream : 5 + stream]
+            sum_e, sum_ex = zero, zero
+            for at in range(chunks):
+                cols = window(at)
+                unit_x = (stream_in[slot, stream, inner, cols] - mean) * scale
+                upstream = parts[stream, rows, cols].astype(F32)
+                e = upstream * gains[stream : stream + 1, cols]
+                gain = upstream * unit_x
+                gain_grad[stream, :, cols] += gain[:8] + gain[8:]
+                sum_e = lanes(sum_e, e)
+                sum_ex = lanes(sum_ex, e * unit_x)
+            mean_e = jnp.sum(sum_e, axis=1, keepdims=True) * inverse
+            mean_ex = jnp.sum(sum_ex, axis=1, keepdims=True) * inverse
+            for at in range(chunks):
+                cols = window(at)
+                unit_x = (stream_in[slot, stream, inner, cols] - mean) * scale
+                e = parts[stream, rows, cols].astype(F32) * gains[stream : stream + 1, cols]
+                grad = scale * (e - mean_e - unit_x * mean_ex)
+                if stream == 3:
+                    grad = grad + total_in[slot, inner, cols]
+                held[stream, :, cols] = grad
+                grad_out[slot, stream, inner, cols] = grad.astype(BF16)
+        for source in range(states):
+            sums = [zero] * 4
+            for at in range(chunks):
+                cols = window(at)
+                state = state_in[slot, source, inner, cols].astype(F32)
+                for stream in range(4):
+                    sums[stream] = lanes(sums[stream], state * held[stream, :, cols])
             for stream in range(4):
-                mean = stats[rows, stream : stream + 1]
-                scale = stats[rows, 4 + stream : 5 + stream]
-                sum_e = jnp.zeros((GROUP, 128), F32)
-                sum_ex = jnp.zeros((GROUP, 128), F32)
-                for at in range(0, width, CHUNK):
-                    cols = pl.ds(at, CHUNK)
-                    unit_x = (stream_in[slot, stream, inner, cols] - mean) * scale
-                    upstream = parts[stream, rows, cols].astype(F32)
-                    e = upstream * gains[stream : stream + 1, cols]
-                    gain = upstream * unit_x
-                    gain_grad[stream, :, cols] += gain[:8] + gain[8:]
-                    ex = e * unit_x
-                    for lane_at in range(0, CHUNK, 128):
-                        sum_e = sum_e + e[:, lane_at : lane_at + 128]
-                        sum_ex = sum_ex + ex[:, lane_at : lane_at + 128]
-                mean_e = jnp.sum(sum_e, axis=1, keepdims=True) * inverse
-                mean_ex = jnp.sum(sum_ex, axis=1, keepdims=True) * inverse
-                for at in range(0, width, CHUNK):
-                    cols = pl.ds(at, CHUNK)
-                    unit_x = (stream_in[slot, stream, inner, cols] - mean) * scale
-                    e = parts[stream, rows, cols].astype(F32) * gains[stream : stream + 1, cols]
-                    grad = scale * (e - mean_e - unit_x * mean_ex)
-                    if stream == 3:
-                        grad = grad + total_in[slot, inner, cols]
-                    held[stream, :, cols] = grad
-            for source in range(states):
-                sums = [jnp.zeros((GROUP, 128), F32) for _ in range(4)]
-                for at in range(0, width, CHUNK):
-                    cols = pl.ds(at, CHUNK)
-                    state = state_in[slot, source, inner, cols].astype(F32)
-                    total = None
-                    for stream in range(4):
-                        k = stream * states + source
-                        grad = held[stream, :, cols]
-                        piece = weights[:, k : k + 1] * grad
-                        total = piece if total is None else total + piece
-                        product = state * grad
-                        for lane_at in range(0, CHUNK, 128):
-                            sums[stream] = sums[stream] + product[:, lane_at : lane_at + 128]
-                    state_out[slot, source, inner, cols] = total.astype(BF16)
-                for stream in range(4):
-                    k = stream * states + source
-                    mix_grad[rows, k : k + 1] = jnp.sum(sums[stream], axis=1, keepdims=True)
-
-        unit_store(unit).start()
+                k = stream * states + source
+                mix_grad[rows, k : k + 1] = jnp.sum(sums[stream], axis=1, keepdims=True)
 
     def gain_copy(step):
         return pltpu.make_async_remote_copy(
@@ -466,13 +513,17 @@
         tasks.append((0.02 + 0.03 * at, to_link, at))
         tasks.append((0.19 + 0.16 * at, to_twin, at))
         tasks.append((0.23 + 0.16 * at, ready, at))
-        for inner in range(per_block):
-            tasks.append((0.24 + 0.16 * at + 0.035 * inner, run_unit, at * per_block + inner))
+        for side in range(2):
+            tasks.append((0.24 + 0.16 * at + 0.07 * side, mix_task, 2 * at + side))
     for step in range(steps + 1):
         tasks.append((0.87 + 0.12 * step / steps, gain_step, step))
     tasks.sort(key=lambda item: item[0])
-    first_part = 0.5 / (half - 0.5)
     for hop in range(1, half + 1):
+        if hop == half:
+            flip(0, 0)
+        else:
+            for way in range(2):
+                flip(way, (half - hop) * (1 - 2 * way))
         for piece in range(len(pieces)):
             passed = ((hop - 1.5 if hop > 1 else 0.0) + (piece + 1) / len(pieces) * (1 if hop > 1 else 0.5)) / (half - 0.5)
             cols = pl.ds(starts[piece], pieces[piece][2])
@@ -480,38 +531,45 @@
                 send(hop - 1, way, piece).wait_recv()
                 if hop == half:
                     continue
-                distance = (half - hop) * (1 - 2 * way)
+
+                def with_got(rows):
+                    got = ring[hop - 1, way, rows, cols].astype(F32)
+                    ring[hop - 1, way, rows, cols] = (term(way, piece, rows) + got).astype(BF16)
+
+                def alone(rows):
+                    ring[hop - 1, way, rows, cols] = term(way, piece, rows).astype(BF16)
+
                 if hop == 1:
-                    with_rows = pl.ds(way * cut, cut)
-                    only_rows = pl.ds((1 - way) * cut, cut)
-                    full = term(distance, piece)
-                    got = ring[0, way, with_rows, cols].astype(F32)
-                    ring[0, way, with_rows, cols] = (full[way * cut : way * cut + cut] + got).astype(BF16)
-                    ring[0, way, only_rows, cols] = full[
-                        (1 - way) * cut : (1 - way) * cut + cut
-                    ].astype(BF16)
+                    row_loop(way * cut, cut, with_got)
+                    row_loop((1 - way) * cut, cut, alone)
                 else:
-                    got = ring[hop - 1, way, :, cols].astype(F32)
-                    ring[hop - 1, way, :, cols] = (term(distance, piece) + got).astype(BF16)
+                    row_loop(0, shard, with_got)
                 send(hop, way, piece).start()
             if hop == half:
-                total = (
-                    term(0, piece)
-                    + ring[hop - 1, 0, :, cols].astype(F32)
-                    + ring[hop - 1, 1, :, cols].astype(F32)
-                )
-                which, at, count = pieces[piece]
-                if which == 0:
-                    grad_up[:, at : at + count] = total
-                else:
-                    (grad_query, grad_key, grad_value)[which - 1][...] = total
+
+                def finish(rows):
+                    total = (
+                        term(0, piece, rows)
+                        + ring[hop - 1, 0, rows, cols].astype(F32)
+                        + ring[hop - 1, 1, rows, cols].astype(F32)
+                    )
+                    which, at, count = pieces[piece]
+                    if which == 0:
+                        grad_up[rows, at : at + count] = total
+                    else:
+                        grad_qkv[which - 1, rows, :] = total
+
+                row_loop(0, shard, finish)
+                grad_copy(piece).start()
             while tasks and tasks[0][0] <= passed:
                 _, run, value = tasks.pop(0)
                 run(value)
     for _, run, value in tasks:
         run(value)
-    for unit in range(max(units - 2, 0), units):
-        unit_store(unit).wait()
+    for piece in range(len(pieces)):
+        grad_copy(piece).wait()
+    for slot in range(2):
+        unit_store(task_base(mixes - 1) + slot * UNIT, slot).wait()
     for step in range(steps):
         gain_copy(step).wait_send()
     for hop in range(half):
@@ -536,18 +594,23 @@
     small = jax.ShapeDtypeStruct((shard, local), F32)
     return pl.pallas_call(
         lambda *refs: back_kernel(size, *refs),
-        in_specs=[vmem] * 6 + [hbm] * 4,
-        out_specs=[vmem] * 4 + [hbm, vmem, vmem],
+        in_specs=[vmem] * 3 + [hbm] * 7,
+        out_specs=[vmem] * 2 + [hbm] * 5,
         out_shape=[
+            jax.ShapeDtypeStruct((tokens, mix.shape[1]), F32),
+            jax.ShapeDtypeStruct((4, width), F32),
             jax.ShapeDtypeStruct((shard, hidden), F32),
             small,
             small,
             small,
-            jax.ShapeDtypeStruct((states, tokens, width), BF16),
-            jax.ShapeDtypeStruct((tokens, mix.shape[1]), F32),
-            jax.ShapeDtypeStruct((4, width), F32),
+            jax.ShapeDtypeStruct((4, tokens, width), BF16),
         ],
         scratch_shapes=[
+            pltpu.VMEM(normed.shape, BF16),
+            pltpu.VMEM((tokens, hidden), BF16),
+            pltpu.VMEM((tokens, 3 * local), BF16),
+            pltpu.VMEM((shard, hidden), F32),
+            pltpu.VMEM((3, shard, local), F32),
             pltpu.VMEM((4, 8, width), F32),
             pltpu.VMEM((steps, 4, width), F32),
             pltpu.VMEM((steps, 4, width), F32),
@@ -559,8 +622,11 @@
             pltpu.VMEM((2, states, UNIT, width), BF16),
             pltpu.VMEM((2, 4, UNIT, width), F32),
             pltpu.VMEM((2, UNIT, width), F32),
-            pltpu.VMEM((2, states, UNIT, width), BF16),
+            pltpu.VMEM((2, 4, UNIT, width), BF16),
             pltpu.VMEM((4, GROUP, width), F32),
+            pltpu.VMEM((2, 4, shard, tokens), BF16),
+            dma((6,)),
+            dma((count,)),
             dma((half, 2, count)),
             dma((half, 2, count)),
             dma((blocks,)),
@@ -583,7 +649,7 @@
             collective_id=1, has_side_effects=True, vmem_limit_bytes=62 * MIB
         ),
         name="back_stage",
-    )(normed, hidden_grad, qkv_low, stats, mix, gains, parts, history, streams, out_total)
+    )(stats, mix, gains, normed, hidden_grad, qkv_low, parts, history, streams, out_total)
 
 
 TILE = 512
@@ -597,39 +663,54 @@
     )
 
 
-def attention_probs(query, key, seg_col, seg_row):
-    tokens = query.shape[0]
+def row_loop(base, count, run, step=128):
+    step = min(step, count)
+
+    @pl.loop(0, count // step)
+    def _(at):
+        run(pl.ds(pl.multiple_of(base + at * step, step), step))
+
+
+def attention_probs(query, key, two, first):
+    shape = (query.shape[0], key.shape[0])
+    middle = key.shape[0] // 2
     scores = dot(query, key, ((1,), (1,))) * (HEAD_DIM ** (-0.5))
-    later = lax.broadcasted_iota(jnp.int32, (tokens, tokens), 1) > lax.broadcasted_iota(
-        jnp.int32, (tokens, tokens), 0
-    )
-    scores = jnp.where(jnp.logical_or(seg_col != seg_row, later), -1e30, scores)
+    row = first + lax.broadcasted_iota(jnp.int32, shape, 0)
+    col = lax.broadcasted_iota(jnp.int32, shape, 1)
+    apart = jnp.where(row >= middle, jnp.where(col < middle, two, 0), 0)
+    scores = jnp.where(jnp.logical_or(apart != 0, col > row), -1e30, scores)
     weights = jnp.exp(scores - jnp.max(scores, axis=1, keepdims=True))
     return weights / jnp.sum(weights, axis=1, keepdims=True)
 
 
 def mid_kernel(
     size,
+    turn,
+    two,
+    gen_grad,
+    gen_gain,
+    gen_mid,
+    low_t_in,
+    grad_blocks_in,
+    hidden_in,
+    heads_in,
+    low_all,
+    up_full,
+    qkv_full,
+    gen_sum,
+    mid_sum,
+    grad_out,
+    grad_down,
+    hidden_grad_out,
+    qkv_low_out,
+    parts,
     low_t,
     grad_blocks,
     hidden,
     heads,
-    turn,
-    seg_col,
-    seg_row,
-    gen_grad,
-    gen_gain,
-    gen_mid,
-    low_all,
-    up_full,
-    qkv_full,
-    grad_out,
-    grad_down,
+    low_sum,
     hidden_grad,
     qkv_low,
-    parts,
-    gen_sum,
-    mid_sum,
     attended_grad,
     far,
     ring,
@@ -641,6 +722,10 @@
     gen_got,
     mid_sent,
     mid_got,
+    value_sum,
+    key_sum,
+    in_sem,
+    out_sem,
     ring_send,
     ring_recv,
     tile_sem,
@@ -659,6 +744,14 @@
     left = index_at(place - 1, size)
     steps = size.bit_length() - 1
     partners = [me + (1 << step) * (1 - 2 * lax.rem(lax.div(me, 1 << step), 2)) for step in range(steps)]
+    loads = [
+        pltpu.make_async_copy(source, target, in_sem.at[at])
+        for at, (source, target) in enumerate(
+            ((low_t_in, low_t), (grad_blocks_in, grad_blocks), (hidden_in, hidden), (heads_in, heads))
+        )
+    ]
+    for copy in loads:
+        copy.start()
     barrier = pltpu.get_barrier_semaphore()
     for there in [right, left] + partners:
         pl.semaphore_signal(barrier, inc=1, device_id=(there, lane), device_id_type=MESH)
@@ -687,11 +780,8 @@
     pieces = rows_all // TILE
     cut = TILE // 2
 
-    def term(distance, piece):
-        owner = index_at(place + distance, size)
-        return jnp.dot(
-            low_t[pl.ds(piece * TILE, TILE), :], grad_blocks[owner], preferred_element_type=F32
-        )
+    def term(owner, rows):
+        return jnp.dot(low_t[rows, :], grad_blocks[owner], preferred_element_type=F32)
 
     def send(hop, way, piece):
         if hop == 0:
@@ -709,43 +799,83 @@
             device_id_type=MESH,
         )
 
+    for copy in loads[:2]:
+        copy.wait()
     for piece in range(pieces):
-        far[pl.ds(piece * TILE, TILE), :] = term(half, piece).astype(BF16)
+
+        def far_rows(rows):
+            far[rows, :] = term(index_at(place + half, size), rows).astype(BF16)
+
+        row_loop(piece * TILE, TILE, far_rows)
         for way in range(2):
             send(0, way, piece).start()
+
+    for copy in loads[2:]:
+        copy.wait()
+
+    def grad_copy(piece):
+        base = piece * TILE
+        source = low_sum.at[pl.ds(base, TILE), :]
+        if base < local:
+            target = grad_out.at[pl.ds(base, TILE), :]
+        else:
+            target = grad_down.at[pl.ds(base - local, TILE), :]
+        return pltpu.make_async_copy(source, target, out_sem.at[2 + piece])
+
+    def hidden_copy():
+        return pltpu.make_async_copy(hidden_grad, hidden_grad_out, out_sem.at[0])
+
+    def qkv_copy():
+        return pltpu.make_async_copy(qkv_low, qkv_low_out, out_sem.at[1])
 
     def low_grad(at):
         index = at
         load(index + 1).start()
         load(index).wait()
-        total = None
-        for owner in range(size):
-            part = dot(grad_blocks[owner], low_tile[at % 2, owner], ((1,), (1,)))
-            total = part if total is None else total + part
         base = at * TILE
-        if base < local:
-            attended_grad[:, base : base + TILE] = total.astype(BF16)
-        else:
-            cols = slice(base - local, base - local + TILE)
-            hidden_grad[:, cols] = (total * gelu_slope(hidden[:, cols])).astype(BF16)
+
+        def run(rows):
+            total = None
+            for owner in range(size):
+                part = dot(grad_blocks[owner, rows, :], low_tile[at % 2, owner], ((1,), (1,)))
+                total = part if total is None else total + part
+            if base < local:
+                attended_grad[rows, base : base + TILE] = total.astype(BF16)
+            else:
+                cols = slice(base - local, base - local + TILE)
+                hidden_grad[rows, cols] = (total * gelu_slope(hidden[rows, cols])).astype(BF16)
+
+        row_loop(0, tokens, run, 256)
+        if at + 1 == low_tiles:
+            hidden_copy().start()
 
     def head_grad(head):
         cols = slice(head * HEAD_DIM, (head + 1) * HEAD_DIM)
         key_cols = slice(local + head * HEAD_DIM, local + (head + 1) * HEAD_DIM)
         value_cols = slice(2 * local + head * HEAD_DIM, 2 * local + (head + 1) * HEAD_DIM)
-        query, key, value = heads[:, cols], heads[:, key_cols], heads[:, value_cols]
-        upstream = attended_grad[:, cols]
-        probs = attention_probs(query, key, seg_col[...], seg_row[...])
-        probs_grad = dot(upstream, value, ((1,), (1,)))
-        qkv_low[:, value_cols] = dot(probs.astype(BF16), upstream, ((0,), (0,))).astype(BF16)
-        row = jnp.sum(probs * probs_grad, axis=1, keepdims=True)
-        scores_grad = (probs * (probs_grad - row)).astype(BF16)
         scale = HEAD_DIM ** (-0.5)
+        value_sum[...] = jnp.zeros_like(value_sum)
+        key_sum[...] = jnp.zeros_like(key_sum)
+
+        def run(rows):
+            query, key, value = heads[rows, cols], heads[:, key_cols], heads[:, value_cols]
+            upstream = attended_grad[rows, cols]
+            probs = attention_probs(query, key, two[...], rows.start)
+            probs_grad = dot(upstream, value, ((1,), (1,)))
+            value_sum[...] += dot(probs.astype(BF16), upstream, ((0,), (0,)))
+            row = jnp.sum(probs * probs_grad, axis=1, keepdims=True)
+            scores_grad = (probs * (probs_grad - row)).astype(BF16)
+            query_grad = dot(scores_grad, key, ((1,), (0,))) * scale
+            turns = [turn[which, rows, :] for which in range(3)]
+            qkv_low[rows, cols] = unrotate(query_grad, turns).astype(BF16)
+            key_sum[...] += dot(scores_grad, query, ((0,), (0,)))
+
+        row_loop(0, tokens, run)
         turns = [turn[which] for which in range(3)]
-        query_grad = dot(scores_grad, key, ((1,), (0,))) * scale
-        qkv_low[:, cols] = unrotate(query_grad, turns).astype(BF16)
-        key_grad = dot(scores_grad, query, ((0,), (0,))) * scale
-        qkv_low[:, key_cols] = unrotate(key_grad, turns).astype(BF16)
+        qkv_low[:, value_cols] = value_sum[...].astype(BF16)
+        qkv_low[:, key_cols] = unrotate(key_sum[...] * scale, turns).astype(BF16)
+        if (head + 1) * HEAD_DIM == local:
+            qkv_copy().start()
 
     def part_store(stream, at):
         return pltpu.make_async_copy(
@@ -758,7 +888,11 @@
         load(index).wait()
         if at:
             part_store(3, at - 1).wait()
-        stage[3] = dot(hidden_grad[...], up_tile[at % 2], ((1,), (1,))).astype(BF16)
+
+        def run(rows):
+            stage[3, rows, :] = dot(hidden_grad[rows, :], up_tile[at % 2], ((1,), (1,))).astype(BF16)
+
+        row_loop(0, tokens, run, 256)
         part_store(3, at).start()
 
     def qkv_part(at):
@@ -769,8 +903,16 @@
         for stream in range(3):
             if at:
                 part_store(stream, at - 1).wait()
-            cols = slice(stream * local, (stream + 1) * local)
-            stage[stream] = dot(qkv_low[:, cols], qkv_tile[at % 2, :, cols], ((1,), (1,))).astype(BF16)
+
+        def run(rows):
+            for stream in range(3):
+                cols = slice(stream * local, (stream + 1) * local)
+                stage[stream, rows, :] = dot(
+                    qkv_low[rows, cols], qkv_tile[at % 2, :, cols], ((1,), (1,))
+                ).astype(BF16)
+
+        row_loop(0, tokens, run, 256)
+        for stream in range(3):
             part_store(stream, at).start()
 
     def gen_copies(step):
@@ -820,39 +962,46 @@
     slot = 0
     for hop in range(1, half + 1):
         for piece in range(pieces):
-            rows = pl.ds(piece * TILE, TILE)
             for way in range(2):
                 send(hop - 1, way, piece).wait_recv()
                 if hop == half:
                     continue
-                full = term((half - hop) * (1 - 2 * way), piece)
+                owner = index_at(place + (half - hop) * (1 - 2 * way), size)
+
+                def with_got(rows):
+                    got = ring[hop - 1, way, rows, :].astype(F32)
+                    ring[hop - 1, way, rows, :] = (term(owner, rows) + got).astype(BF16)
+
+                def alone(rows):
+                    ring[hop - 1, way, rows, :] = term(owner, rows).astype(BF16)
+
                 if hop == 1:
-                    with_rows = pl.ds(piece * TILE + way * cut, cut)
-                    only_rows = pl.ds(piece * TILE + (1 - way) * cut, cut)
-                    got = ring[0, way, with_rows, :].astype(F32)
-                    ring[0, way, with_rows, :] = (full[way * cut : way * cut + cut] + got).astype(BF16)
-                    ring[0, way, only_rows, :] = full[(1 - way) * cut : (1 - way) * cut + cut].astype(BF16)
+                    row_loop(piece * TILE + way * cut, cut, with_got)
+                    row_loop(piece * TILE + (1 - way) * cut, cut, alone)
                 else:
-                    got = ring[hop - 1, way, rows, :].astype(F32)
-                    ring[hop - 1, way, rows, :] = (full + got).astype(BF16)
+                    row_loop(piece * TILE, TILE, with_got)
                 send(hop, way, piece).start()
             if hop == half:
-                total = (
-                    term(0, piece)
-                    + ring[hop - 1, 0, rows, :].astype(F32)
-                    + ring[hop - 1, 1, rows, :].astype(F32)
-                )
-                base = piece * TILE
-                if base < local:
-                    grad_out[base : base + TILE, :] = total
-                else:
-                    grad_down[base - local : base - local + TILE, :] = total
+
+                def finish(rows):
+                    low_sum[rows, :] = (
+                        term(me, rows)
+                        + ring[hop - 1, 0, rows, :].astype(F32)
+                        + ring[hop - 1, 1, rows, :].astype(F32)
+                    )
+
+                row_loop(piece * TILE, TILE, finish)
+                grad_copy(piece).start()
             slot += 1
             while tasks and (slot == slots or len(tasks) * (slots - 2) > count * max(slots - 2 - slot, 0)):
                 run, value = tasks.pop(0)
                 run(value)
     for stream in range(4):
         part_store(stream, width_tiles - 1).wait()
+    hidden_copy().wait()
+    qkv_copy().wait()
+    for piece in range(pieces):
+        grad_copy(piece).wait()
     for step in range(steps):
         for copy in gen_copies(step):
             copy.wait_send()
@@ -869,8 +1018,7 @@
     hidden,
     heads,
     turn,
-    seg_col,
-    seg_row,
+    two,
     gen_grad,
     gen_gain,
     gen_mid,
@@ -892,18 +1040,25 @@
     dma = pltpu.SemaphoreType.DMA
     return pl.pallas_call(
         lambda *refs: mid_kernel(size, *refs),
-        in_specs=[vmem] * 10 + [hbm] * 3,
-        out_specs=[vmem] * 4 + [hbm, vmem, vmem],
+        in_specs=[vmem] * 5 + [hbm] * 7,
+        out_specs=[vmem] * 2 + [hbm] * 5,
         out_shape=[
+            jax.ShapeDtypeStruct((units + 8, width), F32),
+            jax.ShapeDtypeStruct(gen_mid.shape, F32),
             jax.ShapeDtypeStruct((local, shard), F32),
             jax.ShapeDtypeStruct((hidden_cols, shard), F32),
             jax.ShapeDtypeStruct((tokens, hidden_cols), BF16),
             jax.ShapeDtypeStruct((tokens, 3 * local), BF16),
             jax.ShapeDtypeStruct((4, tokens, width), BF16),
-            jax.ShapeDtypeStruct((units + 8, width), F32),
-            jax.ShapeDtypeStruct(gen_mid.shape, F32),
         ],
         scratch_shapes=[
+            pltpu.VMEM((rows_all, tokens), BF16),
+            pltpu.VMEM((size, tokens, shard), BF16),
+            pltpu.VMEM((tokens, hidden_cols), F32),
+            pltpu.VMEM((tokens, 3 * local), BF16),
+            pltpu.VMEM((rows_all, shard), F32),
+            pltpu.VMEM((tokens, hidden_cols), BF16),
+            pltpu.VMEM((tokens, 3 * local), BF16),
             pltpu.VMEM((tokens, local), BF16),
             pltpu.VMEM((rows_all, shard), BF16),
             pltpu.VMEM((half, 2, rows_all, shard), BF16),
@@ -915,6 +1070,10 @@
             pltpu.VMEM((steps, units + 8, width), BF16),
             pltpu.VMEM((steps,) + gen_mid.shape, F32),
             pltpu.VMEM((steps,) + gen_mid.shape, F32),
+            pltpu.VMEM((tokens, HEAD_DIM), F32),
+            pltpu.VMEM((tokens, HEAD_DIM), F32),
+            dma((4,)),
+            dma((2 + pieces,)),
             dma((half, 2, pieces)),
             dma((half, 2, pieces)),
             dma((3, 2)),
@@ -930,16 +1089,15 @@
         ),
         name="mid_stage",
     )(
+        turn,
+        two,
+        gen_grad,
+        gen_gain,
+        gen_mid,
         low_t,
         grad_blocks,
         hidden,
         heads,
-        turn,
-        seg_col,
-        seg_row,
-        gen_grad,
-        gen_gain,
-        gen_mid,
         low_all,
         up_full,
         qkv_full,
@@ -948,11 +1106,10 @@
 
 def front_kernel(
     size,
-    mix,
+    mix_in,
     gains,
-    turn,
-    seg_col,
-    seg_row,
+    segments,
+    frequency,
     history,
     w_query,
     w_key,
@@ -961,15 +1118,21 @@
     w_out,
     w_down,
     stats,
-    heads,
-    hidden,
-    low_t,
     branch,
+    mix,
+    turn,
+    two,
+    heads_out,
+    hidden_out,
+    low_t_out,
     normed_out,
     streams,
     qkv_all,
     up_all,
     low_all,
+    heads,
+    hidden,
+    low_t,
     normed,
     low,
     weight_tile,
@@ -988,6 +1151,7 @@
     state_sem,
     stream_sem,
     normed_sem,
+    out_sem,
     weight_sem,
     tile_sem,
     core_send,
@@ -1074,21 +1238,59 @@
     units = tokens // UNIT
 
     def state_load(unit):
-        return pltpu.make_async_copy(
-            history.at[:, pl.ds(unit * UNIT, UNIT), :], state_in.at[unit % 2], state_sem.at[unit % 2]
-        )
+        rows = pl.ds(pl.multiple_of(unit * UNIT, UNIT), UNIT)
+        slot = lax.rem(unit, 2)
+        return pltpu.make_async_copy(history.at[:, rows, :], state_in.at[slot], state_sem.at[slot])
 
     def stream_store(unit):
-        return pltpu.make_async_copy(
-            stream_out.at[unit % 2], streams.at[:, pl.ds(unit * UNIT, UNIT), :], stream_sem.at[unit % 2]
-        )
-
-    def mix_unit(unit):
-        slot = unit % 2
-        if unit + 1 < units:
+        rows = pl.ds(pl.multiple_of(unit * UNIT, UNIT), UNIT)
+        slot = lax.rem(unit, 2)
+        return pltpu.make_async_copy(stream_out.at[slot], streams.at[:, rows, :], stream_sem.at[slot])
+
+    per_task = 2
+
+    def tables():
+        count = mix_in.shape[0]
+        padded = -(-count // 8) * 8
+        mix[...] = jnp.concatenate(
+            [mix_in[...], jnp.zeros((padded - count, tokens), F32)], axis=0
+        ).T
+        two[...] = jnp.broadcast_to(segments[0:1, tokens - 1 : tokens], (1, tokens))
+        row = lax.broadcasted_iota(jnp.int32, (tokens, HEAD_DIM), 0)
+        lanes = lax.broadcasted_iota(jnp.int32, (tokens, HEAD_DIM), 1)
+        flag = jnp.broadcast_to(segments[0:1, tokens - 1 : tokens], (tokens, HEAD_DIM))
+        place_in = row - jnp.where(row >= tokens // 2, jnp.where(flag != 0, tokens // 2, 0), 0)
+        angles = place_in.astype(F32) * frequency[...]
+        sine = jnp.sin(angles)
+        turn[0] = jnp.cos(angles)
+        turn[1] = jnp.where(lanes < ROT // 2, sine, 0.0)
+        turn[2] = jnp.where(lanes < ROT // 2, 0.0, -sine)
+
+    def out_copies():
+        return [
+            pltpu.make_async_copy(source, target, out_sem.at[at])
+            for at, (source, target) in enumerate(
+                ((heads, heads_out), (hidden, hidden_out), (low_t, low_t_out))
+            )
+        ]
+
+    def mix_task(task):
+        @pl.loop(0, per_task)
+        def _(which):
+            mix_unit(task * per_task + which, task)
+
+        if (task + 1) * per_task == units:
+            normed_store().start()
+
+    def mix_unit(unit, task):
+        slot = lax.rem(unit, 2)
+
+        @pl.when(unit + 1 < units)
+        def _():
             state_load(unit + 1).start()
+
         state_load(unit).wait()
-        if unit >= 2:
+        if task > 0:
             stream_store(unit - 2).wait()
 
         @pl.loop(0, UNIT // GROUP)
@@ -1096,6 +1298,7 @@
             rows = pl.ds(pl.multiple_of(unit * UNIT + step * GROUP, GROUP), GROUP)
             inner = pl.ds(pl.multiple_of(step * GROUP, GROUP), GROUP)
             weights = mix[rows, :]
+
             sums = [jnp.zeros((GROUP, 128), F32) for _ in range(4)]
             for at in range(0, width, CHUNK):
                 cols = pl.ds(at, CHUNK)
@@ -1130,8 +1333,6 @@
                         normed[stream, owner, rows, :] = value[:, base : base + shard]
 
         stream_store(unit).start()
-        if unit == units - 1:
-            normed_store().start()
 
     def normed_store():
         return pltpu.make_async_copy(normed, normed_out, normed_sem)
@@ -1152,12 +1353,11 @@
             for way in range(2):
                 send(group, half, way, piece).wait_recv()
 
-    def tile_product(tile, stream):
-        weight_load(tile).wait()
+    def tile_product(tile, stream, rows):
         total = None
         for owner in range(size):
             part = jnp.dot(
-                normed[stream, owner],
+                normed[stream, owner, rows, :],
                 weight_tile[tile % 2, owner * shard : (owner + 1) * shard, :],
                 preferred_element_type=F32,
             )
@@ -1170,27 +1370,36 @@
             weight_load(0).start()
         if which < 2:
             weight_load(which + 1).start()
-        product = tile_product(which, which)
-        for head in range(local // HEAD_DIM):
-            at = head * HEAD_DIM
-            part = product[:, at : at + HEAD_DIM]
-            if which < 2:
-                part = (
-                    part * turn[0]
-                    - pltpu.roll(part, HEAD_DIM - ROT // 2, 1) * turn[1]
-                    - pltpu.roll(part, ROT // 2, 1) * turn[2]
-                )
-            heads[:, which * local + at : which * local + at + HEAD_DIM] = part.astype(BF16)
+        weight_load(which).wait()
+
+        def run(rows):
+            product = tile_product(which, which, rows)
+            for head in range(local // HEAD_DIM):
+                at = head * HEAD_DIM
+                part = product[:, at : at + HEAD_DIM]
+                if which < 2:
+                    part = (
+                        part * turn[0, rows, :]
+                        - pltpu.roll(part, HEAD_DIM - ROT // 2, 1) * turn[1, rows, :]
+                        - pltpu.roll(part, ROT // 2, 1) * turn[2, rows, :]
+                    )
+                heads[rows, which * local + at : which * local + at + HEAD_DIM] = part.astype(BF16)
+
+        row_loop(0, tokens, run)
 
     def head_task(head):
         at = head * HEAD_DIM
-        query = heads[:, at : at + HEAD_DIM]
-        key = heads[:, local + at : local + at + HEAD_DIM]
-        value = heads[:, 2 * local + at : 2 * local + at + HEAD_DIM]
-        probs = attention_probs(query, key, seg_col[...], seg_row[...]).astype(BF16)
-        attended = jnp.dot(probs, value, preferred_element_type=F32)
-        low[:, at : at + HEAD_DIM] = attended.astype(BF16)
-        low_t[at : at + HEAD_DIM, :] = attended.T.astype(BF16)
+
+        def run(rows):
+            query = heads[rows, at : at + HEAD_DIM]
+            key = heads[:, local + at : local + at + HEAD_DIM]
+            value = heads[:, 2 * local + at : 2 * local + at + HEAD_DIM]
+            probs = attention_probs(query, key, two[...], rows.start).astype(BF16)
+            attended = jnp.dot(probs, value, preferred_element_type=F32)
+            low[rows, at : at + HEAD_DIM] = attended.astype(BF16)
+            low_t[at : at + HEAD_DIM, rows] = attended.T.astype(BF16)
+
+        row_loop(0, tokens, run)
 
     def up_task(at):
         if at == 0:
@@ -1198,12 +1407,21 @@
             weight_load(3).start()
         if at + 1 < tiles - 3:
             weight_load(4 + at).start()
-        product = tile_product(3 + at, 3)
+        weight_load(3 + at).wait()
         cols = slice(at * wide, (at + 1) * wide)
-        hidden[:, cols] = product
-        active = gelu(product)
-        low[:, local + at * wide : local + (at + 1) * wide] = active.astype(BF16)
-        low_t[local + at * wide : local + (at + 1) * wide, :] = active.T.astype(BF16)
+        low_cols = slice(local + at * wide, local + (at + 1) * wide)
+
+        def run(rows):
+            product = tile_product(3 + at, 3, rows)
+            hidden[rows, cols] = product
+            active = gelu(product)
+            low[rows, low_cols] = active.astype(BF16)
+            low_t[low_cols, rows] = active.T.astype(BF16)
+
+        row_loop(0, tokens, run)
+        if at + 1 == tiles - 3:
+            for copy in out_copies():
+                copy.start()
 
     distances = [0]
     for hop in range(1, half):
@@ -1259,7 +1477,13 @@
         load = tile_load(index)
         load.start()
         load.wait()
-        branch[owner] = jnp.dot(low[...], low_tile[index % 2], preferred_element_type=F32).astype(BF16)
+
+        def run(rows):
+            branch[owner, rows, :] = jnp.dot(
+                low[rows, :], low_tile[index % 2], preferred_element_type=F32
+            ).astype(BF16)
+
+        row_loop(0, tokens, run)
         core_copy(index).start()
 
     def add_into(index, other):
@@ -1291,9 +1515,9 @@
     first = [0, counts[0] * half, (counts[0] + counts[1]) * half]
     total_slots = sum(counts) * half
     tasks = []
-    span = max(first[1] - 2, 1)
-    for unit in range(units):
-        tasks.append((counts[0] - 1 + unit * (first[1] - counts[0]) / units, mix_unit, unit))
+    mixes = units // per_task
+    for task in range(mixes):
+        tasks.append((counts[0] - 1 + task * (first[1] - counts[0]) / mixes, mix_task, task))
     early = first[1] + counts[1]
     for which in range(3):
         tasks.append((early + which, qkv_task, which))
@@ -1318,8 +1542,9 @@
             for way in range(2):
                 if hop > 1:
                     send(group, hop - 1, way, piece).wait_recv()
-                if hop < half or True:
-                    send(group, hop, way, piece).start()
+                send(group, hop, way, piece).start()
+            if at_slot == 0:
+                tables()
             while tasks and tasks[0][0] <= at_slot and at_slot < total_slots - 1:
                 _, run, value = tasks.pop(0)
                 run(value)
@@ -1340,13 +1565,15 @@
     for unit in range(units - 2, units):
         stream_store(unit).wait()
     normed_store().wait()
+    for copy in out_copies():
+        copy.wait()
     for group, hop in slots:
         for piece in range(counts[group]):
             for way in range(2):
                 send(group, hop, way, piece).wait_send()
 
 
-def front_stage(size, mix, gains, turn, seg_col, seg_row, history, w_query, w_key, w_value, w_up, w_out, w_down):
+def front_stage(size, mix, gains, segments, frequency, history, w_query, w_key, w_value, w_up, w_out, w_down):
     half = size // 2
     states, tokens, width = history.shape
     shard = width // size
@@ -1360,14 +1587,17 @@
     low_pieces = rows_all // TILE
     return pl.pallas_call(
         lambda *refs: front_kernel(size, *refs),
-        in_specs=[vmem] * 5 + [hbm] * 7,
-        out_specs=[vmem] * 5 + [hbm] * 5,
+        in_specs=[vmem] * 4 + [hbm] * 7,
+        out_specs=[vmem] * 5 + [hbm] * 8,
         out_shape=[
             jax.ShapeDtypeStruct((tokens, 8), F32),
+            jax.ShapeDtypeStruct((size, tokens, shard), BF16),
+            jax.ShapeDtypeStruct((tokens, -(-mix.shape[0] // 8) * 8), F32),
+            jax.ShapeDtypeStruct((3, tokens, HEAD_DIM), F32),
+            jax.ShapeDtypeStruct((1, tokens), jnp.int32),
             jax.ShapeDtypeStruct((tokens, 3 * local), BF16),
             jax.ShapeDtypeStruct((tokens, hidden_cols), F32),
             jax.ShapeDtypeStruct((rows_all, tokens), BF16),
-            jax.ShapeDtypeStruct((size, tokens, shard), BF16),
             jax.ShapeDtypeStruct((4, size, tokens, shard), BF16),
             jax.ShapeDtypeStruct((4, tokens, width), F32),
             jax.ShapeDtypeStruct((width, 3 * local), BF16),
@@ -1375,6 +1605,9 @@
             jax.ShapeDtypeStruct((size, rows_all, shard), BF16),
         ],
         scratch_shapes=[
+            pltpu.VMEM((tokens, 3 * local), BF16),
+            pltpu.VMEM((tokens, hidden_cols), F32),
+            pltpu.VMEM((rows_all, tokens), BF16),
             pltpu.VMEM((4, size, tokens, shard), BF16),
             pltpu.VMEM((tokens, rows_all), BF16),
             pltpu.VMEM((2, width, TILE), BF16),
@@ -1393,6 +1626,7 @@
             dma((2,)),
             dma((2,)),
             dma(()),
+            dma((3,)),
             dma((2,)),
             dma((2,)),
             dma((size,)),
@@ -1410,7 +1644,84 @@
             collective_id=3, has_side_effects=True, vmem_limit_bytes=62 * MIB
         ),
         name="front_stage",
-    )(mix, gains, turn, seg_col, seg_row, history, w_query, w_key, w_value, w_up, w_out, w_down)
+    )(mix, gains, segments, frequency, history, w_query, w_key, w_value, w_up, w_out, w_down)
+
+
+def finish_kernel(count, mix, grads, mix_grad, gain_sum, gen_gain, *refs):
+    sources = refs[:count]
+    history_grad, mix_out, gain_out = refs[count : count + 3]
+    targets = refs[count + 3 : 2 * count + 3]
+    spread = refs[2 * count + 3]
+    states, tokens, width = history_grad.shape
+    step = pl.program_id(0)
+    for source, target in zip(sources, targets):
+        target[...] = source[...]
+
+    @pl.when(step == 0)
+    def _():
+        gain_out[:4, :] = gain_sum[...]
+        gain_out[4:5, :] = gen_gain[0:1, :]
+        mix_out[...] = mix_grad[...].T[: mix_out.shape[0], :]
+
+    own = lax.broadcasted_iota(jnp.int32, (tokens, tokens), 0) == lax.broadcasted_iota(
+        jnp.int32, (tokens, tokens), 1
+    )
+    weights = mix[...]
+    for source in range(states):
+        parts = [
+            jnp.where(own, weights[:, stream * states + source : stream * states + source + 1], 0.0)
+            for stream in range(4)
+        ]
+        spread[source * tokens : (source + 1) * tokens, :] = jnp.concatenate(parts, axis=1).astype(BF16)
+
+    @pl.loop(0, width // 512)
+    def _(at):
+        cols = pl.ds(pl.multiple_of(at * 512, 512), 512)
+        grad = jnp.concatenate([grads[stream, :, cols] for stream in range(4)], axis=0)
+        mixed = jnp.dot(spread[...], grad, preferred_element_type=F32)
+        for source in range(states):
+            history_grad[source, :, cols] = mixed[source * tokens : (source + 1) * tokens].astype(BF16)
+
+
+def finish_stage(states, mixes, mix, grads, mix_grad, gain_sum, gen_sum, sources, block=64):
+    _, tokens, width = grads.shape
+    steps = tokens // block
+    row = lambda i: (i, 0)
+    passed = [pl.BlockSpec((source.shape[0] // steps, source.shape[1]), row) for source in sources]
+    fixed = lambda i: (0, 0)
+    units = gen_sum.shape[0] - 8
+    return pl.pallas_call(
+        lambda *refs: finish_kernel(len(sources), *refs),
+        grid=(steps,),
+        in_specs=[
+            pl.BlockSpec((block, mix.shape[1]), lambda i: (i, 0)),
+            pl.BlockSpec((4, block, width), lambda i: (0, i, 0)),
+            pl.BlockSpec(mix_grad.shape, fixed),
+            pl.BlockSpec(gain_sum.shape, fixed),
+            pl.BlockSpec((8, width), lambda i: (units // 8, 0)),
+        ]
+        + passed,
+        out_specs=[
+            pl.BlockSpec((states, block, width), lambda i: (0, i, 0)),
+            pl.BlockSpec((mixes, tokens), fixed),
+            pl.BlockSpec((5, width), fixed),
+        ]
+        + passed,
+        out_shape=[
+            jax.ShapeDtypeStruct((states, tokens, width), BF16),
+            jax.ShapeDtypeStruct((mixes, tokens), F32),
+            jax.ShapeDtypeStruct((5, width), F32),
+        ]
+        + [jax.ShapeDtypeStruct(source.shape, source.dtype) for source in sources],
+        scratch_shapes=[
+            pltpu.VMEM((states * block, 4 * block), BF16),
+        ],
+        cost_estimate=pl.CostEstimate(
+            flops=tokens * width * 72, bytes_accessed=tokens * width * 26, transcendentals=0
+        ),
+        compiler_params=pltpu.CompilerParams(vmem_limit_bytes=62 * MIB),
+        name="finish_stage",
+    )(mix, grads, mix_grad, gain_sum, gen_sum, *sources)
 
 
 def body(
@@ -1431,26 +1742,16 @@
     next_grad,
 ):
     dp_size, tensor_size = sizes
-    width = history.shape[2]
-    tok_count = history.shape[1]
-    mix_rows = mix_weights.T
-    cos_row, sin_row = rotary_tables(segments)
-    blank = jnp.zeros((tok_count, HEAD_DIM - ROT // 2), F32)
-    turn = jnp.stack(
-        [
-            jnp.concatenate([cos_row, cos_row, blank[:, ROT // 2 :] + 1.0], axis=1),
-            jnp.concatenate([sin_row, blank], axis=1),
-            jnp.concatenate([blank[:, : ROT // 2], -sin_row, blank[:, ROT // 2 :]], axis=1),
-        ]
-    )
-    seg_col, seg_row = segments[:, None], segments[None, :]
-    stats, heads, hidden, low_t, branch, normed, streams, full_qkv, full_up, low_all = front_stage(
+    places = np.arange(HEAD_DIM)
+    frequency = np.where(
+        places < ROT, np.float32(ROPE_BASE) ** (-2.0 * (places % (ROT // 2)).astype(np.float32) / ROT), 0.0
+    ).astype(np.float32)
+    stats, branch, mix_rows, turn, two, heads, hidden, low_t, normed, streams, full_qkv, full_up, low_all = front_stage(
         dp_size,
-        mix_rows,
+        mix_weights,
         norm_gains,
-        turn,
-        seg_col,
-        seg_row,
+        segments[None, :],
+        jnp.asarray(frequency)[None, :],
         history,
         w_query,
         w_key,
@@ -1460,28 +1761,26 @@
         w_down,
     )
     layer_out, next_mix, out_total, branch_grad, gain_gen_grad, grad_gen_in, grad_gen_out = gen_stage(
-        dp_size, streams, branch, norm_gains, gen_in, gen_out, out_grad, next_grad.T
+        dp_size, streams, branch, norm_gains, gen_in.T, gen_out, out_grad, next_grad
     )
 
     gen_units, gen_next = gen_out.shape
-    gen_mid = jnp.pad(grad_gen_out, ((0, 0), (0, 128 - gen_next)))
-    grad_out, grad_down, hidden_grad, qkv_low, parts, gen_sum, mid_sum = mid_stage(
+    gen_sum, mid_sum, grad_out, grad_down, hidden_grad, qkv_low, parts = mid_stage(
         dp_size,
         low_t,
         branch_grad,
         hidden,
         heads,
         turn,
-        seg_col,
-        seg_row,
+        two,
         grad_gen_in,
         gain_gen_grad,
-        gen_mid,
+        grad_gen_out,
         low_all,
         full_up,
         full_qkv,
     )
-    grad_up, grad_query, grad_key, grad_value, history_grad, mix_grad, gain_sums = back_stage(
+    mix_grad, gain_sums, grad_up, grad_query, grad_key, grad_value, stream_grad = back_stage(
         dp_size,
         normed,
         hidden_grad,
@@ -1494,12 +1793,22 @@
         streams,
         out_total,
     )
+    history_grad, mix_grad, grad_gains, grad_up, grad_query, grad_key, grad_value, grad_out, grad_down = finish_stage(
+        history.shape[0],
+        mix_weights.shape[0],
+        mix_rows,
+        stream_grad,
+        mix_grad,
+        gain_sums,
+        gen_sum,
+        (grad_up, grad_query, grad_key, grad_value, grad_out, grad_down),
+    )
     return (
         layer_out,
-        next_mix.T,
+        next_mix,
         history_grad,
-        mix_grad.T,
-        jnp.concatenate([gain_sums, gen_sum[gen_units : gen_units + 1]], axis=0),
+        mix_grad,
+        grad_gains,
         grad_query,
         grad_key,
         grad_value,

time: 598 us -> 575 us (0.962)
  local copies, waits for them, and re-layouts: 37.2 us -> 1.36 us
  Pallas kernels: 546 us -> 563 us
    unnamed x41 -> x5, local copies, waits for them, and re-layouts: 34.1 us -> 0.62 us
    pallas_call x1 -> x2, Pallas kernels: 121 us -> 140 us  [the longest x1 118 us: mid_stage(): pl.pallas_call(lambda *refs: mid_kernel(size, *refs), in_specs=[vmem] * 5...]
where the time goes in v3:
time: 575 us; the launch traced here: 565 us
  Pallas kernels  563 us (98%)
    pallas_call x1, Pallas kernels, front_stage(): pl.pallas_call(lambda *refs: front_kernel(size, *refs), in_specs=[vmem] *...  257 us
    pallas_call x1, Pallas kernels, back_stage(): pl.pallas_call(lambda *refs: back_kernel(size, *refs), in_specs=[vmem] *...  155 us
    pallas_call x1, Pallas kernels, mid_stage(): pl.pallas_call(lambda *refs: mid_kernel(size, *refs), in_specs=[vmem] * 5...  118 us
    pallas_call x1, Pallas kernels, finish_stage(): pl.pallas_call(lambda *refs: finish_kernel(len(sources), *refs), grid=(st...  22 us

profile of v3, /device:TPU:0, one launch (start us, length us, event | category | flops | bytes accessed | tf_op | source)
XLA Modules:
  0.0 565.2 jit_solution(1214990454452035258)
XLA Ops:
  0.6 257.3 %front_stage.1 = (f32[512,8]{1,0:T(8,128)}, bf16[8,512,256]{2,1,0:T(8,128)(2,1)}, f32[512,40]{1,0:T(8,128)}, f32[3,512,128]{2,1,0:T(8,128)}, s32[1,512]{1,0:T(1,...) custom-call(f32[36,512]{1,0:T(8,128)} %refs_0_.1, ...), custom_call_target="tpu_custom_call" | custom-call | flops 8388608000 | bytes 83886080 | tf_op jit(solution)/shard_map/front_stage/pallas_call | solution.py:1588
  258.0 10.3 %gen_stage.1 = (bf16[512,2048]{1,0:T(8,128)(2,1)}, f32[40,512]{1,0:T(8,128)}, f32[512,2048]{1,0:T(8,128)}, bf16[8,512,256]{2,1,0:T(8,128)(2,1)}, f32[1,2048]{1,0...) custom-call(f32[4,512,2048]{2,1,0:T(8,128)} %get-tuple-element.56.stream.refs_8_, ...), custom_call_target="tpu_custom_call" | custom-call | flops 314572800 | bytes 16777216 | tf_op jit(solution)/shard_map/gen_stage/pallas_call | solution.py:87
  268.4 118.2 %mid_stage.1 = (f32[48,2048]{1,0:T(8,128)}, f32[40,128]{1,0:T(8,128)}, f32[512,256]{1,0:T(8,128)}, f32[2048,256]{1,0:T(8,128)}, bf16[512,2048]{1,0:T(8,128)(2,1)...) custom-call(f32[3,512,128]{2,1,0:T(8,128)} %get-tuple-element.63.refs_0_, ...), custom_call_target="tpu_custom_call" | custom-call | flops 4194304000 | bytes 41943040 | tf_op jit(solution)/shard_map/mid_stage/pallas_call | solution.py:1041
  386.6 0.0 copy-start
  386.6 154.9 %back_stage.1 = (f32[512,40]{1,0:T(8,128)}, f32[4,2048]{1,0:T(4,128)}, f32[256,2048]{1,0:T(8,128)}, f32[256,512]{1,0:T(8,128)}, f32[256,512]{1,0:T(8,128)}, /*in...) custom-call(f32[512,8]{1,0:T(8,128)} %get-tuple-element.61.refs_0_, f32[512,40]{1,0:T(8,128)} %get-tuple-element.60.refs_1_.refs_0_, ...), custom_call_target="tpu_custom_call" | custom-call | flops 2097152000 | bytes 67108864 | tf_op jit(solution)/shard_map/back_stage/pallas_call | solution.py:595
  541.5 0.0 copy-done
  541.5 0.7 slice_bitcast_fusion
  542.3 0.0 copy-start.1
  542.3 22.0 %finish_stage.1 = (bf16[9,512,2048]{2,1,0:T(8,128)(2,1)}, f32[36,512]{1,0:T(8,128)}, f32[5,2048]{1,0:T(8,128)}, f32[256,2048]{1,0:T(8,128)}, f32[256,512]{1,0:T(...) custom-call(f32[512,40]{1,0:T(8,128)} %get-tuple-element.60.refs_1_.refs_0_, ...), custom_call_target="tpu_custom_call" | custom-call | flops 75497472 | bytes 27262976 | tf_op jit(solution)/shard_map/finish_stage/pallas_call | solution.py:1693
  564.3 0.0 copy-done.1
  564.3 0.6 copy.29
Async XLA Ops:
  386.6 154.9 %copy-start = (f32[48,2048]{1,0:T(8,128)S(1)}, f32[48,2048]{1,0:T(8,128)}, u32[]{:S(2)}) copy-start(f32[48,2048]{1,0:T(8,128)} %get-tuple-element.82.refs_4_) | copy-start | bytes 1179652
  542.3 22.0 %copy-start.1 = (f32[40,128]{1,0:T(8,128)S(1)}, f32[40,128]{1,0:T(8,128)}, u32[]{:S(2)}) copy-start(f32[40,128]{1,0:T(8,128)} %get-tuple-element.98) | copy-start | bytes 61444

commit v4 on v3

--- a/solution.py
+++ b/solution.py
@@ -277,34 +277,41 @@
             device_id_type=MESH,
         )
 
+    def open_ring(some):
+        for piece in some:
+            far_term(piece)
+            for way in range(2):
+                send(0, way, piece).start()
+
+    def far_term(piece):
+        cols = pl.ds(starts[piece], pieces[piece][2])
+
+        def far_rows(rows):
+            far[rows, cols] = term(0, piece, rows).astype(BF16)
+
+        row_loop(0, shard, far_rows)
+
+    early = len(pieces) // 2
     for copy in loads[:2]:
         copy.wait()
     flip(0, half, (3,))
-    for piece in range(len(pieces)):
-        if pieces[piece][0] == 1:
-            for copy in loads[2:]:
-                copy.wait()
-            flip(0, half, (0, 1, 2))
-        cols = pl.ds(starts[piece], pieces[piece][2])
-
-        def far_rows(rows):
-            far[rows, cols] = term(0, piece, rows).astype(BF16)
-
-        row_loop(0, shard, far_rows)
-        for way in range(2):
-            send(0, way, piece).start()
-        if piece == 0:
-            load.wait()
-            for at in range(blocks):
-                rows = pl.ds(pl.multiple_of((1 - core) * rows_half + at * block, block), block)
-                pltpu.make_async_remote_copy(
-                    src_ref=parts.at[:, rows, :],
-                    dst_ref=from_core.at[at],
-                    send_sem=core_send.at[at],
-                    recv_sem=core_recv.at[at],
-                    device_id=(me, twin),
-                    device_id_type=MESH,
-                ).start()
+    open_ring(range(early))
+    load.wait()
+    for at in range(blocks):
+        rows = pl.ds(pl.multiple_of((1 - core) * rows_half + at * block, block), block)
+        pltpu.make_async_remote_copy(
+            src_ref=parts.at[:, rows, :],
+            dst_ref=from_core.at[at],
+            send_sem=core_send.at[at],
+            recv_sem=core_recv.at[at],
+            device_id=(me, twin),
+            device_id_type=MESH,
+        ).start()
+    for copy in loads[2:]:
+        copy.wait()
+    flip(0, half, (0, 1, 2))
+    for piece in range(early, len(pieces)):
+        far_term(piece)
 
     def mine(at):
         return pl.ds(pl.multiple_of(core * rows_half + at * block, block), block)
@@ -555,12 +562,16 @@
                     )
                     which, at, count = pieces[piece]
                     if which == 0:
-                        grad_up[rows, at : at + count] = total
+                        grad_up[rows, at : at + count] = total.astype(BF16)
                     else:
-                        grad_qkv[which - 1, rows, :] = total
+                        grad_qkv[which - 1, rows, :] = total.astype(BF16)
 
                 row_loop(0, shard, finish)
                 grad_copy(piece).start()
+            if hop == 1 and piece == early - 1:
+                for late in range(early, len(pieces)):
+                    for way in range(2):
+                        send(0, way, late).start()
             while tasks and tasks[0][0] <= passed:
                 _, run, value = tasks.pop(0)
                 run(value)
@@ -591,7 +602,7 @@
     vmem = pl.BlockSpec(memory_space=pltpu.VMEM)
     hbm = pl.BlockSpec(memory_space=pl.ANY)
     dma = pltpu.SemaphoreType.DMA
-    small = jax.ShapeDtypeStruct((shard, local), F32)
+    small = jax.ShapeDtypeStruct((shard, local), BF16)
     return pl.pallas_call(
         lambda *refs: back_kernel(size, *refs),
         in_specs=[vmem] * 3 + [hbm] * 7,
@@ -599,7 +610,7 @@
         out_shape=[
             jax.ShapeDtypeStruct((tokens, mix.shape[1]), F32),
             jax.ShapeDtypeStruct((4, width), F32),
-            jax.ShapeDtypeStruct((shard, hidden), F32),
+            jax.ShapeDtypeStruct((shard, hidden), BF16),
             small,
             small,
             small,
@@ -609,8 +620,8 @@
             pltpu.VMEM(normed.shape, BF16),
             pltpu.VMEM((tokens, hidden), BF16),
             pltpu.VMEM((tokens, 3 * local), BF16),
-            pltpu.VMEM((shard, hidden), F32),
-            pltpu.VMEM((3, shard, local), F32),
+            pltpu.VMEM((shard, hidden), BF16),
+            pltpu.VMEM((3, shard, local), BF16),
             pltpu.VMEM((4, 8, width), F32),
             pltpu.VMEM((steps, 4, width), F32),
             pltpu.VMEM((steps, 4, width), F32),
@@ -724,6 +735,8 @@
     mid_got,
     value_sum,
     key_sum,
+    gen_all,
+    share_sem,
     in_sem,
     out_sem,
     ring_send,
@@ -752,10 +765,14 @@
     ]
     for copy in loads:
         copy.start()
+    core = lax.rem(lane, 2)
+    chip = lax.div(lane, 2)
+    twin = chip * 2 + 1 - core
+    across = (1 - chip) * 2 + core
     barrier = pltpu.get_barrier_semaphore()
-    for there in [right, left] + partners:
-        pl.semaphore_signal(barrier, inc=1, device_id=(there, lane), device_id_type=MESH)
-    pl.semaphore_wait(barrier, 2 + steps)
+    for there in [(it, lane) for it in [right, left] + partners] + [(me, twin), (me, across)]:
+        pl.semaphore_signal(barrier, inc=1, device_id=there, device_id_type=MESH)
+    pl.semaphore_wait(barrier, 4 + steps)
 
     low_tiles = rows_all // TILE
     width_tiles = up_full.shape[0] // TILE
@@ -801,15 +818,19 @@
 
     for copy in loads[:2]:
         copy.wait()
-    for piece in range(pieces):
-
+    def far_term(piece):
         def far_rows(rows):
             far[rows, :] = term(index_at(place + half, size), rows).astype(BF16)
 
         row_loop(piece * TILE, TILE, far_rows)
+
+    early = pieces // 2
+    for piece in range(early):
+        far_term(piece)
         for way in range(2):
             send(0, way, piece).start()
-
+    for piece in range(early, pieces):
+        far_term(piece)
     for copy in loads[2:]:
         copy.wait()
 
@@ -928,25 +949,51 @@
             for which, (sent, got) in enumerate(((gen_sent, gen_got), (mid_sent, mid_got)))
         ]
 
+    quarter = gen_sent.shape[2]
+
+    def share(which):
+        if which == 0:
+            cols = pl.ds(pl.multiple_of(lane * quarter, quarter), quarter)
+            there = (me, twin)
+        else:
+            cols = pl.ds(pl.multiple_of(chip * 2 * quarter, 2 * quarter), 2 * quarter)
+            there = (me, across)
+        return pltpu.make_async_remote_copy(
+            src_ref=gen_all.at[:, cols],
+            dst_ref=gen_all.at[:, cols],
+            send_sem=share_sem.at[0, which],
+            recv_sem=share_sem.at[1, which],
+            device_id=there,
+            device_id_type=MESH,
+        )
+
     def gen_step(step):
+        cols = pl.ds(pl.multiple_of(lane * quarter, quarter), quarter)
         if step == 0:
             units = gen_grad.shape[0]
-            gen_sent[0, :units, :] = gen_grad[...].astype(BF16)
+            gen_sent[0, :units, :] = gen_grad[:, cols].astype(BF16)
             gen_sent[0, units:, :] = jnp.broadcast_to(
-                gen_gain[...].astype(BF16), (gen_sent.shape[1] - units, gen_sent.shape[2])
+                gen_gain[:, cols].astype(BF16), (gen_sent.shape[1] - units, quarter)
             )
             mid_sent[0] = gen_mid[...]
-        else:
+        elif step <= steps:
             for copy in gen_copies(step - 1):
                 copy.wait_recv()
             total = gen_sent[step - 1].astype(F32) + gen_got[step - 1].astype(F32)
             mid_total = mid_sent[step - 1] + mid_got[step - 1]
             if step == steps:
-                gen_sum[...] = total
+                gen_all[:, cols] = total
                 mid_sum[...] = mid_total
+                share(0).start()
             else:
                 gen_sent[step] = total.astype(BF16)
                 mid_sent[step] = mid_total
+        elif step == steps + 1:
+            share(0).wait_recv()
+            share(1).start()
+        else:
+            share(1).wait_recv()
+            gen_sum[...] = gen_all[...]
         if step < steps:
             for copy in gen_copies(step):
                 copy.start()
@@ -955,8 +1002,8 @@
     tasks += [(head_grad, head) for head in range(local // HEAD_DIM)]
     tasks += [(up_part, at) for at in range(width_tiles)]
     tasks += [(qkv_part, at) for at in range(width_tiles)]
-    for step in range(steps + 1):
-        tasks.insert(2 + 5 * step if steps < 4 else 2 + 3 * step, (gen_step, step))
+    for step in range(steps + 3):
+        tasks.insert(2 + 3 * step, (gen_step, step))
     count = len(tasks)
     slots = half * pieces
     slot = 0
@@ -988,10 +1035,14 @@
                         term(me, rows)
                         + ring[hop - 1, 0, rows, :].astype(F32)
                         + ring[hop - 1, 1, rows, :].astype(F32)
-                    )
+                    ).astype(BF16)
 
                 row_loop(piece * TILE, TILE, finish)
                 grad_copy(piece).start()
+            if hop == 1 and piece == early - 1:
+                for late in range(early, pieces):
+                    for way in range(2):
+                        send(0, way, late).start()
             slot += 1
             while tasks and (slot == slots or len(tasks) * (slots - 2) > count * max(slots - 2 - slot, 0)):
                 run, value = tasks.pop(0)
@@ -1005,6 +1056,8 @@
     for step in range(steps):
         for copy in gen_copies(step):
             copy.wait_send()
+    for which in range(2):
+        share(which).wait_send()
     for hop in range(half):
         for piece in range(pieces):
             for way in range(2):
@@ -1045,8 +1098,8 @@
         out_shape=[
             jax.ShapeDtypeStruct((units + 8, width), F32),
             jax.ShapeDtypeStruct(gen_mid.shape, F32),
-            jax.ShapeDtypeStruct((local, shard), F32),
-            jax.ShapeDtypeStruct((hidden_cols, shard), F32),
+            jax.ShapeDtypeStruct((local, shard), BF16),
+            jax.ShapeDtypeStruct((hidden_cols, shard), BF16),
             jax.ShapeDtypeStruct((tokens, hidden_cols), BF16),
             jax.ShapeDtypeStruct((tokens, 3 * local), BF16),
             jax.ShapeDtypeStruct((4, tokens, width), BF16),
@@ -1056,7 +1109,7 @@
             pltpu.VMEM((size, tokens, shard), BF16),
             pltpu.VMEM((tokens, hidden_cols), F32),
             pltpu.VMEM((tokens, 3 * local), BF16),
-            pltpu.VMEM((rows_all, shard), F32),
+            pltpu.VMEM((rows_all, shard), BF16),
             pltpu.VMEM((tokens, hidden_cols), BF16),
             pltpu.VMEM((tokens, 3 * local), BF16),
             pltpu.VMEM((tokens, local), BF16),
@@ -1066,12 +1119,14 @@
             pltpu.VMEM((2, TILE, hidden_cols), BF16),
             pltpu.VMEM((2, TILE, 3 * local), BF16),
             pltpu.VMEM((4, tokens, TILE), BF16),
-            pltpu.VMEM((steps, units + 8, width), BF16),
-            pltpu.VMEM((steps, units + 8, width), BF16),
+            pltpu.VMEM((steps, units + 8, width // 4), BF16),
+            pltpu.VMEM((steps, units + 8, width // 4), BF16),
             pltpu.VMEM((steps,) + gen_mid.shape, F32),
             pltpu.VMEM((steps,) + gen_mid.shape, F32),
             pltpu.VMEM((tokens, HEAD_DIM), F32),
             pltpu.VMEM((tokens, HEAD_DIM), F32),
+            pltpu.VMEM((units + 8, width), F32),
+            dma((2, 2)),
             dma((4,)),
             dma((2 + pieces,)),
             dma((half, 2, pieces)),
@@ -1655,7 +1710,7 @@
     states, tokens, width = history_grad.shape
     step = pl.program_id(0)
     for source, target in zip(sources, targets):
-        target[...] = source[...]
+        target[...] = source[...].astype(F32)
 
     @pl.when(step == 0)
     def _():
@@ -1712,7 +1767,7 @@
             jax.ShapeDtypeStruct((mixes, tokens), F32),
             jax.ShapeDtypeStruct((5, width), F32),
         ]
-        + [jax.ShapeDtypeStruct(source.shape, source.dtype) for source in sources],
+        + [jax.ShapeDtypeStruct(source.shape, F32) for source in sources],
         scratch_shapes=[
             pltpu.VMEM((states * block, 4 * block), BF16),
         ],

time: 575 us -> 567 us (0.986)
  Pallas kernels: 563 us -> 554 us
    pallas_call x1, Pallas kernels: 118 us -> 112 us  [mid_stage(): pl.pallas_call(lambda *refs: mid_kernel(size, *refs), in_specs=[vmem] * 5...]
where the time goes in v4:
time: 567 us; the launch traced here: 556 us
  Pallas kernels  554 us (98%)
    pallas_call x1, Pallas kernels, front_stage(): pl.pallas_call(lambda *refs: front_kernel(size, *refs), in_specs=[vmem] *...  257 us
    pallas_call x1, Pallas kernels, back_stage(): pl.pallas_call(lambda *refs: back_kernel(size, *refs), in_specs=[vmem] *...  153 us
    pallas_call x1, Pallas kernels, mid_stage(): pl.pallas_call(lambda *refs: mid_kernel(size, *refs), in_specs=[vmem] * 5...  112 us
    pallas_call x1, Pallas kernels, finish_stage(): pl.pallas_call(lambda *refs: finish_kernel(len(sources), *refs), grid=(st...  21.5 us

profile of v4, /device:TPU:0, one launch (start us, length us, event | category | flops | bytes accessed | tf_op | source)
XLA Modules:
  0.0 556.2 jit_solution(15201780299440005016)
XLA Ops:
  0.6 257.2 %front_stage.1 = (f32[512,8]{1,0:T(8,128)}, bf16[8,512,256]{2,1,0:T(8,128)(2,1)}, f32[512,40]{1,0:T(8,128)}, f32[3,512,128]{2,1,0:T(8,128)}, s32[1,512]{1,0:T(1,...) custom-call(f32[36,512]{1,0:T(8,128)} %refs_0_.1, ...), custom_call_target="tpu_custom_call" | custom-call | flops 8388608000 | bytes 83886080 | tf_op jit(solution)/shard_map/front_stage/pallas_call | solution.py:1643
  257.9 10.3 %gen_stage.1 = (bf16[512,2048]{1,0:T(8,128)(2,1)}, f32[40,512]{1,0:T(8,128)}, f32[512,2048]{1,0:T(8,128)}, bf16[8,512,256]{2,1,0:T(8,128)(2,1)}, f32[1,2048]{1,0...) custom-call(f32[4,512,2048]{2,1,0:T(8,128)} %get-tuple-element.56.stream.refs_8_, ...), custom_call_target="tpu_custom_call" | custom-call | flops 314572800 | bytes 16777216 | tf_op jit(solution)/shard_map/gen_stage/pallas_call | solution.py:87
  268.2 112.0 %mid_stage.1 = (f32[48,2048]{1,0:T(8,128)}, f32[40,128]{1,0:T(8,128)}, bf16[512,256]{1,0:T(8,128)(2,1)}, bf16[2048,256]{1,0:T(8,128)(2,1)}, bf16[512,2048]{1,0:T...) custom-call(f32[3,512,128]{2,1,0:T(8,128)} %get-tuple-element.63.refs_0_, ...), custom_call_target="tpu_custom_call" | custom-call | flops 4194304000 | bytes 41943040 | tf_op jit(solution)/shard_map/mid_stage/pallas_call | solution.py:1094
  380.2 0.0 copy-start
  380.2 152.8 %back_stage.1 = (f32[512,40]{1,0:T(8,128)}, f32[4,2048]{1,0:T(4,128)}, bf16[256,2048]{1,0:T(8,128)(2,1)}, bf16[256,512]{1,0:T(8,128)(2,1)}, bf16[256,512]{1,0:T(...) custom-call(f32[512,8]{1,0:T(8,128)} %get-tuple-element.61.refs_0_, ...), custom_call_target="tpu_custom_call" | custom-call | flops 2097152000 | bytes 67108864 | tf_op jit(solution)/shard_map/back_stage/pallas_call | solution.py:606
  533.1 0.0 copy-done
  533.1 0.7 slice_bitcast_fusion
  533.8 0.0 copy-start.1
  533.8 21.5 %finish_stage.1 = (bf16[9,512,2048]{2,1,0:T(8,128)(2,1)}, f32[36,512]{1,0:T(8,128)}, f32[5,2048]{1,0:T(8,128)}, f32[256,2048]{1,0:T(8,128)}, f32[256,512]{1,0:T(...) custom-call(f32[512,40]{1,0:T(8,128)} %get-tuple-element.60.refs_1_.refs_0_, ...), custom_call_target="tpu_custom_call" | custom-call | flops 75497472 | bytes 27262976 | tf_op jit(solution)/shard_map/finish_stage/pallas_call | solution.py:1748
  555.4 0.0 copy-done.1
  555.4 0.6 copy.29
Async XLA Ops:
  380.2 152.9 %copy-start = (f32[48,2048]{1,0:T(8,128)S(1)}, f32[48,2048]{1,0:T(8,128)}, u32[]{:S(2)}) copy-start(f32[48,2048]{1,0:T(8,128)} %get-tuple-element.82.refs_4_) | copy-start | bytes 1179652
  533.8 21.6 %copy-start.1 = (f32[40,128]{1,0:T(8,128)S(1)}, f32[40,128]{1,0:T(8,128)}, u32[]{:S(2)}) copy-start(f32[40,128]{1,0:T(8,128)} %get-tuple-element.98) | copy-start | bytes 61444

commit v5 on v4

--- a/solution.py
+++ b/solution.py
@@ -262,7 +262,7 @@
     def send(hop, way, piece):
         cols = pl.ds(starts[piece], pieces[piece][2])
         if hop == 0:
-            rows = pl.ds(way * cut, cut)
+            rows = pl.ds(pl.multiple_of(way * cut, cut), cut)
             source = far.at[rows, cols]
             target = ring.at[0, way, rows, cols]
         else:
@@ -273,7 +273,7 @@
             dst_ref=target,
             send_sem=ring_send.at[hop, way, piece],
             recv_sem=ring_recv.at[hop, way, piece],
-            device_id=((right, left)[way], lane),
+            device_id=(right + way * (left - right), lane),
             device_id_type=MESH,
         )
 
@@ -401,44 +401,47 @@
         rows = pl.ds(pl.multiple_of(base, UNIT), UNIT)
         return pltpu.make_async_copy(grad_out.at[slot], stream_grad.at[:, rows, :], store_sem.at[slot])
 
-    mixes = 2 * blocks
-
-    def task_base(task):
-        at, side = divmod(task, 2)
-        return side * rows_half + at * block
+    def unit_base(at, unit):
+        return lax.div(unit, 2) * rows_half + at * block + lax.rem(unit, 2) * UNIT
 
     gain_grad[...] = jnp.zeros_like(gain_grad)
     mix_grad[...] = jnp.zeros_like(mix_grad)
     for copy in unit_loads(0, 0):
         copy.start()
 
-    def mix_task(task):
-        first = task_base(task)
-
-        @pl.loop(0, 2)
-        def _(slot):
-            @pl.when(slot == 0)
+    def mix_task(at):
+        @pl.loop(0, 4)
+        def _(unit):
+            slot = lax.rem(unit, 2)
+            base = unit_base(at, unit)
+
+            @pl.when(unit < 3)
             def _():
-                for copy in unit_loads(first + UNIT, 1):
+                for copy in unit_loads(unit_base(at, unit + 1), 1 - slot):
                     copy.start()
 
-            if task + 1 < mixes:
-
-                @pl.when(slot == 1)
+            if at + 1 < blocks:
+
+                @pl.when(unit == 3)
                 def _():
-                    for copy in unit_loads(task_base(task + 1), 0):
+                    for copy in unit_loads((at + 1) * block, 0):
                         copy.start()
 
-            for copy in unit_loads(first + slot * UNIT, slot):
+            for copy in unit_loads(base, slot):
                 copy.wait()
-            if task > 0:
-                unit_store(task_base(task - 1) + slot * UNIT, slot).wait()
+            if at > 0:
+                unit_store(base, slot).wait()
+            else:
+
+                @pl.when(unit >= 2)
+                def _():
+                    unit_store(base, slot).wait()
 
             @pl.loop(0, UNIT // GROUP)
             def _(step):
-                mix_group(first + slot * UNIT + step * GROUP, slot, step * GROUP)
-
-            unit_store(first + slot * UNIT, slot).start()
+                mix_group(base + step * GROUP, slot, step * GROUP)
+
+            unit_store(base, slot).start()
 
     def mix_group(base, slot, inner_base):
         rows = pl.ds(pl.multiple_of(base, GROUP), GROUP)
@@ -520,8 +523,7 @@
         tasks.append((0.02 + 0.03 * at, to_link, at))
         tasks.append((0.19 + 0.16 * at, to_twin, at))
         tasks.append((0.23 + 0.16 * at, ready, at))
-        for side in range(2):
-            tasks.append((0.24 + 0.16 * at + 0.07 * side, mix_task, 2 * at + side))
+        tasks.append((0.24 + 0.16 * at, mix_task, at))
     for step in range(steps + 1):
         tasks.append((0.87 + 0.12 * step / steps, gain_step, step))
     tasks.sort(key=lambda item: item[0])
@@ -529,15 +531,18 @@
         if hop == half:
             flip(0, 0)
         else:
-            for way in range(2):
+
+            @pl.loop(0, 2)
+            def _(way):
                 flip(way, (half - hop) * (1 - 2 * way))
+
         for piece in range(len(pieces)):
             passed = ((hop - 1.5 if hop > 1 else 0.0) + (piece + 1) / len(pieces) * (1 if hop > 1 else 0.5)) / (half - 0.5)
             cols = pl.ds(starts[piece], pieces[piece][2])
-            for way in range(2):
+
+            @pl.loop(0, 2)
+            def _(way):
                 send(hop - 1, way, piece).wait_recv()
-                if hop == half:
-                    continue
 
                 def with_got(rows):
                     got = ring[hop - 1, way, rows, cols].astype(F32)
@@ -549,9 +554,11 @@
                 if hop == 1:
                     row_loop(way * cut, cut, with_got)
                     row_loop((1 - way) * cut, cut, alone)
-                else:
+                elif hop < half:
                     row_loop(0, shard, with_got)
-                send(hop, way, piece).start()
+                if hop < half:
+                    send(hop, way, piece).start()
+
             if hop == half:
 
                 def finish(rows):
@@ -580,7 +587,7 @@
     for piece in range(len(pieces)):
         grad_copy(piece).wait()
     for slot in range(2):
-        unit_store(task_base(mixes - 1) + slot * UNIT, slot).wait()
+        unit_store((blocks - 1) * block, slot).wait()
     for step in range(steps):
         gain_copy(step).wait_send()
     for hop in range(half):
@@ -736,6 +743,7 @@
     value_sum,
     key_sum,
     gen_all,
+    slope_in,
     share_sem,
     in_sem,
     out_sem,
@@ -802,7 +810,7 @@
 
     def send(hop, way, piece):
         if hop == 0:
-            rows = pl.ds(piece * TILE + way * cut, cut)
+            rows = pl.ds(pl.multiple_of(piece * TILE + way * cut, cut), cut)
             source = far.at[rows, :]
         else:
             rows = pl.ds(piece * TILE, TILE)
@@ -812,7 +820,7 @@
             dst_ref=ring.at[hop, way, rows, :],
             send_sem=ring_send.at[hop, way, piece],
             recv_sem=ring_recv.at[hop, way, piece],
-            device_id=((right, left)[way], lane),
+            device_id=(right + way * (left - right), lane),
             device_id_type=MESH,
         )
 
@@ -864,7 +872,14 @@
                 attended_grad[rows, base : base + TILE] = total.astype(BF16)
             else:
                 cols = slice(base - local, base - local + TILE)
-                hidden_grad[rows, cols] = (total * gelu_slope(hidden[rows, cols])).astype(BF16)
+                slope_in[: rows.size, :] = total
+
+                @pl.loop(0, rows.size // 32)
+                def _(part):
+                    inner = pl.ds(pl.multiple_of(part * 32, 32), 32)
+                    there = pl.ds(pl.multiple_of(rows.start + part * 32, 32), 32)
+                    slope = gelu_slope(hidden[there, cols])
+                    hidden_grad[there, cols] = (slope_in[inner, :] * slope).astype(BF16)
 
         row_loop(0, tokens, run, 256)
         if at + 1 == low_tiles:
@@ -1009,10 +1024,10 @@
     slot = 0
     for hop in range(1, half + 1):
         for piece in range(pieces):
-            for way in range(2):
+
+            @pl.loop(0, 2)
+            def _(way):
                 send(hop - 1, way, piece).wait_recv()
-                if hop == half:
-                    continue
                 owner = index_at(place + (half - hop) * (1 - 2 * way), size)
 
                 def with_got(rows):
@@ -1025,9 +1040,11 @@
                 if hop == 1:
                     row_loop(piece * TILE + way * cut, cut, with_got)
                     row_loop(piece * TILE + (1 - way) * cut, cut, alone)
-                else:
+                elif hop < half:
                     row_loop(piece * TILE, TILE, with_got)
-                send(hop, way, piece).start()
+                if hop < half:
+                    send(hop, way, piece).start()
+
             if hop == half:
 
                 def finish(rows):
@@ -1126,6 +1143,7 @@
             pltpu.VMEM((tokens, HEAD_DIM), F32),
             pltpu.VMEM((tokens, HEAD_DIM), F32),
             pltpu.VMEM((units + 8, width), F32),
+            pltpu.VMEM((256, TILE), F32),
             dma((2, 2)),
             dma((4,)),
             dma((2 + pieces,)),
@@ -1302,7 +1320,7 @@
         slot = lax.rem(unit, 2)
         return pltpu.make_async_copy(stream_out.at[slot], streams.at[:, rows, :], stream_sem.at[slot])
 
-    per_task = 2
+    per_task = 4
 
     def tables():
         count = mix_in.shape[0]
@@ -1347,6 +1365,11 @@
         state_load(unit).wait()
         if task > 0:
             stream_store(unit - 2).wait()
+        else:
+
+            @pl.when(unit >= 2)
+            def _():
+                stream_store(unit - 2).wait()
 
         @pl.loop(0, UNIT // GROUP)
         def _(step):
@@ -1440,21 +1463,25 @@
                     )
                 heads[rows, which * local + at : which * local + at + HEAD_DIM] = part.astype(BF16)
 
-        row_loop(0, tokens, run)
-
-    def head_task(head):
-        at = head * HEAD_DIM
-
-        def run(rows):
-            query = heads[rows, at : at + HEAD_DIM]
-            key = heads[:, local + at : local + at + HEAD_DIM]
-            value = heads[:, 2 * local + at : 2 * local + at + HEAD_DIM]
-            probs = attention_probs(query, key, two[...], rows.start).astype(BF16)
-            attended = jnp.dot(probs, value, preferred_element_type=F32)
-            low[rows, at : at + HEAD_DIM] = attended.astype(BF16)
-            low_t[at : at + HEAD_DIM, rows] = attended.T.astype(BF16)
-
-        row_loop(0, tokens, run)
+        row_loop(0, tokens, run, 64)
+
+    def head_task(pair):
+        @pl.loop(0, 2)
+        def _(which):
+            at = pl.multiple_of((2 * pair + which) * HEAD_DIM, HEAD_DIM)
+            query_cols, key_cols, value_cols = (
+                pl.ds(pl.multiple_of(part * local + at, HEAD_DIM), HEAD_DIM) for part in range(3)
+            )
+
+            def run(rows):
+                probs = attention_probs(
+                    heads[rows, query_cols], heads[:, key_cols], two[...], rows.start
+                ).astype(BF16)
+                attended = jnp.dot(probs, heads[:, value_cols], preferred_element_type=F32)
+                low[rows, query_cols] = attended.astype(BF16)
+                low_t[query_cols, rows] = attended.T.astype(BF16)
+
+            row_loop(0, tokens, run, 128)
 
     def up_task(at):
         if at == 0:
@@ -1469,9 +1496,13 @@
         def run(rows):
             product = tile_product(3 + at, 3, rows)
             hidden[rows, cols] = product
-            active = gelu(product)
-            low[rows, low_cols] = active.astype(BF16)
-            low_t[low_cols, rows] = active.T.astype(BF16)
+
+            @pl.loop(0, rows.size // 32)
+            def _(part):
+                there = pl.ds(pl.multiple_of(rows.start + part * 32, 32), 32)
+                low[there, low_cols] = gelu(hidden[there, cols]).astype(BF16)
+
+            low_t[low_cols, rows] = low[rows, low_cols].T
 
         row_loop(0, tokens, run)
         if at + 1 == tiles - 3:
@@ -1576,8 +1607,8 @@
     early = first[1] + counts[1]
     for which in range(3):
         tasks.append((early + which, qkv_task, which))
-    for head in range(local // HEAD_DIM):
-        tasks.append((early + 3 + head, head_task, head))
+    for pair in range(local // HEAD_DIM // 2):
+        tasks.append((early + 3 + 2 * pair, head_task, pair))
     middle = first[2] + counts[2]
     for at in range(tiles - 3):
         tasks.append((middle + at, up_task, at))

time: 567 us -> 557 us (0.982); the launches traced: 556 us -> 555 us
  no operation moved by 1% of the time
where the time goes in v5:
time: 557 us; the launch traced here: 555 us
  Pallas kernels  553 us (99%)
    pallas_call x1, Pallas kernels, front_stage(): pl.pallas_call(lambda *refs: front_kernel(size, *refs), in_specs=[vmem] *...  257 us
    pallas_call x1, Pallas kernels, back_stage(): pl.pallas_call(lambda *refs: back_kernel(size, *refs), in_specs=[vmem] *...  153 us
    pallas_call x1, Pallas kernels, mid_stage(): pl.pallas_call(lambda *refs: mid_kernel(size, *refs), in_specs=[vmem] * 5...  112 us
    pallas_call x1, Pallas kernels, finish_stage(): pl.pallas_call(lambda *refs: finish_kernel(len(sources), *refs), grid=(st...  21.5 us

profile of v5, /device:TPU:0, one launch (start us, length us, event | category | flops | bytes accessed | tf_op | source)
XLA Modules:
  0.0 555.5 jit_solution(1670745501541735913)
XLA Ops:
  0.6 256.9 %front_stage.1 = (f32[512,8]{1,0:T(8,128)}, bf16[8,512,256]{2,1,0:T(8,128)(2,1)}, f32[512,40]{1,0:T(8,128)}, f32[3,512,128]{2,1,0:T(8,128)}, s32[1,512]{1,0:T(1,...) custom-call(f32[36,512]{1,0:T(8,128)} %refs_0_.1, ...), custom_call_target="tpu_custom_call" | custom-call | flops 8388608000 | bytes 83886080 | tf_op jit(solution)/shard_map/front_stage/pallas_call | solution.py:1674
  257.5 10.3 %gen_stage.1 = (bf16[512,2048]{1,0:T(8,128)(2,1)}, f32[40,512]{1,0:T(8,128)}, f32[512,2048]{1,0:T(8,128)}, bf16[8,512,256]{2,1,0:T(8,128)(2,1)}, f32[1,2048]{1,0...) custom-call(f32[4,512,2048]{2,1,0:T(8,128)} %get-tuple-element.56.stream.refs_8_, ...), custom_call_target="tpu_custom_call" | custom-call | flops 314572800 | bytes 16777216 | tf_op jit(solution)/shard_map/gen_stage/pallas_call | solution.py:87
  267.9 112.0 %mid_stage.1 = (f32[48,2048]{1,0:T(8,128)}, f32[40,128]{1,0:T(8,128)}, bf16[512,256]{1,0:T(8,128)(2,1)}, bf16[2048,256]{1,0:T(8,128)(2,1)}, bf16[512,2048]{1,0:T...) custom-call(f32[3,512,128]{2,1,0:T(8,128)} %get-tuple-element.63.refs_0_, ...), custom_call_target="tpu_custom_call" | custom-call | flops 4194304000 | bytes 41943040 | tf_op jit(solution)/shard_map/mid_stage/pallas_call | solution.py:1111
  379.9 0.0 copy-start
  379.9 152.7 %back_stage.1 = (f32[512,40]{1,0:T(8,128)}, f32[4,2048]{1,0:T(4,128)}, bf16[256,2048]{1,0:T(8,128)(2,1)}, bf16[256,512]{1,0:T(8,128)(2,1)}, bf16[256,512]{1,0:T(...) custom-call(f32[512,8]{1,0:T(8,128)} %get-tuple-element.61.refs_0_, ...), custom_call_target="tpu_custom_call" | custom-call | flops 2097152000 | bytes 67108864 | tf_op jit(solution)/shard_map/back_stage/pallas_call | solution.py:613
  532.6 0.0 copy-done
  532.6 0.7 slice_bitcast_fusion
  533.3 0.0 copy-start.1
  533.3 21.5 %finish_stage.1 = (bf16[9,512,2048]{2,1,0:T(8,128)(2,1)}, f32[36,512]{1,0:T(8,128)}, f32[5,2048]{1,0:T(8,128)}, f32[256,2048]{1,0:T(8,128)}, f32[256,512]{1,0:T(...) custom-call(f32[512,40]{1,0:T(8,128)} %get-tuple-element.60.refs_1_.refs_0_, ...), custom_call_target="tpu_custom_call" | custom-call | flops 75497472 | bytes 27262976 | tf_op jit(solution)/shard_map/finish_stage/pallas_call | solution.py:1779
  554.9 0.0 copy-done.1
  554.9 0.6 copy.29
Async XLA Ops:
  379.9 152.7 %copy-start = (f32[48,2048]{1,0:T(8,128)S(1)}, f32[48,2048]{1,0:T(8,128)}, u32[]{:S(2)}) copy-start(f32[48,2048]{1,0:T(8,128)} %get-tuple-element.82.refs_4_) | copy-start | bytes 1179652
  533.3 21.5 %copy-start.1 = (f32[40,128]{1,0:T(8,128)S(1)}, f32[40,128]{1,0:T(8,128)}, u32[]{:S(2)}) copy-start(f32[40,128]{1,0:T(8,128)} %get-tuple-element.98) | copy-start | bytes 61444

commit v6 on v5

--- a/solution.py
+++ b/solution.py
@@ -34,7 +34,7 @@
     return lax.dot_general(a, b, (dims, ((), ())), preferred_element_type=F32)
 
 
-def gen_kernel(stream, branch, gain, gen_in, gen_out, out_grad, next_grad, layer_out, next_mix, out_total, branch_grad, gain_grad, in_grad, mid_grad):
+def gen_kernel(stream, branch, gain, gen_in, gen_out, out_grad, next_grad, layer_out, next_mix, branch_grad, gain_grad, in_grad, mid_grad):
     first = pl.program_id(0) == 0
     x = stream[0] + jnp.concatenate([branch[owner] for owner in range(branch.shape[0])], axis=1).astype(F32)
     layer_out[...] = x.astype(BF16)
@@ -55,7 +55,6 @@
         e - jnp.mean(e, axis=1, keepdims=True) - unit * jnp.mean(e * unit, axis=1, keepdims=True)
     )
     total = out_grad[...].astype(F32) + grad
-    out_total[...] = total
     low_total = total.astype(BF16)
     shard = branch_grad.shape[2]
     for owner in range(branch_grad.shape[0]):
@@ -99,7 +98,6 @@
         out_specs=[
             pl.BlockSpec((block, width), row),
             pl.BlockSpec((nxt, block), lambda i: (0, i)),
-            pl.BlockSpec((block, width), row),
             pl.BlockSpec((size, block, width // size), lambda i: (0, i, 0)),
             pl.BlockSpec((1, width), fixed),
             pl.BlockSpec((units, width), fixed),
@@ -108,7 +106,6 @@
         out_shape=[
             jax.ShapeDtypeStruct((tokens, width), BF16),
             jax.ShapeDtypeStruct((nxt, tokens), F32),
-            jax.ShapeDtypeStruct((tokens, width), F32),
             jax.ShapeDtypeStruct((size, tokens, width // size), BF16),
             jax.ShapeDtypeStruct((1, width), F32),
             jax.ShapeDtypeStruct((units, width), F32),
@@ -394,7 +391,7 @@
         return (
             pltpu.make_async_copy(history.at[:, rows, :], state_in.at[slot], unit_sem.at[slot, 0]),
             pltpu.make_async_copy(streams.at[:, rows, :], stream_in.at[slot], unit_sem.at[slot, 1]),
-            pltpu.make_async_copy(out_total.at[rows, :], total_in.at[slot], unit_sem.at[slot, 2]),
+            pltpu.make_async_copy(out_total.at[:, rows, :], total_in.at[slot], unit_sem.at[slot, 2]),
         )
 
     def unit_store(base, slot):
@@ -478,7 +475,9 @@
                 e = parts[stream, rows, cols].astype(F32) * gains[stream : stream + 1, cols]
                 grad = scale * (e - mean_e - unit_x * mean_ex)
                 if stream == 3:
-                    grad = grad + total_in[slot, inner, cols]
+                    first = at * CHUNK // shard
+                    totals = [total_in[slot, owner, inner, :] for owner in range(first, first + CHUNK // shard)]
+                    grad = grad + jnp.concatenate(totals, axis=1).astype(F32)
                 held[stream, :, cols] = grad
                 grad_out[slot, stream, inner, cols] = grad.astype(BF16)
         for source in range(states):
@@ -639,7 +638,7 @@
             pltpu.VMEM((half, 2, shard, cols), BF16),
             pltpu.VMEM((2, states, UNIT, width), BF16),
             pltpu.VMEM((2, 4, UNIT, width), F32),
-            pltpu.VMEM((2, UNIT, width), F32),
+            pltpu.VMEM((2, size, UNIT, shard), BF16),
             pltpu.VMEM((2, 4, UNIT, width), BF16),
             pltpu.VMEM((4, GROUP, width), F32),
             pltpu.VMEM((2, 4, shard, tokens), BF16),
@@ -1733,11 +1732,12 @@
     )(mix, gains, segments, frequency, history, w_query, w_key, w_value, w_up, w_out, w_down)
 
 
-def finish_kernel(count, mix, grads, mix_grad, gain_sum, gen_gain, *refs):
+def finish_kernel(count, mix, grads, mix_grad, gain_sum, gen_sum, mid_sum, *refs):
     sources = refs[:count]
-    history_grad, mix_out, gain_out = refs[count : count + 3]
-    targets = refs[count + 3 : 2 * count + 3]
-    spread = refs[2 * count + 3]
+    history_grad, mix_out, gain_out, gen_out, mid_out = refs[count : count + 5]
+    targets = refs[count + 5 : 2 * count + 5]
+    spread = refs[2 * count + 5]
+    units = gen_out.shape[0]
     states, tokens, width = history_grad.shape
     step = pl.program_id(0)
     for source, target in zip(sources, targets):
@@ -1746,7 +1746,9 @@
     @pl.when(step == 0)
     def _():
         gain_out[:4, :] = gain_sum[...]
-        gain_out[4:5, :] = gen_gain[0:1, :]
+        gain_out[4:5, :] = gen_sum[units : units + 1, :]
+        gen_out[...] = gen_sum[:units, :]
+        mid_out[...] = mid_sum[:, : mid_out.shape[1]]
         mix_out[...] = mix_grad[...].T[: mix_out.shape[0], :]
 
     own = lax.broadcasted_iota(jnp.int32, (tokens, tokens), 0) == lax.broadcasted_iota(
@@ -1769,7 +1771,7 @@
             history_grad[source, :, cols] = mixed[source * tokens : (source + 1) * tokens].astype(BF16)
 
 
-def finish_stage(states, mixes, mix, grads, mix_grad, gain_sum, gen_sum, sources, block=64):
+def finish_stage(states, mixes, following, mix, grads, mix_grad, gain_sum, gen_sum, mid_sum, sources, block=64):
     _, tokens, width = grads.shape
     steps = tokens // block
     row = lambda i: (i, 0)
@@ -1784,19 +1786,24 @@
             pl.BlockSpec((4, block, width), lambda i: (0, i, 0)),
             pl.BlockSpec(mix_grad.shape, fixed),
             pl.BlockSpec(gain_sum.shape, fixed),
-            pl.BlockSpec((8, width), lambda i: (units // 8, 0)),
+            pl.BlockSpec(gen_sum.shape, fixed),
+            pl.BlockSpec(mid_sum.shape, fixed),
         ]
         + passed,
         out_specs=[
             pl.BlockSpec((states, block, width), lambda i: (0, i, 0)),
             pl.BlockSpec((mixes, tokens), fixed),
             pl.BlockSpec((5, width), fixed),
+            pl.BlockSpec((units, width), fixed),
+            pl.BlockSpec((units, following), fixed),
         ]
         + passed,
         out_shape=[
             jax.ShapeDtypeStruct((states, tokens, width), BF16),
             jax.ShapeDtypeStruct((mixes, tokens), F32),
             jax.ShapeDtypeStruct((5, width), F32),
+            jax.ShapeDtypeStruct((units, width), F32),
+            jax.ShapeDtypeStruct((units, following), F32),
         ]
         + [jax.ShapeDtypeStruct(source.shape, F32) for source in sources],
         scratch_shapes=[
@@ -1807,7 +1814,7 @@
         ),
         compiler_params=pltpu.CompilerParams(vmem_limit_bytes=62 * MIB),
         name="finish_stage",
-    )(mix, grads, mix_grad, gain_sum, gen_sum, *sources)
+    )(mix, grads, mix_grad, gain_sum, gen_sum, mid_sum, *sources)
 
 
 def body(
@@ -1846,11 +1853,10 @@
         w_out,
         w_down,
     )
-    layer_out, next_mix, out_total, branch_grad, gain_gen_grad, grad_gen_in, grad_gen_out = gen_stage(
+    layer_out, next_mix, branch_grad, gain_gen_grad, grad_gen_in, grad_gen_out = gen_stage(
         dp_size, streams, branch, norm_gains, gen_in.T, gen_out, out_grad, next_grad
     )
 
-    gen_units, gen_next = gen_out.shape
     gen_sum, mid_sum, grad_out, grad_down, hidden_grad, qkv_low, parts = mid_stage(
         dp_size,
         low_t,
@@ -1877,16 +1883,18 @@
         parts,
         history,
         streams,
-        out_total,
+        branch_grad,
     )
-    history_grad, mix_grad, grad_gains, grad_up, grad_query, grad_key, grad_value, grad_out, grad_down = finish_stage(
+    history_grad, mix_grad, grad_gains, grad_gen_in, grad_gen_out, grad_up, grad_query, grad_key, grad_value, grad_out, grad_down = finish_stage(
         history.shape[0],
         mix_weights.shape[0],
+        gen_out.shape[1],
         mix_rows,
         stream_grad,
         mix_grad,
         gain_sums,
         gen_sum,
+        mid_sum,
         (grad_up, grad_query, grad_key, grad_value, grad_out, grad_down),
     )
     return (
@@ -1901,8 +1909,8 @@
         grad_out,
         grad_up,
         grad_down,
-        gen_sum[:gen_units].T,
-        mid_sum[:, :gen_next],
+        grad_gen_in.T,
+        grad_gen_out,
     )
 
 

time: 557 us -> 555 us (level)
  no operation moved by 1% of the time
where the time goes in v6:
time: 555 us; the launch traced here: 554 us
  Pallas kernels  553 us (100%)
    pallas_call x1, Pallas kernels, front_stage(): pl.pallas_call(lambda *refs: front_kernel(size, *refs), in_specs=[vmem] *...  257 us
    pallas_call x1, Pallas kernels, back_stage(): pl.pallas_call(lambda *refs: back_kernel(size, *refs), in_specs=[vmem] *...  153 us
    pallas_call x1, Pallas kernels, mid_stage(): pl.pallas_call(lambda *refs: mid_kernel(size, *refs), in_specs=[vmem] * 5...  112 us
    pallas_call x1, Pallas kernels, finish_stage(): pl.pallas_call(lambda *refs: finish_kernel(len(sources), *refs), grid=(st...  21.8 us

profile of v6, /device:TPU:0, one launch (start us, length us, event | category | flops | bytes accessed | tf_op | source)
XLA Modules:
  0.0 553.6 jit_solution(4851369855014667497)
XLA Ops:
  0.6 256.9 %front_stage.1 = (f32[512,8]{1,0:T(8,128)}, bf16[8,512,256]{2,1,0:T(8,128)(2,1)}, f32[512,40]{1,0:T(8,128)}, f32[3,512,128]{2,1,0:T(8,128)}, s32[1,512]{1,0:T(1,...) custom-call(f32[36,512]{1,0:T(8,128)} %refs_0_.1, ...), custom_call_target="tpu_custom_call" | custom-call | flops 8388608000 | bytes 83886080 | tf_op jit(solution)/shard_map/front_stage/pallas_call | solution.py:1673
  257.6 9.5 %gen_stage.1 = (bf16[512,2048]{1,0:T(8,128)(2,1)}, f32[40,512]{1,0:T(8,128)}, bf16[8,512,256]{2,1,0:T(8,128)(2,1)}, f32[1,2048]{1,0:T(1,128)}, f32[40,2048]{1,0:T(8,128)}, /*index=5*/f32[40,128]{1,0:T(8,128)}) custom-call(f32[4,512,2048]{2,1,0:T(8,128)} %get-tuple-element.57.stream.refs_8_, bf16[8,512,256]{2,1,0:T(8,128)(2,1)} %get-tuple-element.58.branch, ...), custom_call_target="tpu_custom_call" | custom-call | flops 314572800 | bytes 16777216 | tf_op jit(solution)/shard_map/gen_stage/pallas_call | solution.py:86
  267.0 112.0 %mid_stage.1 = (f32[48,2048]{1,0:T(8,128)}, f32[40,128]{1,0:T(8,128)}, bf16[512,256]{1,0:T(8,128)(2,1)}, bf16[2048,256]{1,0:T(8,128)(2,1)}, bf16[512,2048]{1,0:T...) custom-call(f32[3,512,128]{2,1,0:T(8,128)} %get-tuple-element.64.refs_0_, ...), custom_call_target="tpu_custom_call" | custom-call | flops 4194304000 | bytes 41943040 | tf_op jit(solution)/shard_map/mid_stage/pallas_call | solution.py:1110
  379.0 152.6 %back_stage.1 = (f32[512,40]{1,0:T(8,128)}, f32[4,2048]{1,0:T(4,128)}, bf16[256,2048]{1,0:T(8,128)(2,1)}, bf16[256,512]{1,0:T(8,128)(2,1)}, bf16[256,512]{1,0:T(...) custom-call(f32[512,8]{1,0:T(8,128)} %get-tuple-element.62.refs_0_, ...), custom_call_target="tpu_custom_call" | custom-call | flops 2097152000 | bytes 67108864 | tf_op jit(solution)/shard_map/back_stage/pallas_call | solution.py:612
  531.7 21.8 %finish_stage.1 = (bf16[9,512,2048]{2,1,0:T(8,128)(2,1)}, f32[36,512]{1,0:T(8,128)}, f32[5,2048]{1,0:T(8,128)}, f32[40,2048]{1,0:T(8,128)}, f32[40,40]{1,0:T(8,1...) custom-call(f32[512,40]{1,0:T(8,128)} %get-tuple-element.61.refs_1_., ...), custom_call_target="tpu_custom_call" | custom-call | flops 75497472 | bytes 27262976 | tf_op jit(solution)/shard_map/finish_stage/pallas_call | solution.py:1781
